TPU v7x, 256 devices: a whole 4x4x8 slice. The times are simulated.
256 devices in a mesh: seg: 16 (over z, x_hi), tp: 8 (over y, core), dp: 2 (over x_lo).
Axes of the slice: x: 4 (x_hi: 2, x_lo: 2; x = x_hi * 2 + x_lo), y: 4, z: 8, core: 2. Of those that a mesh axis runs over, the one named last changes fastest.
Arguments:
- tokens: bfloat16 [32768, 4096], P(('dp', 'seg')), parts along dimension 0, may hold values from -64 to 64
- w_query: bfloat16 [4096, 2048], P(None, 'tp'), may hold values from -1 to 1
- w_key: bfloat16 [4096, 2048], P(None, 'tp'), may hold values from -1 to 1
- w_value: bfloat16 [4096, 2048], P(None, 'tp'), may hold values from -0.09375 to 0.09375
- w_out: bfloat16 [2048, 4096], P('tp'), may hold values from -1 to 1
- mem_gate: float32 [16], P('tp'), may hold values from -2 to 2
- resets: int32 [32], P(('dp', 'seg')), parts along dimension 0, may hold values 0 or 1
Outputs:
- layer_out: bfloat16 [32768, 4096], P(('dp', 'seg'), 'tp'), parts along dimension 0
There are 2 independent parts, one for each index of `dp`. A program takes and returns all parts, laid end to end along the dimension named above; an argument that names none is the same for every part. Nothing has to cross between parts.
All inputs are finite; a program needn't handle non-finite values. No bound on the sum of `resets` on one device may be relied on, other than what follows from the above.
Results may differ from a plain program's by a relative error of at most 0.014.
Values may be sent and summed in bfloat16 or wider, within the bound.
No kernel may reach another device: no remote copies, remote signals or barrier semaphores. Data moves between devices by JAX's collectives and lax.ppermute only.
A program may use at most 128 MiB of HBM per device.

v0:
```python
import math

import jax
import jax.numpy as jnp
from jax import lax
from jax.sharding import PartitionSpec as P

DH = 128


def from_behind(x, axis, by):
    peers = lax.axis_size(axis)
    pairs = [(i, i + by) for i in range(peers) if 0 <= i + by < peers]
    return lax.ppermute(x, axis, pairs)


def features(field):
    return jnp.where(field > 0, field + 1.0, jnp.exp(jnp.minimum(field, 0.0)))


def on_device(tokens, w_query, w_key, w_value, w_out, mem_gate, resets):
    tok_rows = tokens.shape[0]
    local_heads = w_query.shape[1] // DH

    def project(weight):
        whole = jnp.dot(tokens, weight, preferred_element_type=jnp.float32).astype(jnp.bfloat16)
        return whole.reshape(tok_rows, local_heads, DH)

    keys_bf = project(w_key)
    vals_bf = project(w_value)
    queries = project(w_query)
    key_feat = features(keys_bf.astype(jnp.float32))
    delta_mem = jnp.einsum(
        "thd,the->hde", key_feat, vals_bf.astype(jnp.float32), precision=lax.Precision.HIGHEST
    )
    delta_norm = jnp.sum(key_feat, axis=0)
    keep_arr = 1.0 - resets.astype(jnp.float32)
    keep_one = keep_arr[0]
    empty_mem = jnp.zeros_like(delta_mem)
    empty_norm = jnp.zeros_like(delta_norm)

    def relay(turn_index, state):
        mem_in, norm_in = state
        return (
            from_behind((keep_one * mem_in + delta_mem).astype(jnp.bfloat16), "seg", 1).astype(
                jnp.float32
            ),
            from_behind((keep_one * norm_in + delta_norm).astype(jnp.bfloat16), "seg", 1).astype(
                jnp.float32
            ),
        )

    mem_prev, norm_prev = lax.fori_loop(0, lax.axis_size("seg") - 1, relay, (empty_mem, empty_norm))
    scores = jnp.einsum(
        "thd,uhd->htu", queries, keys_bf, preferred_element_type=jnp.float32
    ) / math.sqrt(DH)
    row_index = lax.broadcasted_iota(jnp.int32, (tok_rows, tok_rows), 0)
    col_index = lax.broadcasted_iota(jnp.int32, (tok_rows, tok_rows), 1)
    scores = jnp.where((row_index >= col_index)[None], scores, -1e30)
    peak = jnp.max(scores, axis=-1, keepdims=True)
    expo = jnp.exp(scores - peak)
    probs = (expo / jnp.sum(expo, axis=-1, keepdims=True)).astype(jnp.bfloat16)
    local_att = jnp.einsum("htu,uhd->thd", probs, vals_bf, preferred_element_type=jnp.float32)
    read_mem = keep_one * mem_prev
    read_norm = keep_one * norm_prev
    query_feat = features(queries.astype(jnp.float32))
    numer = jnp.einsum("thd,hde->the", query_feat, read_mem, precision=lax.Precision.HIGHEST)
    denom = jnp.maximum(
        jnp.einsum("thd,hd->th", query_feat, read_norm, precision=lax.Precision.HIGHEST), 1.0
    )
    mem_att = numer / denom[..., None]
    gate = jax.nn.sigmoid(mem_gate)[None, :, None]
    attn = (
        (gate * mem_att + (1.0 - gate) * local_att)
        .astype(jnp.bfloat16)
        .reshape(tok_rows, local_heads * DH)
    )
    summed = lax.psum_scatter(
        lax.dot_general(
            w_out, attn, (((0,), (1,)), ((), ())), preferred_element_type=jnp.float32
        ).astype(jnp.bfloat16),
        "tp",
        scatter_dimension=0,
        tiled=True,
    ).astype(jnp.float32)
    return summed.T.astype(jnp.bfloat16)


def solution(mesh):
    placed = (
        P(("dp", "seg"), None),
        P(None, "tp"),
        P(None, "tp"),
        P(None, "tp"),
        P("tp", None),
        P("tp"),
        P(("dp", "seg")),
    )
    return jax.shard_map(
        on_device, mesh=mesh, in_specs=placed, out_specs=P(("dp", "seg"), "tp"), check_vma=False
    )
```

profile of v0, /device:TPU:1, one launch (start us, length us, event | category | flops | bytes accessed | tf_op | source)
XLA Modules:
  0.0 285.0 jit_solution(11552877802072683965)
XLA Ops:
  6.5 0.3 iota_compare_fusion
  6.9 0.0 copy-start.2
  6.9 0.0 copy-start.3
  6.9 7.3 %convolution_convert_fusion.1 = bf16[1024,256]{0,1:T(8,128)(2,1)} fusion(bf16[1024,4096]{1,0:T(8,128)(2,1)} %param.9, bf16[4096,256]{1,0:T(8,128)(2,1)} %param.12), kind=kOutput, calls=%fused_computation.33 | convolution fusion | flops 2147745792 | bytes 11010048 | tf_op jit(solution)/shard_map/dot_general | solution.py:26
  14.2 3.2 %convolution_convert_fusion = bf16[1024,256]{0,1:T(8,128)(2,1)} fusion(bf16[1024,4096]{1,0:T(8,128)(2,1)S(1)} %copy-done.2, bf16[4096,256]{1,0:T(8,128)(2,1)S(1)} %copy-done.3), kind=kOutput, calls=%fused_computation.32 | convolution fusion | flops 2147745792 | bytes 11010048 | tf_op jit(solution)/shard_map/dot_general | solution.py:26
  17.4 3.3 %fusion.22 = (f32[256]{0:T(256)S(1)}, bf16[1024,256]{0,1:T(8,128)(2,1)}) fusion(bf16[1024,4096]{1,0:T(8,128)(2,1)S(1)} %copy-done.2, bf16[4096,256]{1,0:T(8,128)(2,1)S(1)} %copy-done.4), kind=kOutput, calls=%fused_computation.40 | convolution fusion | flops 2149318400 | bytes 11011072 | tf_op jit(solution)/shard_map/dot_general | solution.py:26
  20.7 2.1 copy.11
  22.8 2.1 copy.8
  24.9 7.8 %fusion.48 = (f32[2,1024]{1,0:T(2,128)S(1)}, f32[2,1024,1024]{1,2,0:T(8,128)}) fusion(pred[1024,1024]{0,1:T(8,128)(4,1)S(1)} %iota_compare_fusion, bf16[1024,2,128]{0,2,1:T(8,128)(2,1)} %bitcast.46, bf16[1024,2,128]{0,2,1:T(8,128)(2,1)} %bitcast.48), kind=kOutput, calls=%fused_computation.67 | convolution fusion | flops 545260544 | bytes 10493952 | tf_op jit(solution)/shard_map/sub | solution.py:61
  33.4 2.5 fusion.17
  35.9 156.7 %while.13 = (s32[]{:T(128)}, f32[2,128,128]{2,1,0:T(8,128)S(1)}, f32[2,128]{1,0:T(2,128)S(1)}, f32[]{:T(128)}, f32[2,128,128]{2,1,0:T(8,128)S(1)}, /*index=5*/f32[2,128]{1,0:T(2,128)S(1)}, s32[]{:T(128)}, s32[]{:T(128)}) while((s32[]{:T(128)}, f32[2,128,128]{2,1,0:T(8,128)S(1)}, f32[2,128]{1,0:T(2,128)S(1)}, f32[]{:T(128)}, ...), condition=%wide.region_2.3_spmd.clone, body=%wide.region_1.2_spmd.clone.sunk | while | flops 165123 | bytes 792760 | solution.py:53
  35.9 5.5 %collective-permute-start = (bf16[2,128,128]{2,1,0:T(8,128)(2,1)S(1)}, bf16[2,128,128]{2,1,0:T(8,128)(2,1)S(1)}, u32[]{:S(2)}, u32[]{:S(2)}) collective-permute-start(bf16[2,128,128]{2,1,0:T(8,128)(2,1)S(1)} %fusion.66), channel_id=1, source_target_pairs={{0,16},{16,32},{32,48},{48,64},{64,80},{80,96},{96,112},{112,128},... | collective-permute-start | bytes 196616 | tf_op jit(solution)/shard_map/while/body/eval_jaxpr/ppermute | solution.py:14
  41.4 3.5 %collective-permute-start.1 = (bf16[2,128]{1,0:T(2,128)(2,1)S(1)}, bf16[2,128]{1,0:T(2,128)(2,1)S(1)}, u32[]{:S(2)}, u32[]{:S(2)}) collective-permute-start(bf16[2,128]{1,0:T(2,128)(2,1)S(1)} %fusion.67), channel_id=1, source_target_pairs={{0,16},{16,32},{32,48},{48,64},{64,80},{80,96},{96,112},{112,128},... | collective-permute-start | bytes 1544 | tf_op jit(solution)/shard_map/while/body/eval_jaxpr/ppermute | solution.py:14
  44.9 0.7 collective-permute-done.1
  45.6 0.0 collective-permute-done
  45.7 5.1 %collective-permute-start = (bf16[2,128,128]{2,1,0:T(8,128)(2,1)S(1)}, bf16[2,128,128]{2,1,0:T(8,128)(2,1)S(1)}, u32[]{:S(2)}, u32[]{:S(2)}) collective-permute-start(bf16[2,128,128]{2,1,0:T(8,128)(2,1)S(1)} %fusion.66), channel_id=1, source_target_pairs={{0,16},{16,32},{32,48},{48,64},{64,80},{80,96},{96,112},{112,128},... | collective-permute-start | bytes 196616 | tf_op jit(solution)/shard_map/while/body/eval_jaxpr/ppermute | solution.py:14
  50.8 5.5 %collective-permute-start.1 = (bf16[2,128]{1,0:T(2,128)(2,1)S(1)}, bf16[2,128]{1,0:T(2,128)(2,1)S(1)}, u32[]{:S(2)}, u32[]{:S(2)}) collective-permute-start(bf16[2,128]{1,0:T(2,128)(2,1)S(1)} %fusion.67), channel_id=1, source_target_pairs={{0,16},{16,32},{32,48},{48,64},{64,80},{80,96},{96,112},{112,128},... | collective-permute-start | bytes 1544 | tf_op jit(solution)/shard_map/while/body/eval_jaxpr/ppermute | solution.py:14
  56.4 0.7 collective-permute-done.1
  57.1 0.0 collective-permute-done
  57.2 5.1 %collective-permute-start = (bf16[2,128,128]{2,1,0:T(8,128)(2,1)S(1)}, bf16[2,128,128]{2,1,0:T(8,128)(2,1)S(1)}, u32[]{:S(2)}, u32[]{:S(2)}) collective-permute-start(bf16[2,128,128]{2,1,0:T(8,128)(2,1)S(1)} %fusion.66), channel_id=1, source_target_pairs={{0,16},{16,32},{32,48},{48,64},{64,80},{80,96},{96,112},{112,128},... | collective-permute-start | bytes 196616 | tf_op jit(solution)/shard_map/while/body/eval_jaxpr/ppermute | solution.py:14
  62.3 3.8 %collective-permute-start.1 = (bf16[2,128]{1,0:T(2,128)(2,1)S(1)}, bf16[2,128]{1,0:T(2,128)(2,1)S(1)}, u32[]{:S(2)}, u32[]{:S(2)}) collective-permute-start(bf16[2,128]{1,0:T(2,128)(2,1)S(1)} %fusion.67), channel_id=1, source_target_pairs={{0,16},{16,32},{32,48},{48,64},{64,80},{80,96},{96,112},{112,128},... | collective-permute-start | bytes 1544 | tf_op jit(solution)/shard_map/while/body/eval_jaxpr/ppermute | solution.py:14
  66.1 0.7 collective-permute-done.1
  66.9 5.1 %collective-permute-start = (bf16[2,128,128]{2,1,0:T(8,128)(2,1)S(1)}, bf16[2,128,128]{2,1,0:T(8,128)(2,1)S(1)}, u32[]{:S(2)}, u32[]{:S(2)}) collective-permute-start(bf16[2,128,128]{2,1,0:T(8,128)(2,1)S(1)} %fusion.66), channel_id=1, source_target_pairs={{0,16},{16,32},{32,48},{48,64},{64,80},{80,96},{96,112},{112,128},... | collective-permute-start | bytes 196616 | tf_op jit(solution)/shard_map/while/body/eval_jaxpr/ppermute | solution.py:14
  72.0 5.5 %collective-permute-start.1 = (bf16[2,128]{1,0:T(2,128)(2,1)S(1)}, bf16[2,128]{1,0:T(2,128)(2,1)S(1)}, u32[]{:S(2)}, u32[]{:S(2)}) collective-permute-start(bf16[2,128]{1,0:T(2,128)(2,1)S(1)} %fusion.67), channel_id=1, source_target_pairs={{0,16},{16,32},{32,48},{48,64},{64,80},{80,96},{96,112},{112,128},... | collective-permute-start | bytes 1544 | tf_op jit(solution)/shard_map/while/body/eval_jaxpr/ppermute | solution.py:14
  77.5 0.7 collective-permute-done.1
  78.3 5.4 %collective-permute-start = (bf16[2,128,128]{2,1,0:T(8,128)(2,1)S(1)}, bf16[2,128,128]{2,1,0:T(8,128)(2,1)S(1)}, u32[]{:S(2)}, u32[]{:S(2)}) collective-permute-start(bf16[2,128,128]{2,1,0:T(8,128)(2,1)S(1)} %fusion.66), channel_id=1, source_target_pairs={{0,16},{16,32},{32,48},{48,64},{64,80},{80,96},{96,112},{112,128},... | collective-permute-start | bytes 196616 | tf_op jit(solution)/shard_map/while/body/eval_jaxpr/ppermute | solution.py:14
  83.7 3.2 %collective-permute-start.1 = (bf16[2,128]{1,0:T(2,128)(2,1)S(1)}, bf16[2,128]{1,0:T(2,128)(2,1)S(1)}, u32[]{:S(2)}, u32[]{:S(2)}) collective-permute-start(bf16[2,128]{1,0:T(2,128)(2,1)S(1)} %fusion.67), channel_id=1, source_target_pairs={{0,16},{16,32},{32,48},{48,64},{64,80},{80,96},{96,112},{112,128},... | collective-permute-start | bytes 1544 | tf_op jit(solution)/shard_map/while/body/eval_jaxpr/ppermute | solution.py:14
  86.9 0.7 collective-permute-done.1
  87.7 5.1 %collective-permute-start = (bf16[2,128,128]{2,1,0:T(8,128)(2,1)S(1)}, bf16[2,128,128]{2,1,0:T(8,128)(2,1)S(1)}, u32[]{:S(2)}, u32[]{:S(2)}) collective-permute-start(bf16[2,128,128]{2,1,0:T(8,128)(2,1)S(1)} %fusion.66), channel_id=1, source_target_pairs={{0,16},{16,32},{32,48},{48,64},{64,80},{80,96},{96,112},{112,128},... | collective-permute-start | bytes 196616 | tf_op jit(solution)/shard_map/while/body/eval_jaxpr/ppermute | solution.py:14
  92.9 5.8 %collective-permute-start.1 = (bf16[2,128]{1,0:T(2,128)(2,1)S(1)}, bf16[2,128]{1,0:T(2,128)(2,1)S(1)}, u32[]{:S(2)}, u32[]{:S(2)}) collective-permute-start(bf16[2,128]{1,0:T(2,128)(2,1)S(1)} %fusion.67), channel_id=1, source_target_pairs={{0,16},{16,32},{32,48},{48,64},{64,80},{80,96},{96,112},{112,128},... | collective-permute-start | bytes 1544 | tf_op jit(solution)/shard_map/while/body/eval_jaxpr/ppermute | solution.py:14
  98.7 0.7 collective-permute-done.1
  99.5 5.1 %collective-permute-start = (bf16[2,128,128]{2,1,0:T(8,128)(2,1)S(1)}, bf16[2,128,128]{2,1,0:T(8,128)(2,1)S(1)}, u32[]{:S(2)}, u32[]{:S(2)}) collective-permute-start(bf16[2,128,128]{2,1,0:T(8,128)(2,1)S(1)} %fusion.66), channel_id=1, source_target_pairs={{0,16},{16,32},{32,48},{48,64},{64,80},{80,96},{96,112},{112,128},... | collective-permute-start | bytes 196616 | tf_op jit(solution)/shard_map/while/body/eval_jaxpr/ppermute | solution.py:14
  104.6 4.9 %collective-permute-start.1 = (bf16[2,128]{1,0:T(2,128)(2,1)S(1)}, bf16[2,128]{1,0:T(2,128)(2,1)S(1)}, u32[]{:S(2)}, u32[]{:S(2)}) collective-permute-start(bf16[2,128]{1,0:T(2,128)(2,1)S(1)} %fusion.67), channel_id=1, source_target_pairs={{0,16},{16,32},{32,48},{48,64},{64,80},{80,96},{96,112},{112,128},... | collective-permute-start | bytes 1544 | tf_op jit(solution)/shard_map/while/body/eval_jaxpr/ppermute | solution.py:14
  109.6 0.7 collective-permute-done.1
  110.3 5.1 %collective-permute-start = (bf16[2,128,128]{2,1,0:T(8,128)(2,1)S(1)}, bf16[2,128,128]{2,1,0:T(8,128)(2,1)S(1)}, u32[]{:S(2)}, u32[]{:S(2)}) collective-permute-start(bf16[2,128,128]{2,1,0:T(8,128)(2,1)S(1)} %fusion.66), channel_id=1, source_target_pairs={{0,16},{16,32},{32,48},{48,64},{64,80},{80,96},{96,112},{112,128},... | collective-permute-start | bytes 196616 | tf_op jit(solution)/shard_map/while/body/eval_jaxpr/ppermute | solution.py:14
  115.5 6.0 %collective-permute-start.1 = (bf16[2,128]{1,0:T(2,128)(2,1)S(1)}, bf16[2,128]{1,0:T(2,128)(2,1)S(1)}, u32[]{:S(2)}, u32[]{:S(2)}) collective-permute-start(bf16[2,128]{1,0:T(2,128)(2,1)S(1)} %fusion.67), channel_id=1, source_target_pairs={{0,16},{16,32},{32,48},{48,64},{64,80},{80,96},{96,112},{112,128},... | collective-permute-start | bytes 1544 | tf_op jit(solution)/shard_map/while/body/eval_jaxpr/ppermute | solution.py:14
  121.5 0.7 collective-permute-done.1
  122.3 5.1 %collective-permute-start = (bf16[2,128,128]{2,1,0:T(8,128)(2,1)S(1)}, bf16[2,128,128]{2,1,0:T(8,128)(2,1)S(1)}, u32[]{:S(2)}, u32[]{:S(2)}) collective-permute-start(bf16[2,128,128]{2,1,0:T(8,128)(2,1)S(1)} %fusion.66), channel_id=1, source_target_pairs={{0,16},{16,32},{32,48},{48,64},{64,80},{80,96},{96,112},{112,128},... | collective-permute-start | bytes 196616 | tf_op jit(solution)/shard_map/while/body/eval_jaxpr/ppermute | solution.py:14
  127.4 4.2 %collective-permute-start.1 = (bf16[2,128]{1,0:T(2,128)(2,1)S(1)}, bf16[2,128]{1,0:T(2,128)(2,1)S(1)}, u32[]{:S(2)}, u32[]{:S(2)}) collective-permute-start(bf16[2,128]{1,0:T(2,128)(2,1)S(1)} %fusion.67), channel_id=1, source_target_pairs={{0,16},{16,32},{32,48},{48,64},{64,80},{80,96},{96,112},{112,128},... | collective-permute-start | bytes 1544 | tf_op jit(solution)/shard_map/while/body/eval_jaxpr/ppermute | solution.py:14
  131.6 0.7 collective-permute-done.1
  132.4 5.1 %collective-permute-start = (bf16[2,128,128]{2,1,0:T(8,128)(2,1)S(1)}, bf16[2,128,128]{2,1,0:T(8,128)(2,1)S(1)}, u32[]{:S(2)}, u32[]{:S(2)}) collective-permute-start(bf16[2,128,128]{2,1,0:T(8,128)(2,1)S(1)} %fusion.66), channel_id=1, source_target_pairs={{0,16},{16,32},{32,48},{48,64},{64,80},{80,96},{96,112},{112,128},... | collective-permute-start | bytes 196616 | tf_op jit(solution)/shard_map/while/body/eval_jaxpr/ppermute | solution.py:14
  137.5 3.8 %collective-permute-start.1 = (bf16[2,128]{1,0:T(2,128)(2,1)S(1)}, bf16[2,128]{1,0:T(2,128)(2,1)S(1)}, u32[]{:S(2)}, u32[]{:S(2)}) collective-permute-start(bf16[2,128]{1,0:T(2,128)(2,1)S(1)} %fusion.67), channel_id=1, source_target_pairs={{0,16},{16,32},{32,48},{48,64},{64,80},{80,96},{96,112},{112,128},... | collective-permute-start | bytes 1544 | tf_op jit(solution)/shard_map/while/body/eval_jaxpr/ppermute | solution.py:14
  141.4 0.7 collective-permute-done.1
  142.1 5.1 %collective-permute-start = (bf16[2,128,128]{2,1,0:T(8,128)(2,1)S(1)}, bf16[2,128,128]{2,1,0:T(8,128)(2,1)S(1)}, u32[]{:S(2)}, u32[]{:S(2)}) collective-permute-start(bf16[2,128,128]{2,1,0:T(8,128)(2,1)S(1)} %fusion.66), channel_id=1, source_target_pairs={{0,16},{16,32},{32,48},{48,64},{64,80},{80,96},{96,112},{112,128},... | collective-permute-start | bytes 196616 | tf_op jit(solution)/shard_map/while/body/eval_jaxpr/ppermute | solution.py:14
  147.3 4.1 %collective-permute-start.1 = (bf16[2,128]{1,0:T(2,128)(2,1)S(1)}, bf16[2,128]{1,0:T(2,128)(2,1)S(1)}, u32[]{:S(2)}, u32[]{:S(2)}) collective-permute-start(bf16[2,128]{1,0:T(2,128)(2,1)S(1)} %fusion.67), channel_id=1, source_target_pairs={{0,16},{16,32},{32,48},{48,64},{64,80},{80,96},{96,112},{112,128},... | collective-permute-start | bytes 1544 | tf_op jit(solution)/shard_map/while/body/eval_jaxpr/ppermute | solution.py:14
  151.4 0.7 collective-permute-done.1
  152.2 5.4 %collective-permute-start = (bf16[2,128,128]{2,1,0:T(8,128)(2,1)S(1)}, bf16[2,128,128]{2,1,0:T(8,128)(2,1)S(1)}, u32[]{:S(2)}, u32[]{:S(2)}) collective-permute-start(bf16[2,128,128]{2,1,0:T(8,128)(2,1)S(1)} %fusion.66), channel_id=1, source_target_pairs={{0,16},{16,32},{32,48},{48,64},{64,80},{80,96},{96,112},{112,128},... | collective-permute-start | bytes 196616 | tf_op jit(solution)/shard_map/while/body/eval_jaxpr/ppermute | solution.py:14
  157.6 4.0 %collective-permute-start.1 = (bf16[2,128]{1,0:T(2,128)(2,1)S(1)}, bf16[2,128]{1,0:T(2,128)(2,1)S(1)}, u32[]{:S(2)}, u32[]{:S(2)}) collective-permute-start(bf16[2,128]{1,0:T(2,128)(2,1)S(1)} %fusion.67), channel_id=1, source_target_pairs={{0,16},{16,32},{32,48},{48,64},{64,80},{80,96},{96,112},{112,128},... | collective-permute-start | bytes 1544 | tf_op jit(solution)/shard_map/while/body/eval_jaxpr/ppermute | solution.py:14
  161.6 0.7 collective-permute-done.1
  162.4 5.1 %collective-permute-start = (bf16[2,128,128]{2,1,0:T(8,128)(2,1)S(1)}, bf16[2,128,128]{2,1,0:T(8,128)(2,1)S(1)}, u32[]{:S(2)}, u32[]{:S(2)}) collective-permute-start(bf16[2,128,128]{2,1,0:T(8,128)(2,1)S(1)} %fusion.66), channel_id=1, source_target_pairs={{0,16},{16,32},{32,48},{48,64},{64,80},{80,96},{96,112},{112,128},... | collective-permute-start | bytes 196616 | tf_op jit(solution)/shard_map/while/body/eval_jaxpr/ppermute | solution.py:14
  167.5 4.3 %collective-permute-start.1 = (bf16[2,128]{1,0:T(2,128)(2,1)S(1)}, bf16[2,128]{1,0:T(2,128)(2,1)S(1)}, u32[]{:S(2)}, u32[]{:S(2)}) collective-permute-start(bf16[2,128]{1,0:T(2,128)(2,1)S(1)} %fusion.67), channel_id=1, source_target_pairs={{0,16},{16,32},{32,48},{48,64},{64,80},{80,96},{96,112},{112,128},... | collective-permute-start | bytes 1544 | tf_op jit(solution)/shard_map/while/body/eval_jaxpr/ppermute | solution.py:14
  171.9 0.7 collective-permute-done.1
  172.6 5.1 %collective-permute-start = (bf16[2,128,128]{2,1,0:T(8,128)(2,1)S(1)}, bf16[2,128,128]{2,1,0:T(8,128)(2,1)S(1)}, u32[]{:S(2)}, u32[]{:S(2)}) collective-permute-start(bf16[2,128,128]{2,1,0:T(8,128)(2,1)S(1)} %fusion.66), channel_id=1, source_target_pairs={{0,16},{16,32},{32,48},{48,64},{64,80},{80,96},{96,112},{112,128},... | collective-permute-start | bytes 196616 | tf_op jit(solution)/shard_map/while/body/eval_jaxpr/ppermute | solution.py:14
  177.8 4.1 %collective-permute-start.1 = (bf16[2,128]{1,0:T(2,128)(2,1)S(1)}, bf16[2,128]{1,0:T(2,128)(2,1)S(1)}, u32[]{:S(2)}, u32[]{:S(2)}) collective-permute-start(bf16[2,128]{1,0:T(2,128)(2,1)S(1)} %fusion.67), channel_id=1, source_target_pairs={{0,16},{16,32},{32,48},{48,64},{64,80},{80,96},{96,112},{112,128},... | collective-permute-start | bytes 1544 | tf_op jit(solution)/shard_map/while/body/eval_jaxpr/ppermute | solution.py:14
  181.9 0.7 collective-permute-done.1
  182.6 5.1 %collective-permute-start = (bf16[2,128,128]{2,1,0:T(8,128)(2,1)S(1)}, bf16[2,128,128]{2,1,0:T(8,128)(2,1)S(1)}, u32[]{:S(2)}, u32[]{:S(2)}) collective-permute-start(bf16[2,128,128]{2,1,0:T(8,128)(2,1)S(1)} %fusion.66), channel_id=1, source_target_pairs={{0,16},{16,32},{32,48},{48,64},{64,80},{80,96},{96,112},{112,128},... | collective-permute-start | bytes 196616 | tf_op jit(solution)/shard_map/while/body/eval_jaxpr/ppermute | solution.py:14
  187.8 4.1 %collective-permute-start.1 = (bf16[2,128]{1,0:T(2,128)(2,1)S(1)}, bf16[2,128]{1,0:T(2,128)(2,1)S(1)}, u32[]{:S(2)}, u32[]{:S(2)}) collective-permute-start(bf16[2,128]{1,0:T(2,128)(2,1)S(1)} %fusion.67), channel_id=1, source_target_pairs={{0,16},{16,32},{32,48},{48,64},{64,80},{80,96},{96,112},{112,128},... | collective-permute-start | bytes 1544 | tf_op jit(solution)/shard_map/while/body/eval_jaxpr/ppermute | solution.py:14
  191.9 0.7 collective-permute-done.1
  192.6 2.1 fusion.26
  194.8 4.4 %fusion.14 = f32[1024,2,128]{0,2,1:T(8,128)S(1)} fusion(bf16[1024,2,128]{0,2,1:T(8,128)(2,1)} %bitcast.53, f32[2,1024,1024]{1,2,0:T(8,128)} %get-tuple-element.76, f32[2,1024]{1,0:T(2,128)S(1)} %get-tuple-element.75, f32[2]{0:T(128)S(1)} %get-tuple-element.73), kind=kOutput, calls=%fused_computation.31 | convolution fusion | flops 541327360 | bytes 9969672 | tf_op jit(solution)/shard_map/htu,uhd->thd/dot_general | solution.py:63
  199.2 1.3 fusion.15
  200.5 5.6 %convert_bitcast_fusion = bf16[4096,1024]{0,1:T(8,128)(2,1)} fusion(bf16[1024,256]{0,1:T(8,128)(2,1)S(1)} %bitcast.49, bf16[256,4096]{1,0:T(8,128)(2,1)S(1)} %copy-done), kind=kOutput, calls=%fused_computation.7 | convolution fusion | flops 2151677952 | bytes 11010048 | tf_op jit(solution)/shard_map/dot_general | solution.py:79
  206.1 0.0 reduce-scatter.2.cloned.1.call-update
  206.2 72.0 %reduce-scatter.2.cloned.1.call-done = bf16[512,1024]{0,1:T(8,128)(2,1)} async-done(((bf16[4096,1024]{0,1:T(8,128)(2,1)}), bf16[512,1024]{0,1:T(8,128)(2,1)}) %reduce-scatter.2.cloned.1.call-update) | async-done | bytes 1048592 | tf_op jit(solution)/shard_map/reduce_scatter | solution.py:78
  (89 shorter events, 0.8 us)
Async XLA Ops:
  6.5 194.0 %copy-start = (bf16[256,4096]{1,0:T(8,128)(2,1)S(1)}, bf16[256,4096]{1,0:T(8,128)(2,1)}, u32[]{:S(2)}) copy-start(bf16[256,4096]{1,0:T(8,128)(2,1)} %param.13) | copy-start | bytes 6291460
  6.5 271.6 %reduce-scatter.2.cloned.1.call-start = ((), (), s32[]{:S(2)}) async-start(), calls=%async_computation.1 | async-start | bytes 9437184 | tf_op jit(solution)/shard_map/reduce_scatter | solution.py:78
  6.9 7.3 %copy-start.2 = (bf16[1024,4096]{1,0:T(8,128)(2,1)S(1)}, bf16[1024,4096]{1,0:T(8,128)(2,1)}, u32[]{:S(2)}) copy-start(bf16[1024,4096]{1,0:T(8,128)(2,1)} %param.9) | copy-start | bytes 25165828
  6.9 7.3 %copy-start.3 = (bf16[4096,256]{1,0:T(8,128)(2,1)S(1)}, bf16[4096,256]{1,0:T(8,128)(2,1)}, u32[]{:S(2)}) copy-start(bf16[4096,256]{1,0:T(8,128)(2,1)} %param.10) | copy-start | bytes 6291460
  14.2 3.2 %copy-start.4 = (bf16[4096,256]{1,0:T(8,128)(2,1)S(1)}, bf16[4096,256]{1,0:T(8,128)(2,1)}, u32[]{:S(2)}) copy-start(bf16[4096,256]{1,0:T(8,128)(2,1)} %param.11) | copy-start | bytes 6291460
  24.9 7.8 %copy-start.5 = (f32[2]{0:T(128)S(1)}, f32[2]{0:T(128)}, u32[]{:S(2)}) copy-start(f32[2]{0:T(128)} %param.14) | copy-start | bytes 28
  35.9 9.7 %collective-permute-start = (bf16[2,128,128]{2,1,0:T(8,128)(2,1)S(1)}, bf16[2,128,128]{2,1,0:T(8,128)(2,1)S(1)}, u32[]{:S(2)}, u32[]{:S(2)}) collective-permute-start(bf16[2,128,128]{2,1,0:T(8,128)(2,1)S(1)} %fusion.66), channel_id=1, source_target_pairs={{0,16},{16,32},{32,48},{48,64},{64,80},{80,96},{96,112},{112,128},... | collective-permute-start | bytes 196616 | tf_op jit(solution)/shard_map/while/body/eval_jaxpr/ppermute | solution.py:14
  41.4 4.2 %collective-permute-start.1 = (bf16[2,128]{1,0:T(2,128)(2,1)S(1)}, bf16[2,128]{1,0:T(2,128)(2,1)S(1)}, u32[]{:S(2)}, u32[]{:S(2)}) collective-permute-start(bf16[2,128]{1,0:T(2,128)(2,1)S(1)} %fusion.67), channel_id=1, source_target_pairs={{0,16},{16,32},{32,48},{48,64},{64,80},{80,96},{96,112},{112,128},... | collective-permute-start | bytes 1544 | tf_op jit(solution)/shard_map/while/body/eval_jaxpr/ppermute | solution.py:14
  45.7 11.4 %collective-permute-start = (bf16[2,128,128]{2,1,0:T(8,128)(2,1)S(1)}, bf16[2,128,128]{2,1,0:T(8,128)(2,1)S(1)}, u32[]{:S(2)}, u32[]{:S(2)}) collective-permute-start(bf16[2,128,128]{2,1,0:T(8,128)(2,1)S(1)} %fusion.66), channel_id=1, source_target_pairs={{0,16},{16,32},{32,48},{48,64},{64,80},{80,96},{96,112},{112,128},... | collective-permute-start | bytes 196616 | tf_op jit(solution)/shard_map/while/body/eval_jaxpr/ppermute | solution.py:14
  50.8 6.3 %collective-permute-start.1 = (bf16[2,128]{1,0:T(2,128)(2,1)S(1)}, bf16[2,128]{1,0:T(2,128)(2,1)S(1)}, u32[]{:S(2)}, u32[]{:S(2)}) collective-permute-start(bf16[2,128]{1,0:T(2,128)(2,1)S(1)} %fusion.67), channel_id=1, source_target_pairs={{0,16},{16,32},{32,48},{48,64},{64,80},{80,96},{96,112},{112,128},... | collective-permute-start | bytes 1544 | tf_op jit(solution)/shard_map/while/body/eval_jaxpr/ppermute | solution.py:14
  57.2 9.6 %collective-permute-start = (bf16[2,128,128]{2,1,0:T(8,128)(2,1)S(1)}, bf16[2,128,128]{2,1,0:T(8,128)(2,1)S(1)}, u32[]{:S(2)}, u32[]{:S(2)}) collective-permute-start(bf16[2,128,128]{2,1,0:T(8,128)(2,1)S(1)} %fusion.66), channel_id=1, source_target_pairs={{0,16},{16,32},{32,48},{48,64},{64,80},{80,96},{96,112},{112,128},... | collective-permute-start | bytes 196616 | tf_op jit(solution)/shard_map/while/body/eval_jaxpr/ppermute | solution.py:14
  62.3 4.5 %collective-permute-start.1 = (bf16[2,128]{1,0:T(2,128)(2,1)S(1)}, bf16[2,128]{1,0:T(2,128)(2,1)S(1)}, u32[]{:S(2)}, u32[]{:S(2)}) collective-permute-start(bf16[2,128]{1,0:T(2,128)(2,1)S(1)} %fusion.67), channel_id=1, source_target_pairs={{0,16},{16,32},{32,48},{48,64},{64,80},{80,96},{96,112},{112,128},... | collective-permute-start | bytes 1544 | tf_op jit(solution)/shard_map/while/body/eval_jaxpr/ppermute | solution.py:14
  66.9 11.4 %collective-permute-start = (bf16[2,128,128]{2,1,0:T(8,128)(2,1)S(1)}, bf16[2,128,128]{2,1,0:T(8,128)(2,1)S(1)}, u32[]{:S(2)}, u32[]{:S(2)}) collective-permute-start(bf16[2,128,128]{2,1,0:T(8,128)(2,1)S(1)} %fusion.66), channel_id=1, source_target_pairs={{0,16},{16,32},{32,48},{48,64},{64,80},{80,96},{96,112},{112,128},... | collective-permute-start | bytes 196616 | tf_op jit(solution)/shard_map/while/body/eval_jaxpr/ppermute | solution.py:14
  72.0 6.3 %collective-permute-start.1 = (bf16[2,128]{1,0:T(2,128)(2,1)S(1)}, bf16[2,128]{1,0:T(2,128)(2,1)S(1)}, u32[]{:S(2)}, u32[]{:S(2)}) collective-permute-start(bf16[2,128]{1,0:T(2,128)(2,1)S(1)} %fusion.67), channel_id=1, source_target_pairs={{0,16},{16,32},{32,48},{48,64},{64,80},{80,96},{96,112},{112,128},... | collective-permute-start | bytes 1544 | tf_op jit(solution)/shard_map/while/body/eval_jaxpr/ppermute | solution.py:14
  78.3 9.3 %collective-permute-start = (bf16[2,128,128]{2,1,0:T(8,128)(2,1)S(1)}, bf16[2,128,128]{2,1,0:T(8,128)(2,1)S(1)}, u32[]{:S(2)}, u32[]{:S(2)}) collective-permute-start(bf16[2,128,128]{2,1,0:T(8,128)(2,1)S(1)} %fusion.66), channel_id=1, source_target_pairs={{0,16},{16,32},{32,48},{48,64},{64,80},{80,96},{96,112},{112,128},... | collective-permute-start | bytes 196616 | tf_op jit(solution)/shard_map/while/body/eval_jaxpr/ppermute | solution.py:14
  83.7 3.9 %collective-permute-start.1 = (bf16[2,128]{1,0:T(2,128)(2,1)S(1)}, bf16[2,128]{1,0:T(2,128)(2,1)S(1)}, u32[]{:S(2)}, u32[]{:S(2)}) collective-permute-start(bf16[2,128]{1,0:T(2,128)(2,1)S(1)} %fusion.67), channel_id=1, source_target_pairs={{0,16},{16,32},{32,48},{48,64},{64,80},{80,96},{96,112},{112,128},... | collective-permute-start | bytes 1544 | tf_op jit(solution)/shard_map/while/body/eval_jaxpr/ppermute | solution.py:14
  87.7 11.7 %collective-permute-start = (bf16[2,128,128]{2,1,0:T(8,128)(2,1)S(1)}, bf16[2,128,128]{2,1,0:T(8,128)(2,1)S(1)}, u32[]{:S(2)}, u32[]{:S(2)}) collective-permute-start(bf16[2,128,128]{2,1,0:T(8,128)(2,1)S(1)} %fusion.66), channel_id=1, source_target_pairs={{0,16},{16,32},{32,48},{48,64},{64,80},{80,96},{96,112},{112,128},... | collective-permute-start | bytes 196616 | tf_op jit(solution)/shard_map/while/body/eval_jaxpr/ppermute | solution.py:14
  92.9 6.6 %collective-permute-start.1 = (bf16[2,128]{1,0:T(2,128)(2,1)S(1)}, bf16[2,128]{1,0:T(2,128)(2,1)S(1)}, u32[]{:S(2)}, u32[]{:S(2)}) collective-permute-start(bf16[2,128]{1,0:T(2,128)(2,1)S(1)} %fusion.67), channel_id=1, source_target_pairs={{0,16},{16,32},{32,48},{48,64},{64,80},{80,96},{96,112},{112,128},... | collective-permute-start | bytes 1544 | tf_op jit(solution)/shard_map/while/body/eval_jaxpr/ppermute | solution.py:14
  99.5 10.8 %collective-permute-start = (bf16[2,128,128]{2,1,0:T(8,128)(2,1)S(1)}, bf16[2,128,128]{2,1,0:T(8,128)(2,1)S(1)}, u32[]{:S(2)}, u32[]{:S(2)}) collective-permute-start(bf16[2,128,128]{2,1,0:T(8,128)(2,1)S(1)} %fusion.66), channel_id=1, source_target_pairs={{0,16},{16,32},{32,48},{48,64},{64,80},{80,96},{96,112},{112,128},... | collective-permute-start | bytes 196616 | tf_op jit(solution)/shard_map/while/body/eval_jaxpr/ppermute | solution.py:14
  104.6 5.7 %collective-permute-start.1 = (bf16[2,128]{1,0:T(2,128)(2,1)S(1)}, bf16[2,128]{1,0:T(2,128)(2,1)S(1)}, u32[]{:S(2)}, u32[]{:S(2)}) collective-permute-start(bf16[2,128]{1,0:T(2,128)(2,1)S(1)} %fusion.67), channel_id=1, source_target_pairs={{0,16},{16,32},{32,48},{48,64},{64,80},{80,96},{96,112},{112,128},... | collective-permute-start | bytes 1544 | tf_op jit(solution)/shard_map/while/body/eval_jaxpr/ppermute | solution.py:14
  110.3 11.9 %collective-permute-start = (bf16[2,128,128]{2,1,0:T(8,128)(2,1)S(1)}, bf16[2,128,128]{2,1,0:T(8,128)(2,1)S(1)}, u32[]{:S(2)}, u32[]{:S(2)}) collective-permute-start(bf16[2,128,128]{2,1,0:T(8,128)(2,1)S(1)} %fusion.66), channel_id=1, source_target_pairs={{0,16},{16,32},{32,48},{48,64},{64,80},{80,96},{96,112},{112,128},... | collective-permute-start | bytes 196616 | tf_op jit(solution)/shard_map/while/body/eval_jaxpr/ppermute | solution.py:14
  115.5 6.7 %collective-permute-start.1 = (bf16[2,128]{1,0:T(2,128)(2,1)S(1)}, bf16[2,128]{1,0:T(2,128)(2,1)S(1)}, u32[]{:S(2)}, u32[]{:S(2)}) collective-permute-start(bf16[2,128]{1,0:T(2,128)(2,1)S(1)} %fusion.67), channel_id=1, source_target_pairs={{0,16},{16,32},{32,48},{48,64},{64,80},{80,96},{96,112},{112,128},... | collective-permute-start | bytes 1544 | tf_op jit(solution)/shard_map/while/body/eval_jaxpr/ppermute | solution.py:14
  122.3 10.1 %collective-permute-start = (bf16[2,128,128]{2,1,0:T(8,128)(2,1)S(1)}, bf16[2,128,128]{2,1,0:T(8,128)(2,1)S(1)}, u32[]{:S(2)}, u32[]{:S(2)}) collective-permute-start(bf16[2,128,128]{2,1,0:T(8,128)(2,1)S(1)} %fusion.66), channel_id=1, source_target_pairs={{0,16},{16,32},{32,48},{48,64},{64,80},{80,96},{96,112},{112,128},... | collective-permute-start | bytes 196616 | tf_op jit(solution)/shard_map/while/body/eval_jaxpr/ppermute | solution.py:14
  127.4 4.9 %collective-permute-start.1 = (bf16[2,128]{1,0:T(2,128)(2,1)S(1)}, bf16[2,128]{1,0:T(2,128)(2,1)S(1)}, u32[]{:S(2)}, u32[]{:S(2)}) collective-permute-start(bf16[2,128]{1,0:T(2,128)(2,1)S(1)} %fusion.67), channel_id=1, source_target_pairs={{0,16},{16,32},{32,48},{48,64},{64,80},{80,96},{96,112},{112,128},... | collective-permute-start | bytes 1544 | tf_op jit(solution)/shard_map/while/body/eval_jaxpr/ppermute | solution.py:14
  132.4 9.7 %collective-permute-start = (bf16[2,128,128]{2,1,0:T(8,128)(2,1)S(1)}, bf16[2,128,128]{2,1,0:T(8,128)(2,1)S(1)}, u32[]{:S(2)}, u32[]{:S(2)}) collective-permute-start(bf16[2,128,128]{2,1,0:T(8,128)(2,1)S(1)} %fusion.66), channel_id=1, source_target_pairs={{0,16},{16,32},{32,48},{48,64},{64,80},{80,96},{96,112},{112,128},... | collective-permute-start | bytes 196616 | tf_op jit(solution)/shard_map/while/body/eval_jaxpr/ppermute | solution.py:14
  137.5 4.5 %collective-permute-start.1 = (bf16[2,128]{1,0:T(2,128)(2,1)S(1)}, bf16[2,128]{1,0:T(2,128)(2,1)S(1)}, u32[]{:S(2)}, u32[]{:S(2)}) collective-permute-start(bf16[2,128]{1,0:T(2,128)(2,1)S(1)} %fusion.67), channel_id=1, source_target_pairs={{0,16},{16,32},{32,48},{48,64},{64,80},{80,96},{96,112},{112,128},... | collective-permute-start | bytes 1544 | tf_op jit(solution)/shard_map/while/body/eval_jaxpr/ppermute | solution.py:14
  142.1 10.0 %collective-permute-start = (bf16[2,128,128]{2,1,0:T(8,128)(2,1)S(1)}, bf16[2,128,128]{2,1,0:T(8,128)(2,1)S(1)}, u32[]{:S(2)}, u32[]{:S(2)}) collective-permute-start(bf16[2,128,128]{2,1,0:T(8,128)(2,1)S(1)} %fusion.66), channel_id=1, source_target_pairs={{0,16},{16,32},{32,48},{48,64},{64,80},{80,96},{96,112},{112,128},... | collective-permute-start | bytes 196616 | tf_op jit(solution)/shard_map/while/body/eval_jaxpr/ppermute | solution.py:14
  147.3 4.8 %collective-permute-start.1 = (bf16[2,128]{1,0:T(2,128)(2,1)S(1)}, bf16[2,128]{1,0:T(2,128)(2,1)S(1)}, u32[]{:S(2)}, u32[]{:S(2)}) collective-permute-start(bf16[2,128]{1,0:T(2,128)(2,1)S(1)} %fusion.67), channel_id=1, source_target_pairs={{0,16},{16,32},{32,48},{48,64},{64,80},{80,96},{96,112},{112,128},... | collective-permute-start | bytes 1544 | tf_op jit(solution)/shard_map/while/body/eval_jaxpr/ppermute | solution.py:14
  152.2 10.1 %collective-permute-start = (bf16[2,128,128]{2,1,0:T(8,128)(2,1)S(1)}, bf16[2,128,128]{2,1,0:T(8,128)(2,1)S(1)}, u32[]{:S(2)}, u32[]{:S(2)}) collective-permute-start(bf16[2,128,128]{2,1,0:T(8,128)(2,1)S(1)} %fusion.66), channel_id=1, source_target_pairs={{0,16},{16,32},{32,48},{48,64},{64,80},{80,96},{96,112},{112,128},... | collective-permute-start | bytes 196616 | tf_op jit(solution)/shard_map/while/body/eval_jaxpr/ppermute | solution.py:14
  157.6 4.7 %collective-permute-start.1 = (bf16[2,128]{1,0:T(2,128)(2,1)S(1)}, bf16[2,128]{1,0:T(2,128)(2,1)S(1)}, u32[]{:S(2)}, u32[]{:S(2)}) collective-permute-start(bf16[2,128]{1,0:T(2,128)(2,1)S(1)} %fusion.67), channel_id=1, source_target_pairs={{0,16},{16,32},{32,48},{48,64},{64,80},{80,96},{96,112},{112,128},... | collective-permute-start | bytes 1544 | tf_op jit(solution)/shard_map/while/body/eval_jaxpr/ppermute | solution.py:14
  162.4 10.2 %collective-permute-start = (bf16[2,128,128]{2,1,0:T(8,128)(2,1)S(1)}, bf16[2,128,128]{2,1,0:T(8,128)(2,1)S(1)}, u32[]{:S(2)}, u32[]{:S(2)}) collective-permute-start(bf16[2,128,128]{2,1,0:T(8,128)(2,1)S(1)} %fusion.66), channel_id=1, source_target_pairs={{0,16},{16,32},{32,48},{48,64},{64,80},{80,96},{96,112},{112,128},... | collective-permute-start | bytes 196616 | tf_op jit(solution)/shard_map/while/body/eval_jaxpr/ppermute | solution.py:14
  167.5 5.0 %collective-permute-start.1 = (bf16[2,128]{1,0:T(2,128)(2,1)S(1)}, bf16[2,128]{1,0:T(2,128)(2,1)S(1)}, u32[]{:S(2)}, u32[]{:S(2)}) collective-permute-start(bf16[2,128]{1,0:T(2,128)(2,1)S(1)} %fusion.67), channel_id=1, source_target_pairs={{0,16},{16,32},{32,48},{48,64},{64,80},{80,96},{96,112},{112,128},... | collective-permute-start | bytes 1544 | tf_op jit(solution)/shard_map/while/body/eval_jaxpr/ppermute | solution.py:14
  172.6 9.9 %collective-permute-start = (bf16[2,128,128]{2,1,0:T(8,128)(2,1)S(1)}, bf16[2,128,128]{2,1,0:T(8,128)(2,1)S(1)}, u32[]{:S(2)}, u32[]{:S(2)}) collective-permute-start(bf16[2,128,128]{2,1,0:T(8,128)(2,1)S(1)} %fusion.66), channel_id=1, source_target_pairs={{0,16},{16,32},{32,48},{48,64},{64,80},{80,96},{96,112},{112,128},... | collective-permute-start | bytes 196616 | tf_op jit(solution)/shard_map/while/body/eval_jaxpr/ppermute | solution.py:14
  177.8 4.8 %collective-permute-start.1 = (bf16[2,128]{1,0:T(2,128)(2,1)S(1)}, bf16[2,128]{1,0:T(2,128)(2,1)S(1)}, u32[]{:S(2)}, u32[]{:S(2)}) collective-permute-start(bf16[2,128]{1,0:T(2,128)(2,1)S(1)} %fusion.67), channel_id=1, source_target_pairs={{0,16},{16,32},{32,48},{48,64},{64,80},{80,96},{96,112},{112,128},... | collective-permute-start | bytes 1544 | tf_op jit(solution)/shard_map/while/body/eval_jaxpr/ppermute | solution.py:14
  182.6 9.9 %collective-permute-start = (bf16[2,128,128]{2,1,0:T(8,128)(2,1)S(1)}, bf16[2,128,128]{2,1,0:T(8,128)(2,1)S(1)}, u32[]{:S(2)}, u32[]{:S(2)}) collective-permute-start(bf16[2,128,128]{2,1,0:T(8,128)(2,1)S(1)} %fusion.66), channel_id=1, source_target_pairs={{0,16},{16,32},{32,48},{48,64},{64,80},{80,96},{96,112},{112,128},... | collective-permute-start | bytes 196616 | tf_op jit(solution)/shard_map/while/body/eval_jaxpr/ppermute | solution.py:14
  187.8 4.8 %collective-permute-start.1 = (bf16[2,128]{1,0:T(2,128)(2,1)S(1)}, bf16[2,128]{1,0:T(2,128)(2,1)S(1)}, u32[]{:S(2)}, u32[]{:S(2)}) collective-permute-start(bf16[2,128]{1,0:T(2,128)(2,1)S(1)} %fusion.67), channel_id=1, source_target_pairs={{0,16},{16,32},{32,48},{48,64},{64,80},{80,96},{96,112},{112,128},... | collective-permute-start | bytes 1544 | tf_op jit(solution)/shard_map/while/body/eval_jaxpr/ppermute | solution.py:14
  194.8 4.4 %copy-start.1 = (bf16[1024,2,128]{2,0,1:T(8,128)(2,1)S(1)}, bf16[1024,2,128]{2,0,1:T(8,128)(2,1)}, u32[]{:S(2)}) copy-start(bf16[1024,2,128]{2,0,1:T(8,128)(2,1)} %copy.11) | copy-start | bytes 1572868
Sparse Core Ops, SparseCore 0:
  206.3 71.7 reduce-scatter.1
where the time goes:
time: 286 us; the launch traced here: 285 us
  starting transfers between devices  145 us (51%)
  waiting for transfers between devices  82.6 us (29%)
  matrix products  37.6 us (13%)
  between operations  14.2 us (5%)
  local copies, waits for them, and re-layouts  4.2 us (1%)
    ppermute x30, starting transfers between devices, from_behind(): return lax.ppermute(x, axis, pairs)  145 us
    reduce_scatter x1, waiting for transfers between devices, on_device(): lax.psum_scatter(lax.dot_general(w_out, attn, (((0,), (1,)), ((), ())), p...  72 us
    dot_general x3, matrix products, project(): jnp.dot(tokens, weight, preferred_element_type=jnp.float32)  13.8 us
    ppermute x30, waiting for transfers between devices, from_behind(): return lax.ppermute(x, axis, pairs)  10.6 us
    sub x1, matrix products, on_device(): expo = jnp.exp(scores - peak)  7.81 us
  transfers between devices with their start and end apart: 31, of which 16 were waited for; matrix products, arithmetic and copies ran while one was open for 0% of the time, Pallas kernels for 0%

commit v1 on v0

v1 whole, which is shorter than its diff:
```python
import functools
import math

import jax
import jax.numpy as jnp
from jax import lax
from jax.experimental import pallas as pl
from jax.experimental.pallas import tpu as pltpu
from jax.sharding import PartitionSpec as P


DH = 128
ROWS = DH + 8
BF = jnp.bfloat16
F32 = jnp.float32
MIB = 1 << 20


def features(field):
    return jnp.where(field > 0, field + 1.0, jnp.exp(jnp.minimum(field, 0.0)))


def stay(value):
    return pltpu.with_memory_space_constraint(value, pltpu.HBM)


def dot(a, b, dims=((1,), (0,))):
    return lax.dot_general(a, b, (dims, ((), ())), preferred_element_type=F32)


def call(kernel, out_shape, vmem, flops, moved, exps=0, **kw):
    return pl.pallas_call(
        kernel,
        out_shape=out_shape,
        cost_estimate=pl.CostEstimate(flops=flops, bytes_accessed=moved, transcendentals=exps),
        compiler_params=pltpu.CompilerParams(vmem_limit_bytes=vmem * MIB),
        **kw,
    )


def qkv_kernel(cuts, dp_ref, resets_ref, x_hbm, wq_hbm, wk_hbm, wv_hbm, wo_hbm, q_ref, k_ref, v_ref, s_ref, o_hbm, x_ref, w_ref, acc_ref, o_ref, sem, in_sem, out_sem):
    toks, cols = q_ref.shape
    heads = cols // DH
    copies = []
    for i, (lo, hi) in enumerate(cuts):
        at = slice(lo, hi)
        batch = [pltpu.make_async_copy(x_hbm.at[:, at], x_ref.at[:, at], sem.at[i, 0])]
        for j, w_hbm in enumerate((wk_hbm, wv_hbm, wq_hbm)):
            to = slice(j * cols, (j + 1) * cols)
            batch.append(pltpu.make_async_copy(w_hbm.at[at, :], w_ref.at[at, to], sem.at[i, j + 1]))
        for copy in batch:
            copy.start()
        copies.append(batch)
    pieces, _, slim = o_ref.shape
    wide = wo_hbm.shape[1] // pieces
    packs = []
    for j in range(pieces):
        share = pl.ds(pl.multiple_of(j * wide + dp_ref[0] * slim, slim), slim)
        packs.append(pltpu.make_async_copy(wo_hbm.at[:, share], o_ref.at[j], in_sem.at[j]))
    for copy in packs:
        copy.start()
    part = toks // 8
    for i, (lo, hi) in enumerate(cuts):
        at = slice(lo, hi)
        for copy in copies[i]:
            copy.wait()
        for r in range(8):
            rows = slice(r * part, (r + 1) * part)
            piece = dot(x_ref[rows, at], w_ref[at, :])
            if i == 0:
                acc_ref[rows, :] = piece
            else:
                acc_ref[rows, :] += piece
    moves = [pltpu.make_async_copy(o_ref.at[j], o_hbm.at[j], out_sem.at[j]) for j in range(pieces)]
    for pack, move in zip(packs, moves):
        pack.wait()
        move.start()
    keys = acc_ref[:, :cols].astype(BF)
    vals = acc_ref[:, cols : 2 * cols].astype(BF)
    queries = acc_ref[:, 2 * cols :].astype(BF)
    k_ref[...] = keys
    v_ref[...] = vals
    q_ref[...] = queries
    feat = features(keys.astype(F32))
    norm = jnp.sum(feat, axis=0, keepdims=True)
    feat_bf = feat.astype(BF)
    row = lax.broadcasted_iota(jnp.int32, (8, DH), 0)
    keep = 1.0 - resets_ref[0].astype(F32)
    for h in range(heads):
        at = slice(h * DH, (h + 1) * DH)
        memory = dot(vals[:, at], feat_bf[:, at], ((0,), (0,)))
        tail = jnp.where(row == 0, norm[:, at], keep)
        s_ref[h] = jnp.concatenate([memory, tail], axis=0).astype(BF)
    for move in moves:
        move.wait()


def joined(bit, seg, got, before, flag):
    upper = jnp.where(jnp.bitwise_and(seg, bit) != 0, 1.0, 0.0)
    below = got * before[DH + 1 : DH + 2, :]
    after = jnp.where(flag, below, below + before)
    return upper * after + (1.0 - upper) * before


def merge_kernel(bit, seg_ref, total_ref, got_ref, *rest):
    old_ref, new_ref, before_ref = rest if len(rest) == 3 else (None,) + rest
    flag = lax.broadcasted_iota(jnp.int32, (ROWS, DH), 0) > DH
    upper = jnp.where(jnp.bitwise_and(seg_ref[0], bit) != 0, 1.0, 0.0)
    for h in range(total_ref.shape[0]):
        total, got = total_ref[h].astype(F32), got_ref[h].astype(F32)
        before = jnp.where(flag, 1.0, 0.0) if old_ref is None else old_ref[h]
        before_ref[h] = joined(bit, seg_ref[0], got, before, flag)
        mine, theirs = total[DH + 1 : DH + 2, :], got[DH + 1 : DH + 2, :]
        low_first = upper * (mine * got + total) + (1.0 - upper) * (theirs * total + got)
        new_ref[h] = jnp.where(flag, got * total, low_first).astype(BF)


def attend_kernel(q_ref, k_ref, v_ref, o_ref, wide_ref):
    toks = q_ref.shape[0]
    tile = 256
    scale = math.log2(math.e) / math.sqrt(DH)
    row = lax.broadcasted_iota(jnp.int32, (tile, tile), 0)
    col = lax.broadcasted_iota(jnp.int32, (tile, tile), 1)
    wide_ref[:, :DH] = v_ref[...]
    wide_ref[:, DH:] = jnp.ones((toks, DH), BF)
    for i in range(toks // tile):
        at = slice(i * tile, (i + 1) * tile)
        q = q_ref[at, :]
        diag = jnp.where(row >= col, dot(q, k_ref[at, :], ((1,), (1,))), -1e30)
        peak = jnp.max(diag, axis=-1, keepdims=True)
        if i:
            past = dot(q, k_ref[: i * tile, :], ((1,), (1,)))
            peak = jnp.maximum(peak, jnp.max(past, axis=-1, keepdims=True))
        out = dot(jnp.exp2((diag - peak) * scale).astype(BF), wide_ref[at, :])
        if i:
            out = out + dot(jnp.exp2((past - peak) * scale).astype(BF), wide_ref[: i * tile, :])
        o_ref[at, :] = out[:, :DH] / out[:, DH:]


def read_kernel(bit, seg_ref, resets_ref, gate_ref, q_ref, got_ref, before_ref, *rest):
    local_refs, top_ref, low_ref = rest[:-2], rest[-2], rest[-1]
    half = top_ref.shape[0]
    flag = lax.broadcasted_iota(jnp.int32, (ROWS, DH), 0) > DH
    keep = 1.0 - resets_ref[0].astype(F32)
    for h, l_ref in enumerate(local_refs):
        at = slice(h * DH, (h + 1) * DH)
        state = (keep * joined(bit, seg_ref[0], got_ref[h].astype(F32), before_ref[h], flag)).astype(BF)
        gate = 1.0 / (1.0 + jnp.exp(-jnp.full((1, DH), gate_ref[h], F32)))
        got = dot(features(q_ref[:, at].astype(F32)).astype(BF), state, ((1,), (1,)))
        part = gate[:, :1] / jnp.maximum(got[:, DH : DH + 1], 1.0)
        mixed = (got[:, :DH] * part + (1.0 - gate) * l_ref[...]).astype(BF)
        top_ref[:, at] = mixed[:half]
        low_ref[:, at] = mixed[half:]


def source(at_ref, shift, flip, size):
    j = jnp.bitwise_and(at_ref[0] + shift, size - 1)
    return jnp.bitwise_xor(j, 1) if flip else j


def project_kernel(plan, chained, reach, at_ref, w_hbm, *rest):
    values, rest = rest[: len(plan)], rest[len(plan) :]
    if chained:
        acc_ref, rest = rest[0], rest[1:]
    if reach:
        o_ref, far_ref, w_ref, sem, far_sem = rest
    else:
        o_ref, w_ref, sem = rest
    size = w_hbm.shape[0]
    half = values[0].shape[0]
    places = []
    for _, shift, flip in plan:
        if (shift, flip) not in places:
            places.append((shift, flip))
    copies = [
        pltpu.make_async_copy(w_hbm.at[source(at_ref, *where, size)], w_ref.at[i], sem.at[i])
        for i, where in enumerate(places)
    ]
    late = []
    if reach:
        late = [
            pltpu.make_async_copy(w_hbm.at[source(at_ref, 4, i == 1, size)], far_ref.at[i], far_sem.at[i])
            for i in range(2)
        ]
    for copy in copies + late:
        copy.start()
    for copy in copies:
        copy.wait()
    for side in range(2):
        rows = slice(side * half, (side + 1) * half)
        total = acc_ref[rows, :] if chained else None
        for value, (place, shift, flip) in zip(values, plan):
            if place == side:
                term = dot(value[...], w_ref[places.index((shift, flip))])
                total = term if total is None else total + term
        o_ref[rows, :] = total
    for copy in late:
        copy.wait()


def finish_kernel(dp_ref, mine_ref, twin_ref, acc_mine_ref, acc_twin_ref, top_ref, top_swap_ref, low_ref, low_swap_ref, o_ref):
    half = o_ref.shape[0]
    slim = mine_ref.shape[2]
    for side, parts in enumerate(((top_ref, top_swap_ref), (low_ref, low_swap_ref))):

        @pl.when(pl.program_id(0) == side)
        def _():
            rows = slice(side * half, (side + 1) * half)
            for index, w_ref, acc_ref in ((dp_ref[0], mine_ref, acc_mine_ref), (1 - dp_ref[0], twin_ref, acc_twin_ref)):
                total = acc_ref[rows, :]
                for i, part in enumerate(parts):
                    total = total + dot(part[...], w_ref[i])
                o_ref[:, pl.ds(pl.multiple_of(index * slim, slim), slim)] = total.astype(BF)


def on_device(tokens, w_query, w_key, w_value, w_out, mem_gate, resets):
    toks, width = tokens.shape
    cols = w_query.shape[1]
    heads = cols // DH
    half = toks // 2
    n_tp = lax.axis_size("tp")
    n_seg = lax.axis_size("seg")
    tp = lax.axis_index("tp")
    seg = lax.axis_index("seg")
    out_cols = w_out.shape[1] // n_tp

    n_dp = lax.axis_size("dp")
    twin = lax.axis_index("dp").astype(jnp.int32).reshape(1)
    place = tp.astype(jnp.int32).reshape(1)
    slim = out_cols // n_dp
    spot = seg.astype(jnp.int32).reshape(1)

    smem = pl.BlockSpec(memory_space=pltpu.SMEM)
    remote = pl.BlockSpec(memory_space=pltpu.HBM)
    whole = pl.BlockSpec(memory_space=pltpu.VMEM)

    edges = [0, 512, 1536, 2816, 4096]
    cuts = tuple(zip(edges[:-1], edges[1:]))
    flat = jax.ShapeDtypeStruct((toks, cols), BF)
    payload = jax.ShapeDtypeStruct((heads, ROWS, DH), BF)
    operands = (tokens, w_query, w_key, w_value, w_out)
    queries, keys, vals, state, w_cut = call(
        functools.partial(qkv_kernel, cuts),
        (flat, flat, flat, payload, jax.ShapeDtypeStruct((n_tp, cols, slim), BF)),
        36,
        6 * toks * width * cols,
        2 * (toks * width + 3 * width * cols + 4 * toks * cols),
        in_specs=[smem] * 2 + [remote] * 5,
        out_specs=(whole,) * 4 + (remote,),
        scratch_shapes=[
            pltpu.VMEM((toks, width), BF),
            pltpu.VMEM((width, 3 * cols), BF),
            pltpu.VMEM((toks, 3 * cols), F32),
            pltpu.VMEM((n_tp, cols, slim), BF),
            pltpu.SemaphoreType.DMA((len(cuts), 4)),
            pltpu.SemaphoreType.DMA((n_tp,)),
            pltpu.SemaphoreType.DMA((n_tp,)),
        ],
        name="qkv",
    )(twin, resets, *(stay(a) for a in operands))

    def attend(h):
        spec = pl.BlockSpec((toks, DH), lambda i: (0, h))
        return call(
            attend_kernel,
            jax.ShapeDtypeStruct((toks, DH), F32),
            10,
            4 * toks * toks * DH,
            10 * toks * DH,
            toks * toks,
            grid=(1,),
            in_specs=[spec] * 3,
            out_specs=pl.BlockSpec((toks, DH), lambda i: (0, 0)),
            scratch_shapes=[pltpu.VMEM((toks, 2 * DH), BF)],
            name="attend",
        )(queries, keys, vals)

    w_mine = stay(lax.all_to_all(stay(w_cut), "tp", 0, 0, tiled=True))
    w_twin = stay(lax.ppermute(w_mine, "dp", [(i, n_dp - 1 - i) for i in range(n_dp)]))

    local = []
    for h in range(heads):
        local.append(attend(h))

    total, before, bit, step = state, [], 1, 0
    while True:
        last = 2 * bit == n_seg
        if last:
            pairs = [(i, (n_seg // 2 - 1 - i // 2) * 2 + i % 2) for i in range(n_seg)]
        else:
            pairs = [(i, i ^ bit) for i in range(n_seg)]
        got = lax.ppermute(total, "seg", pairs)
        if last:
            break
        total, kept = call(
            functools.partial(merge_kernel, bit),
            (payload, jax.ShapeDtypeStruct(payload.shape, F32)),
            4,
            10 * heads * ROWS * DH,
            14 * heads * ROWS * DH,
            in_specs=[smem] + [whole] * (2 + len(before)),
            out_specs=(whole, whole),
            name="merge",
        )(spot, total, got, *before)
        before = [kept]
        bit *= 2
        step += 1

    row_half = jax.ShapeDtypeStruct((half, cols), BF)
    top, low = call(
        functools.partial(read_kernel, bit),
        (row_half, row_half),
        10,
        4 * toks * DH * cols,
        8 * toks * cols,
        in_specs=[smem] * 3 + [whole] * (3 + heads),
        out_specs=(whole, whole),
        name="read",
    )(spot, resets, mem_gate, queries, got, before[0], *local)

    def along(value, by):
        return lax.ppermute(value, "tp", [(i, (i + 2 * by) % n_tp) for i in range(n_tp)])

    def swap(value):
        return lax.ppermute(value, "tp", [(i, i ^ 1) for i in range(n_tp)])

    below_top, above_low = along(top, 1), along(low, -1)
    below_low, above_top = along(low, 1), along(top, -1)
    far_top, far_low = along(below_top, 1), along(above_low, -1)

    def pair(value, side, shift):
        return [(value, (side, shift, False)), (swap(value), (side, shift, True))]

    early = pair(top, 0, 0) + pair(low, 1, 0) + pair(below_top, 0, -2) + pair(above_low, 1, 2)
    second = pair(below_low, 1, -2) + pair(above_top, 0, 2)

    def project(parts, weights, acc, reach):
        values, plan = zip(*parts)
        places = len({where[1:] for where in plan})
        out = (jax.ShapeDtypeStruct((toks, slim), F32), jax.ShapeDtypeStruct((2, cols, slim), BF))
        return call(
            functools.partial(project_kernel, plan, acc is not None, reach),
            out if reach else out[0],
            14,
            2 * len(values) * half * cols * slim,
            2 * len(values) * half * cols + 6 * toks * slim,
            in_specs=[smem, remote] + [whole] * (len(values) + (acc is not None)),
            out_specs=(whole, whole) if reach else whole,
            scratch_shapes=[pltpu.VMEM((places, cols, slim), BF), pltpu.SemaphoreType.DMA((places,))]
            + [pltpu.SemaphoreType.DMA((2,))] * reach,
            name="project",
        )(place, weights, *values, *([] if acc is None else [acc]))

    acc_mine = project(early, w_mine, None, False)
    acc_mine, far_mine = project(second, w_mine, acc_mine, True)
    acc_twin, far_twin = project(early + second, w_twin, None, True)
    return call(
        finish_kernel,
        jax.ShapeDtypeStruct((toks, out_cols), BF),
        10,
        4 * toks * cols * out_cols,
        2 * toks * cols + 6 * toks * out_cols,
        grid=(2,),
        in_specs=[smem] + [whole] * 8,
        out_specs=pl.BlockSpec((half, out_cols), lambda i: (i, 0)),
        name="finish",
    )(twin, far_mine, far_twin, acc_mine, acc_twin, far_top, swap(far_top), far_low, swap(far_low))


def solution(mesh):
    placed = (
        P(("dp", "seg"), None),
        P(None, "tp"),
        P(None, "tp"),
        P(None, "tp"),
        P("tp", None),
        P("tp"),
        P(("dp", "seg")),
    )

    return jax.shard_map(on_device, mesh=mesh, in_specs=placed, out_specs=P(("dp", "seg"), "tp"), check_vma=False)
```

time: 286 us -> 77.7 us (0.27)
  starting transfers between devices: 145 us -> 37.5 us
  waiting for transfers between devices: 82.6 us -> 15.3 us
  matrix products: 37.6 us -> 0 us
  Pallas kernels: 0 us -> 23.9 us
  between operations: 14.2 us -> 0.79 us
  local copies, waits for them, and re-layouts: 4.2 us -> 0.01 us
    ppermute x30 -> x19, starting transfers between devices: 145 us -> 30.2 us  [the longest x8 11.5 us: swap(): return lax.ppermute(value, 'tp', [(i, i ^ 1) for i in range(n_tp)])]
    reduce_scatter x1 -> x0, waiting for transfers between devices: 72 us -> none  [on_device(): lax.psum_scatter(lax.dot_general(w_out, attn, (((0,), (1,)), ((), ())), p...]
    dot_general x8 -> x0, matrix products: 29.8 us -> none  [the longest x3 13.8 us: project(): jnp.dot(tokens, weight, preferred_element_type=jnp.float32)]
    pallas_call x0 -> x11, Pallas kernels: none -> 23.9 us  [the longest x1 9.93 us: on_device(): call(functools.partial(qkv_kernel, cuts), (flat, flat, flat, payload, jax...]
    sub x1 -> x0, matrix products: 7.81 us -> none  [on_device(): expo = jnp.exp(scores - peak)]
    all_to_all x0 -> x1, starting transfers between devices: none -> 7.35 us  [on_device(): w_mine = stay(lax.all_to_all(stay(w_cut), 'tp', 0, 0, tiled=True))]
    ppermute x30 -> x19, waiting for transfers between devices: 10.6 us -> 15.3 us  [the longest x4 9.28 us: on_device(): got = lax.ppermute(total, 'seg', pairs)]
    reshape x2 -> x0, local copies, waits for them, and re-layouts: 4.17 us -> none  [project(): return whole.reshape(tok_rows, local_heads, DH)]
  transfers between devices with their start and end apart: 31 -> 20, of which waited for: 16 -> 5; matrix products, arithmetic and copies ran while one was open for 0% -> 0% of each run, Pallas kernels for 0% -> 14%
where the time goes in v1:
time: 77.7 us; the launch traced here: 77.5 us
  starting transfers between devices  37.5 us (48%)
  Pallas kernels  23.9 us (31%)
  waiting for transfers between devices  15.3 us (20%)
  between operations  0.79 us (1%)
    ppermute x8, starting transfers between devices, swap(): return lax.ppermute(value, 'tp', [(i, i ^ 1) for i in range(n_tp)])  11.5 us
    pallas_call x1, Pallas kernels, on_device(): call(functools.partial(qkv_kernel, cuts), (flat, flat, flat, payload, jax...  9.93 us
    ppermute x4, starting transfers between devices, on_device(): got = lax.ppermute(total, 'seg', pairs)  9.29 us
    ppermute x4, waiting for transfers between devices, on_device(): got = lax.ppermute(total, 'seg', pairs)  9.28 us
    ppermute x6, starting transfers between devices, along(): lax.ppermute(value, 'tp', [(i, (i + 2 * by) % n_tp) for i in range(n_tp)])  8.18 us
    all_to_all x1, starting transfers between devices, on_device(): w_mine = stay(lax.all_to_all(stay(w_cut), 'tp', 0, 0, tiled=True))  7.35 us
    ppermute x6, waiting for transfers between devices, along(): lax.ppermute(value, 'tp', [(i, (i + 2 * by) % n_tp) for i in range(n_tp)])  5.97 us
    pallas_call x3, Pallas kernels, project(): call(functools.partial(project_kernel, plan, acc is not None, reach), out...  5.93 us
  transfers between devices with their start and end apart: 20, of which 5 were waited for; matrix products, arithmetic and copies ran while one was open for 0% of the time, Pallas kernels for 14%

profile of v1, /device:TPU:1, one launch (start us, length us, event | category | flops | bytes accessed | tf_op | source)
XLA Modules:
  0.0 77.5 jit_solution(7819982487833144199)
XLA Ops:
  0.7 9.9 %qkv.1 = (bf16[1024,256]{1,0:T(8,128)(2,1)S(1)}, bf16[1024,256]{1,0:T(8,128)(2,1)S(1)}, bf16[1024,256]{1,0:T(8,128)(2,1)S(1)}, bf16[2,136,128]{2,1,0:T(8,128)(2,1)S(1)}, bf16[8,256,256]{2,1,0:T(8,128)(2,1)}) custom-call(s32[1]{0:T(128)} %bitcast.dp_ref, s32[1]{0:T(128)S(6)} %copy.8.resets_ref, bf16[1024,4096]{1,0:T(8,128)(2,1)} %x_hbm.1, ...), custom_call_target="tpu_custom_call" | custom-call | flops 6442450944 | bytes 16777216 | tf_op jit(solution)/shard_map/qkv/pallas_call | solution.py:242
  10.6 7.3 %all-to-all-start = ((bf16[8,256,256]{2,1,0:T(8,128)(2,1)}), bf16[8,256,256]{2,1,0:T(8,128)(2,1)}, u32[]{:S(2)}, u32[]{:S(2)}) async-start(bf16[8,256,256]{2,1,0:T(8,128)(2,1)} %get-tuple-element.22), calls=%async_computation | async-start | bytes 2097152 | tf_op jit(solution)/shard_map/all_to_all | solution.py:278
  17.9 1.4 %collective-permute-start = (bf16[2,136,128]{2,1,0:T(8,128)(2,1)S(1)}, bf16[2,136,128]{2,1,0:T(8,128)(2,1)S(1)}, u32[]{:S(2)}, u32[]{:S(2)}) collective-permute-start(bf16[2,136,128]{2,1,0:T(8,128)(2,1)S(1)} %get-tuple-element.24.total_ref), channel_id=1, source_target_pairs={{0,16},{16,0},{32,48},{48,32},{64,80},{80,64},{96,112},{112,96},{1... | collective-permute-start | bytes 208904 | tf_op jit(solution)/shard_map/ppermute | solution.py:292
  19.3 3.8 %collective-permute-done.got_ref = bf16[2,136,128]{2,1,0:T(8,128)(2,1)S(1)} collective-permute-done((bf16[2,136,128]{2,1,0:T(8,128)(2,1)S(1)}, bf16[2,136,128]{2,1,0:T(8,128)(2,1)S(1)}, u32[]{:S(2)}, u32[]{:S(2)}) %collective-permute-start) | collective-permute-done | bytes 69664 | tf_op jit(solution)/shard_map/ppermute | solution.py:292
  23.1 0.1 merge.3
  23.1 0.6 collective-permute-start.1
  23.7 3.1 %collective-permute-done.1.got_ref = bf16[2,136,128]{2,1,0:T(8,128)(2,1)S(1)} collective-permute-done((bf16[2,136,128]{2,1,0:T(8,128)(2,1)S(1)}, bf16[2,136,128]{2,1,0:T(8,128)(2,1)S(1)}, u32[]{:S(2)}, u32[]{:S(2)}) %collective-permute-start.1) | collective-permute-done | bytes 69664 | tf_op jit(solution)/shard_map/ppermute | solution.py:292
  26.8 0.1 merge.4
  26.9 2.1 %collective-permute-start.2 = (bf16[2,136,128]{2,1,0:T(8,128)(2,1)S(1)}, bf16[2,136,128]{2,1,0:T(8,128)(2,1)S(1)}, u32[]{:S(2)}, u32[]{:S(2)}) collective-permute-start(bf16[2,136,128]{2,1,0:T(8,128)(2,1)S(1)} %get-tuple-element.27.total_ref), channel_id=1, source_target_pairs={{0,64},{16,80},{32,96},{48,112},{64,0},{80,16},{96,32},{112,48},{1... | collective-permute-start | bytes 208904 | tf_op jit(solution)/shard_map/ppermute | solution.py:292
  29.0 2.4 %collective-permute-done.2.got_ref = bf16[2,136,128]{2,1,0:T(8,128)(2,1)S(1)} collective-permute-done((bf16[2,136,128]{2,1,0:T(8,128)(2,1)S(1)}, bf16[2,136,128]{2,1,0:T(8,128)(2,1)S(1)}, u32[]{:S(2)}, u32[]{:S(2)}) %collective-permute-start.2) | collective-permute-done | bytes 69664 | tf_op jit(solution)/shard_map/ppermute | solution.py:292
  31.4 0.1 merge.5
  31.5 5.2 %collective-permute-start.3 = (bf16[2,136,128]{2,1,0:T(8,128)(2,1)S(1)}, bf16[2,136,128]{2,1,0:T(8,128)(2,1)S(1)}, u32[]{:S(2)}, u32[]{:S(2)}) collective-permute-start(bf16[2,136,128]{2,1,0:T(8,128)(2,1)S(1)} %get-tuple-element.29), channel_id=1, source_target_pairs={{0,224},{16,240},{32,192},{48,208},{64,160},{80,176},{96,128},{112... | collective-permute-start | bytes 208904 | tf_op jit(solution)/shard_map/ppermute | solution.py:292
  36.7 0.0 all-to-all-done.w_hbm
  36.7 1.2 %collective-permute-start.14 = (bf16[8,256,256]{2,1,0:T(8,128)(2,1)}, bf16[8,256,256]{2,1,0:T(8,128)(2,1)}, u32[]{:S(2)}, u32[]{:S(2)}) collective-permute-start(bf16[8,256,256]{2,1,0:T(8,128)(2,1)} %all-to-all-done.w_hbm), channel_id=1, source_target_pairs={{0,1},{1,0},{2,3},{3,2},{4,5},{5,4},{6,7},{7,6},{8,9},{9,8},{10,11... | collective-permute-start | bytes 3145736 | tf_op jit(solution)/shard_map/ppermute | solution.py:279
  37.9 0.0 copy-start
  38.0 1.9 %attend.3.rest_1_ = f32[1024,128]{1,0:T(8,128)S(1)} custom-call(bf16[1024,256]{1,0:T(8,128)(2,1)S(1)} %get-tuple-element.23.q_ref, bf16[1024,256]{1,0:T(8,128)(2,1)S(1)} %get-tuple-element.31.k_ref, bf16[1024,256]{1,0:T(8,128)(2,1)S(1)} %get-tuple-element.32.v_ref), custom_call_target="tpu_custom_call" | custom-call | flops 536870912 | bytes 1310720 | tf_op jit(solution)/shard_map/attend/pallas_call | solution.py:264
  39.8 1.9 %attend.2.rest_0_ = f32[1024,128]{1,0:T(8,128)S(1)} custom-call(bf16[1024,256]{1,0:T(8,128)(2,1)S(1)} %get-tuple-element.23.q_ref, bf16[1024,256]{1,0:T(8,128)(2,1)S(1)} %get-tuple-element.31.k_ref, bf16[1024,256]{1,0:T(8,128)(2,1)S(1)} %get-tuple-element.32.v_ref), custom_call_target="tpu_custom_call" | custom-call | flops 536870912 | bytes 1310720 | tf_op jit(solution)/shard_map/attend/pallas_call | solution.py:264
  41.7 0.0 collective-permute-done.3.got_ref
  41.7 0.0 copy-done
  41.7 1.2 %read.1 = (bf16[512,256]{1,0:T(8,128)(2,1)S(1)}, bf16[512,256]{1,0:T(8,128)(2,1)S(1)}) custom-call(s32[1]{0:T(128)} %bitcast.2.seg_ref, s32[1]{0:T(128)S(6)} %copy.8.resets_ref, f32[2]{0:T(128)S(1)} %copy-done, bf16[1024,256]{1,0:T(8,128)(2,1)S(1)} %get-tuple-element.23.q_ref, bf16[2,136,128]{2,1,0:T(8,128)(2,1)S(1)} %collective-permute-done.3.got_ref, ...), custom_call_target="tpu_custom_call" | custom-call | flops 134217728 | bytes 2097152 | tf_op jit(solution)/shard_map/read/pallas_call | solution.py:310
  42.9 1.2 %collective-permute-start.10 = (bf16[512,256]{1,0:T(8,128)(2,1)S(1)}, bf16[512,256]{1,0:T(8,128)(2,1)S(1)}, u32[]{:S(2)}, u32[]{:S(2)}) collective-permute-start(bf16[512,256]{1,0:T(8,128)(2,1)S(1)} %get-tuple-element.34.rest_0_), channel_id=1, source_target_pairs={{0,4},{2,6},{4,8},{6,10},{8,12},{10,14},{12,0},{14,2},{1,5},{3,7},... | collective-permute-start | bytes 786440 | tf_op jit(solution)/shard_map/ppermute | solution.py:322
  44.1 1.6 %collective-permute-start.12 = (bf16[512,256]{1,0:T(8,128)(2,1)S(1)}, bf16[512,256]{1,0:T(8,128)(2,1)S(1)}, u32[]{:S(2)}, u32[]{:S(2)}) collective-permute-start(bf16[512,256]{1,0:T(8,128)(2,1)S(1)} %get-tuple-element.33.rest_2_), channel_id=1, source_target_pairs={{0,12},{2,14},{4,0},{6,2},{8,4},{10,6},{12,8},{14,10},{1,13},{3,15... | collective-permute-start | bytes 786440 | tf_op jit(solution)/shard_map/ppermute | solution.py:322
  45.7 0.0 collective-permute-start.4
  45.7 2.7 %collective-permute-start.6 = (bf16[512,256]{1,0:T(8,128)(2,1)S(1)}, bf16[512,256]{1,0:T(8,128)(2,1)S(1)}, u32[]{:S(2)}, u32[]{:S(2)}) collective-permute-start(bf16[512,256]{1,0:T(8,128)(2,1)S(1)} %get-tuple-element.34.rest_0_), channel_id=1, source_target_pairs={{0,12},{2,14},{4,0},{6,2},{8,4},{10,6},{12,8},{14,10},{1,13},{3,15... | collective-permute-start | bytes 786440 | tf_op jit(solution)/shard_map/ppermute | solution.py:322
  48.3 1.1 %collective-permute-done.10.rest_4_ = bf16[512,256]{1,0:T(8,128)(2,1)S(1)} collective-permute-done((bf16[512,256]{1,0:T(8,128)(2,1)S(1)}, bf16[512,256]{1,0:T(8,128)(2,1)S(1)}, u32[]{:S(2)}, u32[]{:S(2)}) %collective-permute-start.10) | collective-permute-done | bytes 262176 | tf_op jit(solution)/shard_map/ppermute | solution.py:322
  49.4 6.3 %collective-permute-start.8 = (bf16[512,256]{1,0:T(8,128)(2,1)S(1)}, bf16[512,256]{1,0:T(8,128)(2,1)S(1)}, u32[]{:S(2)}, u32[]{:S(2)}) collective-permute-start(bf16[512,256]{1,0:T(8,128)(2,1)S(1)} %get-tuple-element.34.rest_0_), channel_id=1, source_target_pairs={{0,2},{2,0},{4,6},{6,4},{8,10},{10,8},{12,14},{14,12},{1,3},{3,1},... | collective-permute-start | bytes 786440 | tf_op jit(solution)/shard_map/ppermute | solution.py:325
  55.7 0.0 collective-permute-done.12.rest_6_
  55.7 0.0 collective-permute-start.9
  55.7 0.0 collective-permute-done.4.rest_0_.rest_8_
  55.7 2.8 %collective-permute-start.11 = (bf16[512,256]{1,0:T(8,128)(2,1)S(1)}, bf16[512,256]{1,0:T(8,128)(2,1)S(1)}, u32[]{:S(2)}, u32[]{:S(2)}) collective-permute-start(bf16[512,256]{1,0:T(8,128)(2,1)S(1)} %collective-permute-done.10.rest_4_), channel_id=1, source_target_pairs={{0,2},{2,0},{4,6},{6,4},{8,10},{10,8},{12,14},{14,12},{1,3},{3,1},... | collective-permute-start | bytes 786440 | tf_op jit(solution)/shard_map/ppermute | solution.py:325
  58.5 0.0 collective-permute-done.6.rest_2_.rest_10_
  58.5 0.0 collective-permute-start.13
  58.5 0.0 collective-permute-done.8.rest_1_
  58.5 0.3 collective-permute-start.15
  58.8 0.0 collective-permute-done.9.rest_3_
  58.8 2.5 %collective-permute-start.17 = (bf16[512,256]{1,0:T(8,128)(2,1)S(1)}, bf16[512,256]{1,0:T(8,128)(2,1)}, u32[]{:S(2)}, u32[]{:S(2)}) collective-permute-start(bf16[512,256]{1,0:T(8,128)(2,1)S(1)} %collective-permute-done.12.rest_6_), channel_id=1, source_target_pairs={{0,12},{2,14},{4,0},{6,2},{8,4},{10,6},{12,8},{14,10},{1,13},{3,15... | collective-permute-start | bytes 786440 | tf_op jit(solution)/shard_map/ppermute | solution.py:322
  61.3 0.0 collective-permute-done.11.rest_5_
  61.3 1.0 %collective-permute-start.5 = (bf16[512,256]{1,0:T(8,128)(2,1)S(1)}, bf16[512,256]{1,0:T(8,128)(2,1)S(1)}, u32[]{:S(2)}, u32[]{:S(2)}) collective-permute-start(bf16[512,256]{1,0:T(8,128)(2,1)S(1)} %collective-permute-done.4.rest_0_.rest_8_), channel_id=1, source_target_pairs={{0,2},{2,0},{4,6},{6,4},{8,10},{10,8},{12,14},{14,12},{1,3},{3,1},... | collective-permute-start | bytes 786440 | tf_op jit(solution)/shard_map/ppermute | solution.py:325
  62.3 0.0 collective-permute-done.13.rest_7_
  62.3 0.1 collective-permute-start.7
  62.4 4.9 %collective-permute-done.15.top_ref = bf16[512,256]{1,0:T(8,128)(2,1)S(1)} collective-permute-done((bf16[512,256]{1,0:T(8,128)(2,1)S(1)}, bf16[512,256]{1,0:T(8,128)(2,1)S(1)}, u32[]{:S(2)}, u32[]{:S(2)}) %collective-permute-start.15) | collective-permute-done | bytes 262176 | tf_op jit(solution)/shard_map/ppermute | solution.py:322
  67.3 1.3 %collective-permute-start.16 = (bf16[512,256]{1,0:T(8,128)(2,1)S(1)}, bf16[512,256]{1,0:T(8,128)(2,1)}, u32[]{:S(2)}, u32[]{:S(2)}) collective-permute-start(bf16[512,256]{1,0:T(8,128)(2,1)S(1)} %collective-permute-done.15.top_ref), channel_id=1, source_target_pairs={{0,2},{2,0},{4,6},{6,4},{8,10},{10,8},{12,14},{14,12},{1,3},{3,1},... | collective-permute-start | bytes 786440 | tf_op jit(solution)/shard_map/ppermute | solution.py:325
  68.6 0.0 collective-permute-done.17.low_ref
  68.6 0.0 collective-permute-start.18
  68.6 2.0 %project.3.rest_4_ = f32[1024,256]{1,0:T(8,128)S(1)} custom-call(s32[1]{0:T(128)} %bitcast.1.at_ref, bf16[8,256,256]{2,1,0:T(8,128)(2,1)} %all-to-all-done.w_hbm, bf16[512,256]{1,0:T(8,128)(2,1)S(1)} %get-tuple-element.34.rest_0_, bf16[512,256]{1,0:T(8,128)(2,1)S(1)} %collective-permute-done.8.rest_1_, bf16[512,256]{1,0:T(8,128)(2,1)S(1)} %get-tuple-element.33.rest_2_, ...), custom_call_target="tpu_custom_call" | custom-call | flops 536870912 | bytes 3670016 | tf_op jit(solution)/shard_map/project/pallas_call | solution.py:341
  70.5 0.0 collective-permute-done.5.rest_1_.rest_9_
  70.5 0.0 collective-permute-done.7.rest_3_.rest_11_
  70.5 1.7 %project.4 = (f32[1024,256]{1,0:T(8,128)S(1)}, bf16[2,256,256]{2,1,0:T(8,128)(2,1)S(1)}) custom-call(s32[1]{0:T(128)} %bitcast.1.at_ref, bf16[8,256,256]{2,1,0:T(8,128)(2,1)} %all-to-all-done.w_hbm, bf16[512,256]{1,0:T(8,128)(2,1)S(1)} %collective-permute-done.4.rest_0_.rest_8_, bf16[512,256]{1,0:T(8,128)(2,1)S(1)} %collective-permute-done.5.rest_1_.rest_9_, ...), custom_call_target="tpu_custom_call" | custom-call | flops 268435456 | bytes 2621440 | tf_op jit(solution)/shard_map/project/pallas_call | solution.py:341
  72.2 0.0 collective-permute-done.14.w_hbm
  72.2 2.3 %project.5 = (f32[1024,256]{1,0:T(8,128)S(1)}, bf16[2,256,256]{2,1,0:T(8,128)(2,1)S(1)}) custom-call(s32[1]{0:T(128)} %bitcast.1.at_ref, bf16[8,256,256]{2,1,0:T(8,128)(2,1)} %collective-permute-done.14.w_hbm, bf16[512,256]{1,0:T(8,128)(2,1)S(1)} %get-tuple-element.34.rest_0_, bf16[512,256]{1,0:T(8,128)(2,1)S(1)} %collective-permute-done.8.rest_1_, ...), custom_call_target="tpu_custom_call" | custom-call | flops 805306368 | bytes 4718592 | tf_op jit(solution)/shard_map/project/pallas_call | solution.py:341
  74.5 0.0 collective-permute-done.16.top_swap_ref
  74.6 0.0 collective-permute-done.18.low_swap_ref
  74.6 2.9 %finish.1 = bf16[1024,512]{1,0:T(8,128)(2,1)} custom-call(s32[1]{0:T(128)} %bitcast.dp_ref, bf16[2,256,256]{2,1,0:T(8,128)(2,1)S(1)} %get-tuple-element.35.mine_ref, bf16[2,256,256]{2,1,0:T(8,128)(2,1)S(1)} %get-tuple-element.36.twin_ref, f32[1024,256]{1,0:T(8,128)S(1)} %get-tuple-element.37.acc_mine_ref, f32[1024,256]{1,0:T(8,128)S(1)} %get-tuple-element.38.acc_twin_ref, ...), custom_call_target="tpu_custom_call" | custom-call | flops 536870912 | bytes 3670016 | tf_op jit(solution)/shard_map/finish/pallas_call | solution.py:357
Async XLA Ops:
  10.6 26.1 %all-to-all-start = ((bf16[8,256,256]{2,1,0:T(8,128)(2,1)}), bf16[8,256,256]{2,1,0:T(8,128)(2,1)}, u32[]{:S(2)}, u32[]{:S(2)}) async-start(bf16[8,256,256]{2,1,0:T(8,128)(2,1)} %get-tuple-element.22), calls=%async_computation | async-start | bytes 2097152 | tf_op jit(solution)/shard_map/all_to_all | solution.py:278
  17.9 5.1 %collective-permute-start = (bf16[2,136,128]{2,1,0:T(8,128)(2,1)S(1)}, bf16[2,136,128]{2,1,0:T(8,128)(2,1)S(1)}, u32[]{:S(2)}, u32[]{:S(2)}) collective-permute-start(bf16[2,136,128]{2,1,0:T(8,128)(2,1)S(1)} %get-tuple-element.24.total_ref), channel_id=1, source_target_pairs={{0,16},{16,0},{32,48},{48,32},{64,80},{80,64},{96,112},{112,96},{1... | collective-permute-start | bytes 208904 | tf_op jit(solution)/shard_map/ppermute | solution.py:292
  23.1 3.6 %collective-permute-start.1 = (bf16[2,136,128]{2,1,0:T(8,128)(2,1)S(1)}, bf16[2,136,128]{2,1,0:T(8,128)(2,1)S(1)}, u32[]{:S(2)}, u32[]{:S(2)}) collective-permute-start(bf16[2,136,128]{2,1,0:T(8,128)(2,1)S(1)} %get-tuple-element.25.total_ref), channel_id=1, source_target_pairs={{0,32},{16,48},{32,0},{48,16},{64,96},{80,112},{96,64},{112,80},{1... | collective-permute-start | bytes 208904 | tf_op jit(solution)/shard_map/ppermute | solution.py:292
  26.9 4.5 %collective-permute-start.2 = (bf16[2,136,128]{2,1,0:T(8,128)(2,1)S(1)}, bf16[2,136,128]{2,1,0:T(8,128)(2,1)S(1)}, u32[]{:S(2)}, u32[]{:S(2)}) collective-permute-start(bf16[2,136,128]{2,1,0:T(8,128)(2,1)S(1)} %get-tuple-element.27.total_ref), channel_id=1, source_target_pairs={{0,64},{16,80},{32,96},{48,112},{64,0},{80,16},{96,32},{112,48},{1... | collective-permute-start | bytes 208904 | tf_op jit(solution)/shard_map/ppermute | solution.py:292
  31.5 10.2 %collective-permute-start.3 = (bf16[2,136,128]{2,1,0:T(8,128)(2,1)S(1)}, bf16[2,136,128]{2,1,0:T(8,128)(2,1)S(1)}, u32[]{:S(2)}, u32[]{:S(2)}) collective-permute-start(bf16[2,136,128]{2,1,0:T(8,128)(2,1)S(1)} %get-tuple-element.29), channel_id=1, source_target_pairs={{0,224},{16,240},{32,192},{48,208},{64,160},{80,176},{96,128},{112... | collective-permute-start | bytes 208904 | tf_op jit(solution)/shard_map/ppermute | solution.py:292
  36.7 35.5 %collective-permute-start.14 = (bf16[8,256,256]{2,1,0:T(8,128)(2,1)}, bf16[8,256,256]{2,1,0:T(8,128)(2,1)}, u32[]{:S(2)}, u32[]{:S(2)}) collective-permute-start(bf16[8,256,256]{2,1,0:T(8,128)(2,1)} %all-to-all-done.w_hbm), channel_id=1, source_target_pairs={{0,1},{1,0},{2,3},{3,2},{4,5},{5,4},{6,7},{7,6},{8,9},{9,8},{10,11... | collective-permute-start | bytes 3145736 | tf_op jit(solution)/shard_map/ppermute | solution.py:279
  37.9 3.8 %copy-start = (f32[2]{0:T(128)S(1)}, f32[2]{0:T(128)}, u32[]{:S(2)}) copy-start(f32[2]{0:T(128)} %gate_ref.1) | copy-start | bytes 28
  42.9 6.5 %collective-permute-start.10 = (bf16[512,256]{1,0:T(8,128)(2,1)S(1)}, bf16[512,256]{1,0:T(8,128)(2,1)S(1)}, u32[]{:S(2)}, u32[]{:S(2)}) collective-permute-start(bf16[512,256]{1,0:T(8,128)(2,1)S(1)} %get-tuple-element.34.rest_0_), channel_id=1, source_target_pairs={{0,4},{2,6},{4,8},{6,10},{8,12},{10,14},{12,0},{14,2},{1,5},{3,7},... | collective-permute-start | bytes 786440 | tf_op jit(solution)/shard_map/ppermute | solution.py:322
  44.1 11.7 %collective-permute-start.12 = (bf16[512,256]{1,0:T(8,128)(2,1)S(1)}, bf16[512,256]{1,0:T(8,128)(2,1)S(1)}, u32[]{:S(2)}, u32[]{:S(2)}) collective-permute-start(bf16[512,256]{1,0:T(8,128)(2,1)S(1)} %get-tuple-element.33.rest_2_), channel_id=1, source_target_pairs={{0,12},{2,14},{4,0},{6,2},{8,4},{10,6},{12,8},{14,10},{1,13},{3,15... | collective-permute-start | bytes 786440 | tf_op jit(solution)/shard_map/ppermute | solution.py:322
  45.7 10.1 %collective-permute-start.4 = (bf16[512,256]{1,0:T(8,128)(2,1)S(1)}, bf16[512,256]{1,0:T(8,128)(2,1)S(1)}, u32[]{:S(2)}, u32[]{:S(2)}) collective-permute-start(bf16[512,256]{1,0:T(8,128)(2,1)S(1)} %get-tuple-element.33.rest_2_), channel_id=1, source_target_pairs={{0,4},{2,6},{4,8},{6,10},{8,12},{10,14},{12,0},{14,2},{1,5},{3,7},... | collective-permute-start | bytes 786440 | tf_op jit(solution)/shard_map/ppermute | solution.py:322
  45.7 12.9 %collective-permute-start.6 = (bf16[512,256]{1,0:T(8,128)(2,1)S(1)}, bf16[512,256]{1,0:T(8,128)(2,1)S(1)}, u32[]{:S(2)}, u32[]{:S(2)}) collective-permute-start(bf16[512,256]{1,0:T(8,128)(2,1)S(1)} %get-tuple-element.34.rest_0_), channel_id=1, source_target_pairs={{0,12},{2,14},{4,0},{6,2},{8,4},{10,6},{12,8},{14,10},{1,13},{3,15... | collective-permute-start | bytes 786440 | tf_op jit(solution)/shard_map/ppermute | solution.py:322
  49.4 9.1 %collective-permute-start.8 = (bf16[512,256]{1,0:T(8,128)(2,1)S(1)}, bf16[512,256]{1,0:T(8,128)(2,1)S(1)}, u32[]{:S(2)}, u32[]{:S(2)}) collective-permute-start(bf16[512,256]{1,0:T(8,128)(2,1)S(1)} %get-tuple-element.34.rest_0_), channel_id=1, source_target_pairs={{0,2},{2,0},{4,6},{6,4},{8,10},{10,8},{12,14},{14,12},{1,3},{3,1},... | collective-permute-start | bytes 786440 | tf_op jit(solution)/shard_map/ppermute | solution.py:325
  55.7 3.1 %collective-permute-start.9 = (bf16[512,256]{1,0:T(8,128)(2,1)S(1)}, bf16[512,256]{1,0:T(8,128)(2,1)S(1)}, u32[]{:S(2)}, u32[]{:S(2)}) collective-permute-start(bf16[512,256]{1,0:T(8,128)(2,1)S(1)} %get-tuple-element.33.rest_2_), channel_id=1, source_target_pairs={{0,2},{2,0},{4,6},{6,4},{8,10},{10,8},{12,14},{14,12},{1,3},{3,1},... | collective-permute-start | bytes 786440 | tf_op jit(solution)/shard_map/ppermute | solution.py:325
  55.7 5.6 %collective-permute-start.11 = (bf16[512,256]{1,0:T(8,128)(2,1)S(1)}, bf16[512,256]{1,0:T(8,128)(2,1)S(1)}, u32[]{:S(2)}, u32[]{:S(2)}) collective-permute-start(bf16[512,256]{1,0:T(8,128)(2,1)S(1)} %collective-permute-done.10.rest_4_), channel_id=1, source_target_pairs={{0,2},{2,0},{4,6},{6,4},{8,10},{10,8},{12,14},{14,12},{1,3},{3,1},... | collective-permute-start | bytes 786440 | tf_op jit(solution)/shard_map/ppermute | solution.py:325
  58.5 3.8 %collective-permute-start.13 = (bf16[512,256]{1,0:T(8,128)(2,1)S(1)}, bf16[512,256]{1,0:T(8,128)(2,1)S(1)}, u32[]{:S(2)}, u32[]{:S(2)}) collective-permute-start(bf16[512,256]{1,0:T(8,128)(2,1)S(1)} %collective-permute-done.12.rest_6_), channel_id=1, source_target_pairs={{0,2},{2,0},{4,6},{6,4},{8,10},{10,8},{12,14},{14,12},{1,3},{3,1},... | collective-permute-start | bytes 786440 | tf_op jit(solution)/shard_map/ppermute | solution.py:325
  58.5 8.7 %collective-permute-start.15 = (bf16[512,256]{1,0:T(8,128)(2,1)S(1)}, bf16[512,256]{1,0:T(8,128)(2,1)S(1)}, u32[]{:S(2)}, u32[]{:S(2)}) collective-permute-start(bf16[512,256]{1,0:T(8,128)(2,1)S(1)} %collective-permute-done.10.rest_4_), channel_id=1, source_target_pairs={{0,4},{2,6},{4,8},{6,10},{8,12},{10,14},{12,0},{14,2},{1,5},{3,7},... | collective-permute-start | bytes 786440 | tf_op jit(solution)/shard_map/ppermute | solution.py:322
  58.8 9.7 %collective-permute-start.17 = (bf16[512,256]{1,0:T(8,128)(2,1)S(1)}, bf16[512,256]{1,0:T(8,128)(2,1)}, u32[]{:S(2)}, u32[]{:S(2)}) collective-permute-start(bf16[512,256]{1,0:T(8,128)(2,1)S(1)} %collective-permute-done.12.rest_6_), channel_id=1, source_target_pairs={{0,12},{2,14},{4,0},{6,2},{8,4},{10,6},{12,8},{14,10},{1,13},{3,15... | collective-permute-start | bytes 786440 | tf_op jit(solution)/shard_map/ppermute | solution.py:322
  61.3 9.2 %collective-permute-start.5 = (bf16[512,256]{1,0:T(8,128)(2,1)S(1)}, bf16[512,256]{1,0:T(8,128)(2,1)S(1)}, u32[]{:S(2)}, u32[]{:S(2)}) collective-permute-start(bf16[512,256]{1,0:T(8,128)(2,1)S(1)} %collective-permute-done.4.rest_0_.rest_8_), channel_id=1, source_target_pairs={{0,2},{2,0},{4,6},{6,4},{8,10},{10,8},{12,14},{14,12},{1,3},{3,1},... | collective-permute-start | bytes 786440 | tf_op jit(solution)/shard_map/ppermute | solution.py:325
  62.3 8.2 %collective-permute-start.7 = (bf16[512,256]{1,0:T(8,128)(2,1)S(1)}, bf16[512,256]{1,0:T(8,128)(2,1)S(1)}, u32[]{:S(2)}, u32[]{:S(2)}) collective-permute-start(bf16[512,256]{1,0:T(8,128)(2,1)S(1)} %collective-permute-done.6.rest_2_.rest_10_), channel_id=1, source_target_pairs={{0,2},{2,0},{4,6},{6,4},{8,10},{10,8},{12,14},{14,12},{1,3},{3,1},... | collective-permute-start | bytes 786440 | tf_op jit(solution)/shard_map/ppermute | solution.py:325
  67.3 7.3 %collective-permute-start.16 = (bf16[512,256]{1,0:T(8,128)(2,1)S(1)}, bf16[512,256]{1,0:T(8,128)(2,1)}, u32[]{:S(2)}, u32[]{:S(2)}) collective-permute-start(bf16[512,256]{1,0:T(8,128)(2,1)S(1)} %collective-permute-done.15.top_ref), channel_id=1, source_target_pairs={{0,2},{2,0},{4,6},{6,4},{8,10},{10,8},{12,14},{14,12},{1,3},{3,1},... | collective-permute-start | bytes 786440 | tf_op jit(solution)/shard_map/ppermute | solution.py:325
  68.6 6.0 %collective-permute-start.18 = (bf16[512,256]{1,0:T(8,128)(2,1)}, bf16[512,256]{1,0:T(8,128)(2,1)}, u32[]{:S(2)}, u32[]{:S(2)}) collective-permute-start(bf16[512,256]{1,0:T(8,128)(2,1)} %collective-permute-done.17.low_ref), channel_id=1, source_target_pairs={{0,2},{2,0},{4,6},{6,4},{8,10},{10,8},{12,14},{14,12},{1,3},{3,1},... | collective-permute-start | bytes 786440 | tf_op jit(solution)/shard_map/ppermute | solution.py:325

commit v2 on v1

--- a/solution.py
+++ b/solution.py
@@ -59,11 +59,12 @@
         packs.append(pltpu.make_async_copy(wo_hbm.at[:, share], o_ref.at[j], in_sem.at[j]))
     for copy in packs:
         copy.start()
-    part = toks // 8
-    for i, (lo, hi) in enumerate(cuts):
+    moves = [pltpu.make_async_copy(o_ref.at[j], o_hbm.at[j], out_sem.at[j]) for j in range(pieces)]
+    for i, (lo, hi) in enumerate(cuts[:-1]):
         at = slice(lo, hi)
         for copy in copies[i]:
             copy.wait()
+        part = toks // 8
         for r in range(8):
             rows = slice(r * part, (r + 1) * part)
             piece = dot(x_ref[rows, at], w_ref[at, :])
@@ -71,26 +72,35 @@
                 acc_ref[rows, :] = piece
             else:
                 acc_ref[rows, :] += piece
-    moves = [pltpu.make_async_copy(o_ref.at[j], o_hbm.at[j], out_sem.at[j]) for j in range(pieces)]
-    for pack, move in zip(packs, moves):
-        pack.wait()
-        move.start()
-    keys = acc_ref[:, :cols].astype(BF)
-    vals = acc_ref[:, cols : 2 * cols].astype(BF)
-    queries = acc_ref[:, 2 * cols :].astype(BF)
-    k_ref[...] = keys
-    v_ref[...] = vals
-    q_ref[...] = queries
-    feat = features(keys.astype(F32))
-    norm = jnp.sum(feat, axis=0, keepdims=True)
-    feat_bf = feat.astype(BF)
+    at = slice(*cuts[-1])
+    for copy in copies[-1]:
+        copy.wait()
+    part = toks // 4
+    norm, memory = None, [None] * heads
+    for r in range(4):
+        rows = slice(r * part, (r + 1) * part)
+        whole = (acc_ref[rows, :] + dot(x_ref[rows, at], w_ref[at, :])).astype(BF)
+        keys, vals = whole[:, :cols], whole[:, cols : 2 * cols]
+        k_ref[rows, :] = keys
+        v_ref[rows, :] = vals
+        q_ref[rows, :] = whole[:, 2 * cols :]
+        feat = features(keys.astype(F32))
+        term = jnp.sum(feat, axis=0, keepdims=True)
+        norm = term if norm is None else norm + term
+        feat_bf = feat.astype(BF)
+        for h in range(heads):
+            of = slice(h * DH, (h + 1) * DH)
+            term = dot(vals[:, of], feat_bf[:, of], ((0,), (0,)))
+            memory[h] = term if memory[h] is None else memory[h] + term
+        if r == 2:
+            for pack, move in zip(packs, moves):
+                pack.wait()
+                move.start()
     row = lax.broadcasted_iota(jnp.int32, (8, DH), 0)
     keep = 1.0 - resets_ref[0].astype(F32)
     for h in range(heads):
-        at = slice(h * DH, (h + 1) * DH)
-        memory = dot(vals[:, at], feat_bf[:, at], ((0,), (0,)))
-        tail = jnp.where(row == 0, norm[:, at], keep)
-        s_ref[h] = jnp.concatenate([memory, tail], axis=0).astype(BF)
+        tail = jnp.where(row == 0, norm[:, h * DH : (h + 1) * DH], keep)
+        s_ref[h] = jnp.concatenate([memory[h], tail], axis=0).astype(BF)
     for move in moves:
         move.wait()
 
@@ -115,17 +125,19 @@
         new_ref[h] = jnp.where(flag, got * total, low_first).astype(BF)
 
 
-def attend_kernel(q_ref, k_ref, v_ref, o_ref, wide_ref):
+def attend_kernel(head, gate_ref, q_ref, k_ref, v_ref, o_ref, f_ref, wide_ref):
     toks = q_ref.shape[0]
     tile = 256
     scale = math.log2(math.e) / math.sqrt(DH)
     row = lax.broadcasted_iota(jnp.int32, (tile, tile), 0)
     col = lax.broadcasted_iota(jnp.int32, (tile, tile), 1)
+    other = 1.0 / (1.0 + jnp.exp(jnp.full((1, DH), gate_ref[head], F32)))
     wide_ref[:, :DH] = v_ref[...]
     wide_ref[:, DH:] = jnp.ones((toks, DH), BF)
     for i in range(toks // tile):
         at = slice(i * tile, (i + 1) * tile)
         q = q_ref[at, :]
+        f_ref[at, :] = features(q.astype(F32)).astype(BF)
         diag = jnp.where(row >= col, dot(q, k_ref[at, :], ((1,), (1,))), -1e30)
         peak = jnp.max(diag, axis=-1, keepdims=True)
         if i:
@@ -134,21 +146,22 @@
         out = dot(jnp.exp2((diag - peak) * scale).astype(BF), wide_ref[at, :])
         if i:
             out = out + dot(jnp.exp2((past - peak) * scale).astype(BF), wide_ref[: i * tile, :])
-        o_ref[at, :] = out[:, :DH] / out[:, DH:]
-
-
-def read_kernel(bit, seg_ref, resets_ref, gate_ref, q_ref, got_ref, before_ref, *rest):
+        o_ref[at, :] = (out[:, :DH] * (other / out[:, DH:])).astype(BF)
+
+
+def read_kernel(bit, seg_ref, resets_ref, gate_ref, got_ref, before_ref, *rest):
     local_refs, top_ref, low_ref = rest[:-2], rest[-2], rest[-1]
+    heads = len(local_refs) // 2
     half = top_ref.shape[0]
     flag = lax.broadcasted_iota(jnp.int32, (ROWS, DH), 0) > DH
     keep = 1.0 - resets_ref[0].astype(F32)
-    for h, l_ref in enumerate(local_refs):
+    for h, (l_ref, f_ref) in enumerate(zip(local_refs[:heads], local_refs[heads:])):
         at = slice(h * DH, (h + 1) * DH)
         state = (keep * joined(bit, seg_ref[0], got_ref[h].astype(F32), before_ref[h], flag)).astype(BF)
         gate = 1.0 / (1.0 + jnp.exp(-jnp.full((1, DH), gate_ref[h], F32)))
-        got = dot(features(q_ref[:, at].astype(F32)).astype(BF), state, ((1,), (1,)))
+        got = dot(f_ref[...], state, ((1,), (1,)))
         part = gate[:, :1] / jnp.maximum(got[:, DH : DH + 1], 1.0)
-        mixed = (got[:, :DH] * part + (1.0 - gate) * l_ref[...]).astype(BF)
+        mixed = (got[:, :DH] * part + l_ref[...].astype(F32)).astype(BF)
         top_ref[:, at] = mixed[:half]
         low_ref[:, at] = mixed[half:]
 
@@ -198,18 +211,28 @@
         copy.wait()
 
 
-def finish_kernel(dp_ref, mine_ref, twin_ref, acc_mine_ref, acc_twin_ref, top_ref, top_swap_ref, low_ref, low_swap_ref, o_ref):
-    half = o_ref.shape[0]
-    slim = mine_ref.shape[2]
-    for side, parts in enumerate(((top_ref, top_swap_ref), (low_ref, low_swap_ref))):
+def later_kernel(plan, at_ref, w_hbm, far_ref, acc_ref, *rest):
+    values, (mine_ref, o_ref, last_ref, w_ref, sem, last_sem) = rest[: len(plan)], rest[len(plan) :]
+    half = values[0].shape[0]
+    last = pltpu.make_async_copy(w_hbm.at[source(at_ref, 4, True, w_hbm.shape[0])], last_ref, last_sem)
+    last.start()
+    project_kernel(plan, False, False, at_ref, w_hbm, *values, o_ref, w_ref, sem)
+    for side, value in enumerate(values[-2:]):
+        rows = slice(side * half, (side + 1) * half)
+        mine_ref[rows, :] = acc_ref[rows, :] + dot(value[...], far_ref[0])
+    last.wait()
+
+
+def finish_kernel(dp_ref, mine_ref, twin_ref, acc_mine_ref, acc_twin_ref, top_ref, low_ref, o_ref):
+    half, slim = o_ref.shape[0], twin_ref.shape[1]
+    for side, part in enumerate((top_ref, low_ref)):
 
         @pl.when(pl.program_id(0) == side)
         def _():
             rows = slice(side * half, (side + 1) * half)
-            for index, w_ref, acc_ref in ((dp_ref[0], mine_ref, acc_mine_ref), (1 - dp_ref[0], twin_ref, acc_twin_ref)):
-                total = acc_ref[rows, :]
-                for i, part in enumerate(parts):
-                    total = total + dot(part[...], w_ref[i])
+            mine = acc_mine_ref[rows, :] + dot(part[...], mine_ref[1])
+            theirs = acc_twin_ref[rows, :] + dot(part[...], twin_ref[...])
+            for index, total in ((dp_ref[0], mine), (1 - dp_ref[0], theirs)):
                 o_ref[:, pl.ds(pl.multiple_of(index * slim, slim), slim)] = total.astype(BF)
 
 
@@ -262,25 +285,27 @@
     def attend(h):
         spec = pl.BlockSpec((toks, DH), lambda i: (0, h))
         return call(
-            attend_kernel,
-            jax.ShapeDtypeStruct((toks, DH), F32),
+            functools.partial(attend_kernel, h),
+            (jax.ShapeDtypeStruct((toks, DH), BF),) * 2,
             10,
             4 * toks * toks * DH,
             10 * toks * DH,
             toks * toks,
             grid=(1,),
-            in_specs=[spec] * 3,
-            out_specs=pl.BlockSpec((toks, DH), lambda i: (0, 0)),
+            in_specs=[smem] + [spec] * 3,
+            out_specs=(pl.BlockSpec((toks, DH), lambda i: (0, 0)),) * 2,
             scratch_shapes=[pltpu.VMEM((toks, 2 * DH), BF)],
             name="attend",
-        )(queries, keys, vals)
+        )(mem_gate, queries, keys, vals)
 
     w_mine = stay(lax.all_to_all(stay(w_cut), "tp", 0, 0, tiled=True))
     w_twin = stay(lax.ppermute(w_mine, "dp", [(i, n_dp - 1 - i) for i in range(n_dp)]))
 
-    local = []
+    local, q_feat = [], []
     for h in range(heads):
-        local.append(attend(h))
+        got = attend(h)
+        local.append(got[0])
+        q_feat.append(got[1])
 
     total, before, bit, step = state, [], 1, 0
     while True:
@@ -313,10 +338,10 @@
         10,
         4 * toks * DH * cols,
         8 * toks * cols,
-        in_specs=[smem] * 3 + [whole] * (3 + heads),
+        in_specs=[smem] * 3 + [whole] * (2 + 2 * heads),
         out_specs=(whole, whole),
         name="read",
-    )(spot, resets, mem_gate, queries, got, before[0], *local)
+    )(spot, resets, mem_gate, got, before[0], *local, *q_feat)
 
     def along(value, by):
         return lax.ppermute(value, "tp", [(i, (i + 2 * by) % n_tp) for i in range(n_tp)])
@@ -353,18 +378,37 @@
 
     acc_mine = project(early, w_mine, None, False)
     acc_mine, far_mine = project(second, w_mine, acc_mine, True)
-    acc_twin, far_twin = project(early + second, w_twin, None, True)
+    ends = [(far_top, (0, 4, False)), (far_low, (1, 4, False))]
+    far_swaps = (swap(far_top), swap(far_low))
+    values, plan = zip(*(early + second + ends))
+    places = len({where[1:] for where in plan})
+    block = jax.ShapeDtypeStruct((toks, slim), F32)
+    acc_mine, acc_twin, last_twin = call(
+        functools.partial(later_kernel, plan),
+        (block, block, jax.ShapeDtypeStruct((cols, slim), BF)),
+        16,
+        2 * (len(values) + 2) * half * cols * slim,
+        2 * len(values) * half * cols + 10 * toks * slim,
+        in_specs=[smem, remote] + [whole] * (2 + len(values)),
+        out_specs=(whole,) * 3,
+        scratch_shapes=[
+            pltpu.VMEM((places, cols, slim), BF),
+            pltpu.SemaphoreType.DMA((places,)),
+            pltpu.SemaphoreType.DMA(()),
+        ],
+        name="later",
+    )(place, w_twin, far_mine, acc_mine, *values)
     return call(
         finish_kernel,
         jax.ShapeDtypeStruct((toks, out_cols), BF),
         10,
-        4 * toks * cols * out_cols,
+        2 * toks * cols * out_cols,
         2 * toks * cols + 6 * toks * out_cols,
         grid=(2,),
-        in_specs=[smem] + [whole] * 8,
+        in_specs=[smem] + [whole] * 6,
         out_specs=pl.BlockSpec((half, out_cols), lambda i: (i, 0)),
         name="finish",
-    )(twin, far_mine, far_twin, acc_mine, acc_twin, far_top, swap(far_top), far_low, swap(far_low))
+    )(twin, far_mine, last_twin, acc_mine, acc_twin, *far_swaps)
 
 
 def solution(mesh):

time: 77.7 us -> 80.3 us (1.033)
  starting transfers between devices: 37.5 us -> 44.1 us
  waiting for transfers between devices: 15.3 us -> 9.55 us
  Pallas kernels: 23.9 us -> 25.6 us
    ppermute x8, starting transfers between devices: 11.5 us -> 18.1 us  [swap(): return lax.ppermute(value, 'tp', [(i, i ^ 1) for i in range(n_tp)])]
    ppermute x6, waiting for transfers between devices: 5.97 us -> 0.29 us  [along(): lax.ppermute(value, 'tp', [(i, (i + 2 * by) % n_tp) for i in range(n_tp)])]
    pallas_call x3 -> x4, Pallas kernels: 6.62 us -> 10.7 us  [the longest x2 4.64 us: attend(): call(functools.partial(attend_kernel, h), (jax.ShapeDtypeStruct((toks, DH...]
    pallas_call x3 -> x2, Pallas kernels: 5.93 us -> 3.63 us  [project(): call(functools.partial(project_kernel, plan, acc is not None, reach), out...]
  transfers between devices with their start and end apart: 20 -> 20, of which waited for: 5 -> 4; matrix products, arithmetic and copies ran while one was open for 0% -> 0% of each run, Pallas kernels for 14% -> 16%
where the time goes in v2:
time: 80.3 us; the launch traced here: 80.1 us
  starting transfers between devices  44.1 us (55%)
  Pallas kernels  25.6 us (32%)
  waiting for transfers between devices  9.55 us (12%)
    ppermute x8, starting transfers between devices, swap(): return lax.ppermute(value, 'tp', [(i, i ^ 1) for i in range(n_tp)])  18.1 us
    pallas_call x1, Pallas kernels, on_device(): call(functools.partial(qkv_kernel, cuts), (flat, flat, flat, payload, jax...  9.97 us
    ppermute x4, starting transfers between devices, on_device(): got = lax.ppermute(total, 'seg', pairs)  9.35 us
    ppermute x4, waiting for transfers between devices, on_device(): got = lax.ppermute(total, 'seg', pairs)  9.23 us
    ppermute x6, starting transfers between devices, along(): lax.ppermute(value, 'tp', [(i, (i + 2 * by) % n_tp) for i in range(n_tp)])  8.11 us
    all_to_all x1, starting transfers between devices, on_device(): w_mine = stay(lax.all_to_all(stay(w_cut), 'tp', 0, 0, tiled=True))  7.33 us
    pallas_call x2, Pallas kernels, attend(): call(functools.partial(attend_kernel, h), (jax.ShapeDtypeStruct((toks, DH...  4.64 us
    pallas_call x2, Pallas kernels, project(): call(functools.partial(project_kernel, plan, acc is not None, reach), out...  3.63 us
  transfers between devices with their start and end apart: 20, of which 4 were waited for; matrix products, arithmetic and copies ran while one was open for 0% of the time, Pallas kernels for 16%

profile of v2, /device:TPU:1, one launch (start us, length us, event | category | flops | bytes accessed | tf_op | source)
XLA Modules:
  0.0 80.1 jit_solution(13792437927302831764)
XLA Ops:
  0.7 10.0 %qkv.1 = (bf16[1024,256]{1,0:T(8,128)(2,1)S(1)}, bf16[1024,256]{1,0:T(8,128)(2,1)S(1)}, bf16[1024,256]{1,0:T(8,128)(2,1)S(1)}, bf16[2,136,128]{2,1,0:T(8,128)(2,1)S(1)}, bf16[8,256,256]{2,1,0:T(8,128)(2,1)}) custom-call(s32[1]{0:T(128)} %bitcast.dp_ref, s32[1]{0:T(128)S(6)} %copy.8.resets_ref, bf16[1024,4096]{1,0:T(8,128)(2,1)} %x_hbm.1, ...), custom_call_target="tpu_custom_call" | custom-call | flops 6442450944 | bytes 16777216 | tf_op jit(solution)/shard_map/qkv/pallas_call | solution.py:265
  10.6 0.0 copy-start
  10.6 7.3 %all-to-all-start = ((bf16[8,256,256]{2,1,0:T(8,128)(2,1)}), bf16[8,256,256]{2,1,0:T(8,128)(2,1)}, u32[]{:S(2)}, u32[]{:S(2)}) async-start(bf16[8,256,256]{2,1,0:T(8,128)(2,1)} %get-tuple-element.27), calls=%async_computation | async-start | bytes 2097152 | tf_op jit(solution)/shard_map/all_to_all | solution.py:301
  18.0 1.4 %collective-permute-start = (bf16[2,136,128]{2,1,0:T(8,128)(2,1)S(1)}, bf16[2,136,128]{2,1,0:T(8,128)(2,1)S(1)}, u32[]{:S(2)}, u32[]{:S(2)}) collective-permute-start(bf16[2,136,128]{2,1,0:T(8,128)(2,1)S(1)} %get-tuple-element.28.total_ref), channel_id=1, source_target_pairs={{0,16},{16,0},{32,48},{48,32},{64,80},{80,64},{96,112},{112,96},{1... | collective-permute-start | bytes 208904 | tf_op jit(solution)/shard_map/ppermute | solution.py:317
  19.4 3.7 %collective-permute-done.got_ref = bf16[2,136,128]{2,1,0:T(8,128)(2,1)S(1)} collective-permute-done((bf16[2,136,128]{2,1,0:T(8,128)(2,1)S(1)}, bf16[2,136,128]{2,1,0:T(8,128)(2,1)S(1)}, u32[]{:S(2)}, u32[]{:S(2)}) %collective-permute-start) | collective-permute-done | bytes 69664 | tf_op jit(solution)/shard_map/ppermute | solution.py:317
  23.1 0.1 merge.3
  23.2 0.6 collective-permute-start.1
  23.8 3.1 %collective-permute-done.1.got_ref = bf16[2,136,128]{2,1,0:T(8,128)(2,1)S(1)} collective-permute-done((bf16[2,136,128]{2,1,0:T(8,128)(2,1)S(1)}, bf16[2,136,128]{2,1,0:T(8,128)(2,1)S(1)}, u32[]{:S(2)}, u32[]{:S(2)}) %collective-permute-start.1) | collective-permute-done | bytes 69664 | tf_op jit(solution)/shard_map/ppermute | solution.py:317
  26.8 0.1 merge.4
  26.9 2.1 %collective-permute-start.2 = (bf16[2,136,128]{2,1,0:T(8,128)(2,1)S(1)}, bf16[2,136,128]{2,1,0:T(8,128)(2,1)S(1)}, u32[]{:S(2)}, u32[]{:S(2)}) collective-permute-start(bf16[2,136,128]{2,1,0:T(8,128)(2,1)S(1)} %get-tuple-element.31.total_ref), channel_id=1, source_target_pairs={{0,64},{16,80},{32,96},{48,112},{64,0},{80,16},{96,32},{112,48},{1... | collective-permute-start | bytes 208904 | tf_op jit(solution)/shard_map/ppermute | solution.py:317
  29.0 2.4 %collective-permute-done.2.got_ref = bf16[2,136,128]{2,1,0:T(8,128)(2,1)S(1)} collective-permute-done((bf16[2,136,128]{2,1,0:T(8,128)(2,1)S(1)}, bf16[2,136,128]{2,1,0:T(8,128)(2,1)S(1)}, u32[]{:S(2)}, u32[]{:S(2)}) %collective-permute-start.2) | collective-permute-done | bytes 69664 | tf_op jit(solution)/shard_map/ppermute | solution.py:317
  31.4 0.1 merge.5
  31.5 5.3 %collective-permute-start.3 = (bf16[2,136,128]{2,1,0:T(8,128)(2,1)S(1)}, bf16[2,136,128]{2,1,0:T(8,128)(2,1)S(1)}, u32[]{:S(2)}, u32[]{:S(2)}) collective-permute-start(bf16[2,136,128]{2,1,0:T(8,128)(2,1)S(1)} %get-tuple-element.33), channel_id=1, source_target_pairs={{0,224},{16,240},{32,192},{48,208},{64,160},{80,176},{96,128},{112... | collective-permute-start | bytes 208904 | tf_op jit(solution)/shard_map/ppermute | solution.py:317
  36.8 0.0 all-to-all-done.w_hbm
  36.8 1.2 %collective-permute-start.14 = (bf16[8,256,256]{2,1,0:T(8,128)(2,1)}, bf16[8,256,256]{2,1,0:T(8,128)(2,1)}, u32[]{:S(2)}, u32[]{:S(2)}) collective-permute-start(bf16[8,256,256]{2,1,0:T(8,128)(2,1)} %all-to-all-done.w_hbm), channel_id=1, source_target_pairs={{0,1},{1,0},{2,3},{3,2},{4,5},{5,4},{6,7},{7,6},{8,9},{9,8},{10,11... | collective-permute-start | bytes 3145736 | tf_op jit(solution)/shard_map/ppermute | solution.py:302
  38.0 0.0 copy-done
  38.0 2.3 %attend.3 = (bf16[1024,128]{1,0:T(8,128)(2,1)S(1)}, bf16[1024,128]{1,0:T(8,128)(2,1)S(1)}) custom-call(f32[2]{0:T(128)S(1)} %copy-done, bf16[1024,256]{1,0:T(8,128)(2,1)S(1)} %get-tuple-element.35.q_ref, bf16[1024,256]{1,0:T(8,128)(2,1)S(1)} %get-tuple-element.36.k_ref, bf16[1024,256]{1,0:T(8,128)(2,1)S(1)} %get-tuple-element.37.v_ref), custom_call_target="tpu_custom_call" | custom-call | flops 536870912 | bytes 1310720 | tf_op jit(solution)/shard_map/attend/pallas_call | solution.py:287
  40.3 2.3 %attend.2 = (bf16[1024,128]{1,0:T(8,128)(2,1)S(1)}, bf16[1024,128]{1,0:T(8,128)(2,1)S(1)}) custom-call(f32[2]{0:T(128)S(1)} %copy-done, bf16[1024,256]{1,0:T(8,128)(2,1)S(1)} %get-tuple-element.35.q_ref, bf16[1024,256]{1,0:T(8,128)(2,1)S(1)} %get-tuple-element.36.k_ref, bf16[1024,256]{1,0:T(8,128)(2,1)S(1)} %get-tuple-element.37.v_ref), custom_call_target="tpu_custom_call" | custom-call | flops 536870912 | bytes 1310720 | tf_op jit(solution)/shard_map/attend/pallas_call | solution.py:287
  42.7 0.0 collective-permute-done.3.got_ref
  42.7 1.1 %read.1 = (bf16[512,256]{1,0:T(8,128)(2,1)S(1)}, bf16[512,256]{1,0:T(8,128)(2,1)S(1)}) custom-call(s32[1]{0:T(128)} %bitcast.2.seg_ref, s32[1]{0:T(128)S(6)} %copy.8.resets_ref, f32[2]{0:T(128)S(1)} %copy-done, bf16[2,136,128]{2,1,0:T(8,128)(2,1)S(1)} %collective-permute-done.3.got_ref, f32[2,136,128]{2,1,0:T(8,128)S(1)} %get-tuple-element.34.before_ref, ...), custom_call_target="tpu_custom_call" | custom-call | flops 134217728 | bytes 2097152 | tf_op jit(solution)/shard_map/read/pallas_call | solution.py:335
  43.7 1.2 %collective-permute-start.10 = (bf16[512,256]{1,0:T(8,128)(2,1)S(1)}, bf16[512,256]{1,0:T(8,128)(2,1)S(1)}, u32[]{:S(2)}, u32[]{:S(2)}) collective-permute-start(bf16[512,256]{1,0:T(8,128)(2,1)S(1)} %get-tuple-element.43.rest_0_), channel_id=1, source_target_pairs={{0,4},{2,6},{4,8},{6,10},{8,12},{10,14},{12,0},{14,2},{1,5},{3,7},... | collective-permute-start | bytes 786440 | tf_op jit(solution)/shard_map/ppermute | solution.py:347
  44.9 1.6 %collective-permute-start.12 = (bf16[512,256]{1,0:T(8,128)(2,1)S(1)}, bf16[512,256]{1,0:T(8,128)(2,1)S(1)}, u32[]{:S(2)}, u32[]{:S(2)}) collective-permute-start(bf16[512,256]{1,0:T(8,128)(2,1)S(1)} %get-tuple-element.42.rest_2_), channel_id=1, source_target_pairs={{0,12},{2,14},{4,0},{6,2},{8,4},{10,6},{12,8},{14,10},{1,13},{3,15... | collective-permute-start | bytes 786440 | tf_op jit(solution)/shard_map/ppermute | solution.py:347
  46.5 3.5 %collective-permute-start.8 = (bf16[512,256]{1,0:T(8,128)(2,1)S(1)}, bf16[512,256]{1,0:T(8,128)(2,1)S(1)}, u32[]{:S(2)}, u32[]{:S(2)}) collective-permute-start(bf16[512,256]{1,0:T(8,128)(2,1)S(1)} %get-tuple-element.43.rest_0_), channel_id=1, source_target_pairs={{0,2},{2,0},{4,6},{6,4},{8,10},{10,8},{12,14},{14,12},{1,3},{3,1},... | collective-permute-start | bytes 786440 | tf_op jit(solution)/shard_map/ppermute | solution.py:350
  50.0 0.0 collective-permute-start.9
  50.0 0.3 collective-permute-done.10.rest_4_
  50.3 0.3 collective-permute-start.4
  50.5 0.0 collective-permute-done.12.rest_6_
  50.5 2.4 %collective-permute-start.6 = (bf16[512,256]{1,0:T(8,128)(2,1)S(1)}, bf16[512,256]{1,0:T(8,128)(2,1)S(1)}, u32[]{:S(2)}, u32[]{:S(2)}) collective-permute-start(bf16[512,256]{1,0:T(8,128)(2,1)S(1)} %get-tuple-element.43.rest_0_), channel_id=1, source_target_pairs={{0,12},{2,14},{4,0},{6,2},{8,4},{10,6},{12,8},{14,10},{1,13},{3,15... | collective-permute-start | bytes 786440 | tf_op jit(solution)/shard_map/ppermute | solution.py:347
  52.9 0.0 collective-permute-done.8.rest_1_
  52.9 4.6 %collective-permute-start.11 = (bf16[512,256]{1,0:T(8,128)(2,1)S(1)}, bf16[512,256]{1,0:T(8,128)(2,1)S(1)}, u32[]{:S(2)}, u32[]{:S(2)}) collective-permute-start(bf16[512,256]{1,0:T(8,128)(2,1)S(1)} %collective-permute-done.10.rest_4_), channel_id=1, source_target_pairs={{0,2},{2,0},{4,6},{6,4},{8,10},{10,8},{12,14},{14,12},{1,3},{3,1},... | collective-permute-start | bytes 786440 | tf_op jit(solution)/shard_map/ppermute | solution.py:350
  57.6 0.0 collective-permute-done.9.rest_3_
  57.6 0.1 collective-permute-start.13
  57.7 0.0 collective-permute-done.4.rest_0_.rest_8_
  57.7 0.2 collective-permute-start.15
  57.9 0.0 collective-permute-done.6.rest_2_.rest_10_
  57.9 2.5 %collective-permute-start.16 = (bf16[512,256]{1,0:T(8,128)(2,1)S(1)}, bf16[512,256]{1,0:T(8,128)(2,1)}, u32[]{:S(2)}, u32[]{:S(2)}) collective-permute-start(bf16[512,256]{1,0:T(8,128)(2,1)S(1)} %collective-permute-done.12.rest_6_), channel_id=1, source_target_pairs={{0,12},{2,14},{4,0},{6,2},{8,4},{10,6},{12,8},{14,10},{1,13},{3,15... | collective-permute-start | bytes 786440 | tf_op jit(solution)/shard_map/ppermute | solution.py:347
  60.4 0.0 collective-permute-done.11.rest_5_
  60.4 5.0 %collective-permute-start.5 = (bf16[512,256]{1,0:T(8,128)(2,1)S(1)}, bf16[512,256]{1,0:T(8,128)(2,1)S(1)}, u32[]{:S(2)}, u32[]{:S(2)}) collective-permute-start(bf16[512,256]{1,0:T(8,128)(2,1)S(1)} %collective-permute-done.4.rest_0_.rest_8_), channel_id=1, source_target_pairs={{0,2},{2,0},{4,6},{6,4},{8,10},{10,8},{12,14},{14,12},{1,3},{3,1},... | collective-permute-start | bytes 786440 | tf_op jit(solution)/shard_map/ppermute | solution.py:350
  65.4 0.0 collective-permute-done.13.rest_7_
  65.4 0.1 collective-permute-start.7
  65.5 0.0 collective-permute-done.15.rest_12_
  65.5 4.0 %collective-permute-start.17 = (bf16[512,256]{1,0:T(8,128)(2,1)S(1)}, bf16[512,256]{1,0:T(8,128)(2,1)}, u32[]{:S(2)}, u32[]{:S(2)}) collective-permute-start(bf16[512,256]{1,0:T(8,128)(2,1)S(1)} %collective-permute-done.15.rest_12_), channel_id=1, source_target_pairs={{0,2},{2,0},{4,6},{6,4},{8,10},{10,8},{12,14},{14,12},{1,3},{3,1},... | collective-permute-start | bytes 786440 | tf_op jit(solution)/shard_map/ppermute | solution.py:350
  69.5 0.0 collective-permute-done.16.rest_13_
  69.5 0.8 %collective-permute-start.18 = (bf16[512,256]{1,0:T(8,128)(2,1)}, bf16[512,256]{1,0:T(8,128)(2,1)}, u32[]{:S(2)}, u32[]{:S(2)}) collective-permute-start(bf16[512,256]{1,0:T(8,128)(2,1)} %collective-permute-done.16.rest_13_), channel_id=1, source_target_pairs={{0,2},{2,0},{4,6},{6,4},{8,10},{10,8},{12,14},{14,12},{1,3},{3,1},... | collective-permute-start | bytes 786440 | tf_op jit(solution)/shard_map/ppermute | solution.py:350
  70.3 2.0 %project.2.rest_4_ = f32[1024,256]{1,0:T(8,128)S(1)} custom-call(s32[1]{0:T(128)} %bitcast.1.at_ref, bf16[8,256,256]{2,1,0:T(8,128)(2,1)} %all-to-all-done.w_hbm, bf16[512,256]{1,0:T(8,128)(2,1)S(1)} %get-tuple-element.43.rest_0_, bf16[512,256]{1,0:T(8,128)(2,1)S(1)} %collective-permute-done.8.rest_1_, bf16[512,256]{1,0:T(8,128)(2,1)S(1)} %get-tuple-element.42.rest_2_, ...), custom_call_target="tpu_custom_call" | custom-call | flops 536870912 | bytes 3670016 | tf_op jit(solution)/shard_map/project/pallas_call | solution.py:366
  72.3 0.0 collective-permute-done.5.rest_1_.rest_9_
  72.3 0.0 collective-permute-done.7.rest_3_.rest_11_
  72.3 1.7 %project.3 = (f32[1024,256]{1,0:T(8,128)S(1)}, bf16[2,256,256]{2,1,0:T(8,128)(2,1)S(1)}) custom-call(s32[1]{0:T(128)} %bitcast.1.at_ref, bf16[8,256,256]{2,1,0:T(8,128)(2,1)} %all-to-all-done.w_hbm, bf16[512,256]{1,0:T(8,128)(2,1)S(1)} %collective-permute-done.4.rest_0_.rest_8_, bf16[512,256]{1,0:T(8,128)(2,1)S(1)} %collective-permute-done.5.rest_1_.rest_9_, ...), custom_call_target="tpu_custom_call" | custom-call | flops 268435456 | bytes 2621440 | tf_op jit(solution)/shard_map/project/pallas_call | solution.py:366
  74.0 0.0 collective-permute-done.14.w_hbm
  74.0 3.6 %later.1 = (f32[1024,256]{1,0:T(8,128)S(1)}, f32[1024,256]{1,0:T(8,128)S(1)}, bf16[256,256]{1,0:T(8,128)(2,1)S(1)}) custom-call(s32[1]{0:T(128)} %bitcast.1.at_ref, bf16[8,256,256]{2,1,0:T(8,128)(2,1)} %collective-permute-done.14.w_hbm, bf16[2,256,256]{2,1,0:T(8,128)(2,1)S(1)} %get-tuple-element.44.far_ref.mine_ref, ...), custom_call_target="tpu_custom_call" | custom-call | flops 1073741824 | bytes 6291456 | tf_op jit(solution)/shard_map/later/pallas_call | solution.py:386
  77.5 0.0 collective-permute-done.17.top_ref
  77.6 0.0 collective-permute-done.18.low_ref
  77.6 2.5 %finish.1 = bf16[1024,512]{1,0:T(8,128)(2,1)} custom-call(s32[1]{0:T(128)} %bitcast.dp_ref, bf16[2,256,256]{2,1,0:T(8,128)(2,1)S(1)} %get-tuple-element.44.far_ref.mine_ref, bf16[256,256]{1,0:T(8,128)(2,1)S(1)} %get-tuple-element.46.twin_ref, f32[1024,256]{1,0:T(8,128)S(1)} %get-tuple-element.47.acc_mine_ref, ...), custom_call_target="tpu_custom_call" | custom-call | flops 268435456 | bytes 3670016 | tf_op jit(solution)/shard_map/finish/pallas_call | solution.py:401
Async XLA Ops:
  10.6 27.4 %copy-start = (f32[2]{0:T(128)S(1)}, f32[2]{0:T(128)}, u32[]{:S(2)}) copy-start(f32[2]{0:T(128)} %gate_ref.5) | copy-start | bytes 28
  10.6 26.1 %all-to-all-start = ((bf16[8,256,256]{2,1,0:T(8,128)(2,1)}), bf16[8,256,256]{2,1,0:T(8,128)(2,1)}, u32[]{:S(2)}, u32[]{:S(2)}) async-start(bf16[8,256,256]{2,1,0:T(8,128)(2,1)} %get-tuple-element.27), calls=%async_computation | async-start | bytes 2097152 | tf_op jit(solution)/shard_map/all_to_all | solution.py:301
  18.0 5.1 %collective-permute-start = (bf16[2,136,128]{2,1,0:T(8,128)(2,1)S(1)}, bf16[2,136,128]{2,1,0:T(8,128)(2,1)S(1)}, u32[]{:S(2)}, u32[]{:S(2)}) collective-permute-start(bf16[2,136,128]{2,1,0:T(8,128)(2,1)S(1)} %get-tuple-element.28.total_ref), channel_id=1, source_target_pairs={{0,16},{16,0},{32,48},{48,32},{64,80},{80,64},{96,112},{112,96},{1... | collective-permute-start | bytes 208904 | tf_op jit(solution)/shard_map/ppermute | solution.py:317
  23.2 3.6 %collective-permute-start.1 = (bf16[2,136,128]{2,1,0:T(8,128)(2,1)S(1)}, bf16[2,136,128]{2,1,0:T(8,128)(2,1)S(1)}, u32[]{:S(2)}, u32[]{:S(2)}) collective-permute-start(bf16[2,136,128]{2,1,0:T(8,128)(2,1)S(1)} %get-tuple-element.29.total_ref), channel_id=1, source_target_pairs={{0,32},{16,48},{32,0},{48,16},{64,96},{80,112},{96,64},{112,80},{1... | collective-permute-start | bytes 208904 | tf_op jit(solution)/shard_map/ppermute | solution.py:317
  26.9 4.5 %collective-permute-start.2 = (bf16[2,136,128]{2,1,0:T(8,128)(2,1)S(1)}, bf16[2,136,128]{2,1,0:T(8,128)(2,1)S(1)}, u32[]{:S(2)}, u32[]{:S(2)}) collective-permute-start(bf16[2,136,128]{2,1,0:T(8,128)(2,1)S(1)} %get-tuple-element.31.total_ref), channel_id=1, source_target_pairs={{0,64},{16,80},{32,96},{48,112},{64,0},{80,16},{96,32},{112,48},{1... | collective-permute-start | bytes 208904 | tf_op jit(solution)/shard_map/ppermute | solution.py:317
  31.5 11.1 %collective-permute-start.3 = (bf16[2,136,128]{2,1,0:T(8,128)(2,1)S(1)}, bf16[2,136,128]{2,1,0:T(8,128)(2,1)S(1)}, u32[]{:S(2)}, u32[]{:S(2)}) collective-permute-start(bf16[2,136,128]{2,1,0:T(8,128)(2,1)S(1)} %get-tuple-element.33), channel_id=1, source_target_pairs={{0,224},{16,240},{32,192},{48,208},{64,160},{80,176},{96,128},{112... | collective-permute-start | bytes 208904 | tf_op jit(solution)/shard_map/ppermute | solution.py:317
  36.8 37.2 %collective-permute-start.14 = (bf16[8,256,256]{2,1,0:T(8,128)(2,1)}, bf16[8,256,256]{2,1,0:T(8,128)(2,1)}, u32[]{:S(2)}, u32[]{:S(2)}) collective-permute-start(bf16[8,256,256]{2,1,0:T(8,128)(2,1)} %all-to-all-done.w_hbm), channel_id=1, source_target_pairs={{0,1},{1,0},{2,3},{3,2},{4,5},{5,4},{6,7},{7,6},{8,9},{9,8},{10,11... | collective-permute-start | bytes 3145736 | tf_op jit(solution)/shard_map/ppermute | solution.py:302
  43.7 6.5 %collective-permute-start.10 = (bf16[512,256]{1,0:T(8,128)(2,1)S(1)}, bf16[512,256]{1,0:T(8,128)(2,1)S(1)}, u32[]{:S(2)}, u32[]{:S(2)}) collective-permute-start(bf16[512,256]{1,0:T(8,128)(2,1)S(1)} %get-tuple-element.43.rest_0_), channel_id=1, source_target_pairs={{0,4},{2,6},{4,8},{6,10},{8,12},{10,14},{12,0},{14,2},{1,5},{3,7},... | collective-permute-start | bytes 786440 | tf_op jit(solution)/shard_map/ppermute | solution.py:347
  44.9 5.6 %collective-permute-start.12 = (bf16[512,256]{1,0:T(8,128)(2,1)S(1)}, bf16[512,256]{1,0:T(8,128)(2,1)S(1)}, u32[]{:S(2)}, u32[]{:S(2)}) collective-permute-start(bf16[512,256]{1,0:T(8,128)(2,1)S(1)} %get-tuple-element.42.rest_2_), channel_id=1, source_target_pairs={{0,12},{2,14},{4,0},{6,2},{8,4},{10,6},{12,8},{14,10},{1,13},{3,15... | collective-permute-start | bytes 786440 | tf_op jit(solution)/shard_map/ppermute | solution.py:347
  46.5 6.4 %collective-permute-start.8 = (bf16[512,256]{1,0:T(8,128)(2,1)S(1)}, bf16[512,256]{1,0:T(8,128)(2,1)S(1)}, u32[]{:S(2)}, u32[]{:S(2)}) collective-permute-start(bf16[512,256]{1,0:T(8,128)(2,1)S(1)} %get-tuple-element.43.rest_0_), channel_id=1, source_target_pairs={{0,2},{2,0},{4,6},{6,4},{8,10},{10,8},{12,14},{14,12},{1,3},{3,1},... | collective-permute-start | bytes 786440 | tf_op jit(solution)/shard_map/ppermute | solution.py:350
  50.0 7.6 %collective-permute-start.9 = (bf16[512,256]{1,0:T(8,128)(2,1)S(1)}, bf16[512,256]{1,0:T(8,128)(2,1)S(1)}, u32[]{:S(2)}, u32[]{:S(2)}) collective-permute-start(bf16[512,256]{1,0:T(8,128)(2,1)S(1)} %get-tuple-element.42.rest_2_), channel_id=1, source_target_pairs={{0,2},{2,0},{4,6},{6,4},{8,10},{10,8},{12,14},{14,12},{1,3},{3,1},... | collective-permute-start | bytes 786440 | tf_op jit(solution)/shard_map/ppermute | solution.py:350
  50.3 7.4 %collective-permute-start.4 = (bf16[512,256]{1,0:T(8,128)(2,1)S(1)}, bf16[512,256]{1,0:T(8,128)(2,1)S(1)}, u32[]{:S(2)}, u32[]{:S(2)}) collective-permute-start(bf16[512,256]{1,0:T(8,128)(2,1)S(1)} %get-tuple-element.42.rest_2_), channel_id=1, source_target_pairs={{0,4},{2,6},{4,8},{6,10},{8,12},{10,14},{12,0},{14,2},{1,5},{3,7},... | collective-permute-start | bytes 786440 | tf_op jit(solution)/shard_map/ppermute | solution.py:347
  50.5 7.4 %collective-permute-start.6 = (bf16[512,256]{1,0:T(8,128)(2,1)S(1)}, bf16[512,256]{1,0:T(8,128)(2,1)S(1)}, u32[]{:S(2)}, u32[]{:S(2)}) collective-permute-start(bf16[512,256]{1,0:T(8,128)(2,1)S(1)} %get-tuple-element.43.rest_0_), channel_id=1, source_target_pairs={{0,12},{2,14},{4,0},{6,2},{8,4},{10,6},{12,8},{14,10},{1,13},{3,15... | collective-permute-start | bytes 786440 | tf_op jit(solution)/shard_map/ppermute | solution.py:347
  52.9 7.4 %collective-permute-start.11 = (bf16[512,256]{1,0:T(8,128)(2,1)S(1)}, bf16[512,256]{1,0:T(8,128)(2,1)S(1)}, u32[]{:S(2)}, u32[]{:S(2)}) collective-permute-start(bf16[512,256]{1,0:T(8,128)(2,1)S(1)} %collective-permute-done.10.rest_4_), channel_id=1, source_target_pairs={{0,2},{2,0},{4,6},{6,4},{8,10},{10,8},{12,14},{14,12},{1,3},{3,1},... | collective-permute-start | bytes 786440 | tf_op jit(solution)/shard_map/ppermute | solution.py:350
  57.6 7.8 %collective-permute-start.13 = (bf16[512,256]{1,0:T(8,128)(2,1)S(1)}, bf16[512,256]{1,0:T(8,128)(2,1)S(1)}, u32[]{:S(2)}, u32[]{:S(2)}) collective-permute-start(bf16[512,256]{1,0:T(8,128)(2,1)S(1)} %collective-permute-done.12.rest_6_), channel_id=1, source_target_pairs={{0,2},{2,0},{4,6},{6,4},{8,10},{10,8},{12,14},{14,12},{1,3},{3,1},... | collective-permute-start | bytes 786440 | tf_op jit(solution)/shard_map/ppermute | solution.py:350
  57.7 7.8 %collective-permute-start.15 = (bf16[512,256]{1,0:T(8,128)(2,1)S(1)}, bf16[512,256]{1,0:T(8,128)(2,1)S(1)}, u32[]{:S(2)}, u32[]{:S(2)}) collective-permute-start(bf16[512,256]{1,0:T(8,128)(2,1)S(1)} %collective-permute-done.10.rest_4_), channel_id=1, source_target_pairs={{0,4},{2,6},{4,8},{6,10},{8,12},{10,14},{12,0},{14,2},{1,5},{3,7},... | collective-permute-start | bytes 786440 | tf_op jit(solution)/shard_map/ppermute | solution.py:347
  57.9 11.6 %collective-permute-start.16 = (bf16[512,256]{1,0:T(8,128)(2,1)S(1)}, bf16[512,256]{1,0:T(8,128)(2,1)}, u32[]{:S(2)}, u32[]{:S(2)}) collective-permute-start(bf16[512,256]{1,0:T(8,128)(2,1)S(1)} %collective-permute-done.12.rest_6_), channel_id=1, source_target_pairs={{0,12},{2,14},{4,0},{6,2},{8,4},{10,6},{12,8},{14,10},{1,13},{3,15... | collective-permute-start | bytes 786440 | tf_op jit(solution)/shard_map/ppermute | solution.py:347
  60.4 11.9 %collective-permute-start.5 = (bf16[512,256]{1,0:T(8,128)(2,1)S(1)}, bf16[512,256]{1,0:T(8,128)(2,1)S(1)}, u32[]{:S(2)}, u32[]{:S(2)}) collective-permute-start(bf16[512,256]{1,0:T(8,128)(2,1)S(1)} %collective-permute-done.4.rest_0_.rest_8_), channel_id=1, source_target_pairs={{0,2},{2,0},{4,6},{6,4},{8,10},{10,8},{12,14},{14,12},{1,3},{3,1},... | collective-permute-start | bytes 786440 | tf_op jit(solution)/shard_map/ppermute | solution.py:350
  65.4 6.9 %collective-permute-start.7 = (bf16[512,256]{1,0:T(8,128)(2,1)S(1)}, bf16[512,256]{1,0:T(8,128)(2,1)S(1)}, u32[]{:S(2)}, u32[]{:S(2)}) collective-permute-start(bf16[512,256]{1,0:T(8,128)(2,1)S(1)} %collective-permute-done.6.rest_2_.rest_10_), channel_id=1, source_target_pairs={{0,2},{2,0},{4,6},{6,4},{8,10},{10,8},{12,14},{14,12},{1,3},{3,1},... | collective-permute-start | bytes 786440 | tf_op jit(solution)/shard_map/ppermute | solution.py:350
  65.5 12.1 %collective-permute-start.17 = (bf16[512,256]{1,0:T(8,128)(2,1)S(1)}, bf16[512,256]{1,0:T(8,128)(2,1)}, u32[]{:S(2)}, u32[]{:S(2)}) collective-permute-start(bf16[512,256]{1,0:T(8,128)(2,1)S(1)} %collective-permute-done.15.rest_12_), channel_id=1, source_target_pairs={{0,2},{2,0},{4,6},{6,4},{8,10},{10,8},{12,14},{14,12},{1,3},{3,1},... | collective-permute-start | bytes 786440 | tf_op jit(solution)/shard_map/ppermute | solution.py:350
  69.5 8.1 %collective-permute-start.18 = (bf16[512,256]{1,0:T(8,128)(2,1)}, bf16[512,256]{1,0:T(8,128)(2,1)}, u32[]{:S(2)}, u32[]{:S(2)}) collective-permute-start(bf16[512,256]{1,0:T(8,128)(2,1)} %collective-permute-done.16.rest_13_), channel_id=1, source_target_pairs={{0,2},{2,0},{4,6},{6,4},{8,10},{10,8},{12,14},{14,12},{1,3},{3,1},... | collective-permute-start | bytes 786440 | tf_op jit(solution)/shard_map/ppermute | solution.py:350

commit v3 on v2

--- a/solution.py
+++ b/solution.py
@@ -38,61 +38,67 @@
     )
 
 
-def qkv_kernel(cuts, dp_ref, resets_ref, x_hbm, wq_hbm, wk_hbm, wv_hbm, wo_hbm, q_ref, k_ref, v_ref, s_ref, o_hbm, x_ref, w_ref, acc_ref, o_ref, sem, in_sem, out_sem):
+def qkv_kernel(cuts, at_ref, dp_ref, resets_ref, x_hbm, wq_hbm, wk_hbm, wv_hbm, wo_hbm, q_ref, k_ref, v_ref, s_ref, o_hbm, own_ref, give_ref, x_ref, w_ref, wq_ref, acc_ref, o_ref, sem, q_sem, in_sem, out_sem, extra_sem):
     toks, cols = q_ref.shape
     heads = cols // DH
     copies = []
     for i, (lo, hi) in enumerate(cuts):
         at = slice(lo, hi)
         batch = [pltpu.make_async_copy(x_hbm.at[:, at], x_ref.at[:, at], sem.at[i, 0])]
-        for j, w_hbm in enumerate((wk_hbm, wv_hbm, wq_hbm)):
+        for j, w_hbm in enumerate((wk_hbm, wv_hbm)):
             to = slice(j * cols, (j + 1) * cols)
             batch.append(pltpu.make_async_copy(w_hbm.at[at, :], w_ref.at[at, to], sem.at[i, j + 1]))
         for copy in batch:
             copy.start()
         copies.append(batch)
+    late = pltpu.make_async_copy(wq_hbm, wq_ref, q_sem)
+    late.start()
     pieces, _, slim = o_ref.shape
     wide = wo_hbm.shape[1] // pieces
-    packs = []
+    packs, extras = [], []
     for j in range(pieces):
         share = pl.ds(pl.multiple_of(j * wide + dp_ref[0] * slim, slim), slim)
         packs.append(pltpu.make_async_copy(wo_hbm.at[:, share], o_ref.at[j], in_sem.at[j]))
-    for copy in packs:
+    for i, to_ref in enumerate((own_ref, give_ref)):
+        lo = jnp.bitwise_xor(at_ref[0], i) * wide + (1 - dp_ref[0]) * slim
+        share = pl.ds(pl.multiple_of(lo, slim), slim)
+        extras.append(pltpu.make_async_copy(wo_hbm.at[:, share], to_ref, extra_sem.at[i]))
+    for copy in packs + extras:
         copy.start()
     moves = [pltpu.make_async_copy(o_ref.at[j], o_hbm.at[j], out_sem.at[j]) for j in range(pieces)]
-    for i, (lo, hi) in enumerate(cuts[:-1]):
+    parts = 8
+    part = toks // parts
+    for i, (lo, hi) in enumerate(cuts):
         at = slice(lo, hi)
         for copy in copies[i]:
             copy.wait()
-        part = toks // 8
-        for r in range(8):
+        for r in range(parts):
             rows = slice(r * part, (r + 1) * part)
             piece = dot(x_ref[rows, at], w_ref[at, :])
-            if i == 0:
+            if i > 0:
+                piece = acc_ref[rows, :] + piece
+            if i < len(cuts) - 1:
                 acc_ref[rows, :] = piece
             else:
-                acc_ref[rows, :] += piece
-    at = slice(*cuts[-1])
-    for copy in copies[-1]:
-        copy.wait()
-    part = toks // 4
+                whole = piece.astype(BF)
+                k_ref[rows, :] = whole[:, :cols]
+                v_ref[rows, :] = whole[:, cols:]
+    late.wait()
     norm, memory = None, [None] * heads
-    for r in range(4):
+    parts = 4
+    part = toks // parts
+    for r in range(parts):
         rows = slice(r * part, (r + 1) * part)
-        whole = (acc_ref[rows, :] + dot(x_ref[rows, at], w_ref[at, :])).astype(BF)
-        keys, vals = whole[:, :cols], whole[:, cols : 2 * cols]
-        k_ref[rows, :] = keys
-        v_ref[rows, :] = vals
-        q_ref[rows, :] = whole[:, 2 * cols :]
-        feat = features(keys.astype(F32))
+        q_ref[rows, :] = dot(x_ref[rows, :], wq_ref[...]).astype(BF)
+        feat = features(k_ref[rows, :].astype(F32))
         term = jnp.sum(feat, axis=0, keepdims=True)
         norm = term if norm is None else norm + term
         feat_bf = feat.astype(BF)
         for h in range(heads):
             of = slice(h * DH, (h + 1) * DH)
-            term = dot(vals[:, of], feat_bf[:, of], ((0,), (0,)))
+            term = dot(v_ref[rows, of], feat_bf[:, of], ((0,), (0,)))
             memory[h] = term if memory[h] is None else memory[h] + term
-        if r == 2:
+        if r == 1:
             for pack, move in zip(packs, moves):
                 pack.wait()
                 move.start()
@@ -101,8 +107,8 @@
     for h in range(heads):
         tail = jnp.where(row == 0, norm[:, h * DH : (h + 1) * DH], keep)
         s_ref[h] = jnp.concatenate([memory[h], tail], axis=0).astype(BF)
-    for move in moves:
-        move.wait()
+    for copy in moves + extras:
+        copy.wait()
 
 
 def joined(bit, seg, got, before, flag):
@@ -166,72 +172,73 @@
         low_ref[:, at] = mixed[half:]
 
 
-def source(at_ref, shift, flip, size):
-    j = jnp.bitwise_and(at_ref[0] + shift, size - 1)
-    return jnp.bitwise_xor(j, 1) if flip else j
-
-
-def project_kernel(plan, chained, reach, at_ref, w_hbm, *rest):
-    values, rest = rest[: len(plan)], rest[len(plan) :]
-    if chained:
-        acc_ref, rest = rest[0], rest[1:]
-    if reach:
-        o_ref, far_ref, w_ref, sem, far_sem = rest
-    else:
-        o_ref, w_ref, sem = rest
-    size = w_hbm.shape[0]
-    half = values[0].shape[0]
-    places = []
-    for _, shift, flip in plan:
-        if (shift, flip) not in places:
-            places.append((shift, flip))
-    copies = [
-        pltpu.make_async_copy(w_hbm.at[source(at_ref, *where, size)], w_ref.at[i], sem.at[i])
-        for i, where in enumerate(places)
-    ]
-    late = []
-    if reach:
-        late = [
-            pltpu.make_async_copy(w_hbm.at[source(at_ref, 4, i == 1, size)], far_ref.at[i], far_sem.at[i])
-            for i in range(2)
-        ]
-    for copy in copies + late:
+def pack_kernel(at_ref, mine_hbm, o_ref, near_ref, sem, near_sem):
+    base = at_ref[0] - jnp.bitwise_and(at_ref[0], 1)
+    size, skip = mine_hbm.shape[0], 2
+    copies = []
+    for r in range(skip, size):
+        j = jnp.bitwise_and(base + r, size - 1)
+        copies.append(pltpu.make_async_copy(mine_hbm.at[j], o_ref.at[r - skip], sem.at[r - skip]))
+    for r in range(size):
+        j = jnp.bitwise_and(base + r, size - 1)
+        copies.append(pltpu.make_async_copy(mine_hbm.at[j], near_ref.at[r], near_sem.at[r]))
+    for copy in copies:
         copy.start()
     for copy in copies:
         copy.wait()
+
+
+def relative(at_ref, shift, flip):
+    core = jnp.bitwise_and(at_ref[0], 1)
+    return {0: 0, 2: 2, 4: 4, -2: 6}[shift] + (1 - core if flip else core)
+
+
+def add_terms(plan, values, w_of, acc_ref, o_ref):
+    half = values[0].shape[0]
     for side in range(2):
         rows = slice(side * half, (side + 1) * half)
-        total = acc_ref[rows, :] if chained else None
+        total = None if acc_ref is None else acc_ref[rows, :]
         for value, (place, shift, flip) in zip(values, plan):
             if place == side:
-                term = dot(value[...], w_ref[places.index((shift, flip))])
+                term = dot(value[...], w_of(shift, flip))
                 total = term if total is None else total + term
         o_ref[rows, :] = total
-    for copy in late:
-        copy.wait()
-
-
-def later_kernel(plan, at_ref, w_hbm, far_ref, acc_ref, *rest):
-    values, (mine_ref, o_ref, last_ref, w_ref, sem, last_sem) = rest[: len(plan)], rest[len(plan) :]
-    half = values[0].shape[0]
-    last = pltpu.make_async_copy(w_hbm.at[source(at_ref, 4, True, w_hbm.shape[0])], last_ref, last_sem)
-    last.start()
-    project_kernel(plan, False, False, at_ref, w_hbm, *values, o_ref, w_ref, sem)
-    for side, value in enumerate(values[-2:]):
+
+
+def near_kernel(plan, at_ref, w_ref, *rest):
+    add_terms(plan, rest[:-1], lambda *where: w_ref[relative(at_ref, *where)], None, rest[-1])
+
+
+def twin_block(at_ref, twin_ref, own_ref, part_ref, shift, flip):
+    if shift == 0:
+        return part_ref[...] if flip else own_ref[...]
+    return twin_ref[relative(at_ref, shift, flip) - 2]
+
+
+def middle_kernel(plan, skip, at_ref, w_ref, twin_ref, own_ref, part_ref, acc_ref, *rest):
+    values, (mine_ref, o_ref) = rest[: len(plan)], rest[len(plan) :]
+    add_terms(plan[skip:], values[skip:], lambda *where: w_ref[relative(at_ref, *where)], acc_ref, mine_ref)
+    add_terms(plan, values, lambda *where: twin_block(at_ref, twin_ref, own_ref, part_ref, *where), None, o_ref)
+
+
+def later_kernel(at_ref, w_ref, twin_ref, mine_in, twin_in, top_ref, low_ref, mine_ref, o_ref):
+    half = top_ref.shape[0]
+    j = relative(at_ref, 4, False)
+    for side, value in enumerate((top_ref, low_ref)):
         rows = slice(side * half, (side + 1) * half)
-        mine_ref[rows, :] = acc_ref[rows, :] + dot(value[...], far_ref[0])
-    last.wait()
-
-
-def finish_kernel(dp_ref, mine_ref, twin_ref, acc_mine_ref, acc_twin_ref, top_ref, low_ref, o_ref):
-    half, slim = o_ref.shape[0], twin_ref.shape[1]
+        mine_ref[rows, :] = mine_in[rows, :] + dot(value[...], w_ref[j])
+        o_ref[rows, :] = twin_in[rows, :] + dot(value[...], twin_ref[j - 2])
+
+
+def finish_kernel(at_ref, dp_ref, mine_ref, twin_ref, acc_mine_ref, acc_twin_ref, top_ref, low_ref, o_ref):
+    half, slim = o_ref.shape[0], twin_ref.shape[2]
     for side, part in enumerate((top_ref, low_ref)):
 
         @pl.when(pl.program_id(0) == side)
         def _():
             rows = slice(side * half, (side + 1) * half)
-            mine = acc_mine_ref[rows, :] + dot(part[...], mine_ref[1])
-            theirs = acc_twin_ref[rows, :] + dot(part[...], twin_ref[...])
+            mine = acc_mine_ref[rows, :] + dot(part[...], mine_ref[relative(at_ref, 4, True)])
+            theirs = acc_twin_ref[rows, :] + dot(part[...], twin_ref[relative(at_ref, 4, True) - 2])
             for index, total in ((dp_ref[0], mine), (1 - dp_ref[0], theirs)):
                 o_ref[:, pl.ds(pl.multiple_of(index * slim, slim), slim)] = total.astype(BF)
 
@@ -257,30 +264,34 @@
     remote = pl.BlockSpec(memory_space=pltpu.HBM)
     whole = pl.BlockSpec(memory_space=pltpu.VMEM)
 
-    edges = [0, 512, 1536, 2816, 4096]
+    edges = [0, 512, 1536, 2560, 3456, 4096]
     cuts = tuple(zip(edges[:-1], edges[1:]))
     flat = jax.ShapeDtypeStruct((toks, cols), BF)
+    piece = jax.ShapeDtypeStruct((cols, slim), BF)
     payload = jax.ShapeDtypeStruct((heads, ROWS, DH), BF)
     operands = (tokens, w_query, w_key, w_value, w_out)
-    queries, keys, vals, state, w_cut = call(
+    queries, keys, vals, state, w_cut, w_own, w_give = call(
         functools.partial(qkv_kernel, cuts),
-        (flat, flat, flat, payload, jax.ShapeDtypeStruct((n_tp, cols, slim), BF)),
+        (flat, flat, flat, payload, jax.ShapeDtypeStruct((n_tp, cols, slim), BF), piece, piece),
         36,
         6 * toks * width * cols,
         2 * (toks * width + 3 * width * cols + 4 * toks * cols),
-        in_specs=[smem] * 2 + [remote] * 5,
-        out_specs=(whole,) * 4 + (remote,),
+        in_specs=[smem] * 3 + [remote] * 5,
+        out_specs=(whole,) * 4 + (remote, whole, whole),
         scratch_shapes=[
             pltpu.VMEM((toks, width), BF),
-            pltpu.VMEM((width, 3 * cols), BF),
-            pltpu.VMEM((toks, 3 * cols), F32),
+            pltpu.VMEM((width, 2 * cols), BF),
+            pltpu.VMEM((width, cols), BF),
+            pltpu.VMEM((toks, 2 * cols), F32),
             pltpu.VMEM((n_tp, cols, slim), BF),
-            pltpu.SemaphoreType.DMA((len(cuts), 4)),
+            pltpu.SemaphoreType.DMA((len(cuts), 3)),
+            pltpu.SemaphoreType.DMA(()),
             pltpu.SemaphoreType.DMA((n_tp,)),
             pltpu.SemaphoreType.DMA((n_tp,)),
+            pltpu.SemaphoreType.DMA((2,)),
         ],
         name="qkv",
-    )(twin, resets, *(stay(a) for a in operands))
+    )(place, twin, resets, *(stay(a) for a in operands))
 
     def attend(h):
         spec = pl.BlockSpec((toks, DH), lambda i: (0, h))
@@ -299,7 +310,20 @@
         )(mem_gate, queries, keys, vals)
 
     w_mine = stay(lax.all_to_all(stay(w_cut), "tp", 0, 0, tiled=True))
-    w_twin = stay(lax.ppermute(w_mine, "dp", [(i, n_dp - 1 - i) for i in range(n_dp)]))
+    others = jax.ShapeDtypeStruct((n_tp - 2, cols, slim), BF)
+    w_send, w_near = call(
+        pack_kernel,
+        (others, jax.ShapeDtypeStruct((n_tp, cols, slim), BF)),
+        8,
+        0,
+        4 * (2 * n_tp - 2) * cols * slim,
+        in_specs=[smem, remote],
+        out_specs=(whole, whole),
+        scratch_shapes=[pltpu.SemaphoreType.DMA((n_tp - 2,)), pltpu.SemaphoreType.DMA((n_tp,))],
+        name="pack",
+    )(place, w_mine)
+    w_twin = lax.ppermute(w_send, "dp", [(i, n_dp - 1 - i) for i in range(n_dp)])
+    w_part = lax.ppermute(w_give, "tp", [(i, i ^ 1) for i in range(n_tp)])
 
     local, q_feat = [], []
     for h in range(heads):
@@ -356,48 +380,32 @@
     def pair(value, side, shift):
         return [(value, (side, shift, False)), (swap(value), (side, shift, True))]
 
-    early = pair(top, 0, 0) + pair(low, 1, 0) + pair(below_top, 0, -2) + pair(above_low, 1, 2)
-    second = pair(below_low, 1, -2) + pair(above_top, 0, 2)
-
-    def project(parts, weights, acc, reach):
-        values, plan = zip(*parts)
-        places = len({where[1:] for where in plan})
-        out = (jax.ShapeDtypeStruct((toks, slim), F32), jax.ShapeDtypeStruct((2, cols, slim), BF))
+    first = pair(below_top, 0, -2) + pair(above_low, 1, 2)
+    early = pair(top, 0, 0) + pair(low, 1, 0) + first[::2]
+    rest = first[1::2] + pair(below_low, 1, -2) + pair(above_top, 0, 2)
+    far_swaps = (swap(far_top), swap(far_low))
+    block = jax.ShapeDtypeStruct((toks, slim), F32)
+
+    def project(kernel, name, shapes, terms, *operands):
         return call(
-            functools.partial(project_kernel, plan, acc is not None, reach),
-            out if reach else out[0],
-            14,
-            2 * len(values) * half * cols * slim,
-            2 * len(values) * half * cols + 6 * toks * slim,
-            in_specs=[smem, remote] + [whole] * (len(values) + (acc is not None)),
-            out_specs=(whole, whole) if reach else whole,
-            scratch_shapes=[pltpu.VMEM((places, cols, slim), BF), pltpu.SemaphoreType.DMA((places,))]
-            + [pltpu.SemaphoreType.DMA((2,))] * reach,
-            name="project",
-        )(place, weights, *values, *([] if acc is None else [acc]))
-
-    acc_mine = project(early, w_mine, None, False)
-    acc_mine, far_mine = project(second, w_mine, acc_mine, True)
-    ends = [(far_top, (0, 4, False)), (far_low, (1, 4, False))]
-    far_swaps = (swap(far_top), swap(far_low))
-    values, plan = zip(*(early + second + ends))
-    places = len({where[1:] for where in plan})
-    block = jax.ShapeDtypeStruct((toks, slim), F32)
-    acc_mine, acc_twin, last_twin = call(
-        functools.partial(later_kernel, plan),
-        (block, block, jax.ShapeDtypeStruct((cols, slim), BF)),
-        16,
-        2 * (len(values) + 2) * half * cols * slim,
-        2 * len(values) * half * cols + 10 * toks * slim,
-        in_specs=[smem, remote] + [whole] * (2 + len(values)),
-        out_specs=(whole,) * 3,
-        scratch_shapes=[
-            pltpu.VMEM((places, cols, slim), BF),
-            pltpu.SemaphoreType.DMA((places,)),
-            pltpu.SemaphoreType.DMA(()),
-        ],
-        name="later",
-    )(place, w_twin, far_mine, acc_mine, *values)
+            kernel,
+            shapes,
+            16,
+            2 * terms * half * cols * slim,
+            2 * terms * half * cols + 8 * toks * slim,
+            in_specs=[smem] + [whole] * (len(operands) - 1),
+            out_specs=(whole,) * len(shapes),
+            name=name,
+        )(*operands)
+
+    values, plan = zip(*early)
+    (acc,) = project(functools.partial(near_kernel, plan), "near", (block,), len(plan), place, w_near, *values)
+    values, plan = zip(*(early + rest))
+    accs = project(
+        functools.partial(middle_kernel, plan, len(early)), "middle", (block, block), len(plan) + len(rest),
+        place, w_near, w_twin, w_own, w_part, acc, *values,
+    )
+    accs = project(later_kernel, "later", (block, block), 4, place, w_near, w_twin, *accs, far_top, far_low)
     return call(
         finish_kernel,
         jax.ShapeDtypeStruct((toks, out_cols), BF),
@@ -405,10 +413,10 @@
         2 * toks * cols * out_cols,
         2 * toks * cols + 6 * toks * out_cols,
         grid=(2,),
-        in_specs=[smem] + [whole] * 6,
+        in_specs=[smem] * 2 + [whole] * 6,
         out_specs=pl.BlockSpec((half, out_cols), lambda i: (i, 0)),
         name="finish",
-    )(twin, far_mine, last_twin, acc_mine, acc_twin, *far_swaps)
+    )(place, twin, w_near, w_twin, *accs, *far_swaps)
 
 
 def solution(mesh):

time: 80.3 us -> 72.9 us (0.908)
  starting transfers between devices: 44.1 us -> 39 us
  Pallas kernels: 25.6 us -> 21.3 us
  waiting for transfers between devices: 9.55 us -> 11.6 us
    ppermute x8, starting transfers between devices: 18.1 us -> 11.3 us  [swap(): return lax.ppermute(value, 'tp', [(i, i ^ 1) for i in range(n_tp)])]
    ppermute x6, waiting for transfers between devices: 0.29 us -> 3.95 us  [along(): lax.ppermute(value, 'tp', [(i, (i + 2 * by) % n_tp) for i in range(n_tp)])]
    pallas_call x3 -> x4, Pallas kernels: 7.19 us -> 4.06 us  [the longest x3 2.42 us: project(): call(kernel, shapes, 16, 2 * terms * half * cols * slim, 2 * terms * half...]
    ppermute x1 -> x2, starting transfers between devices: 1.22 us -> 2.91 us  [the longest x1 1.61 us: on_device(): w_part = lax.ppermute(w_give, 'tp', [(i, i ^ 1) for i in range(n_tp)])]
    ppermute x4, waiting for transfers between devices: 9.23 us -> 7.64 us  [on_device(): got = lax.ppermute(total, 'seg', pairs)]
    pallas_call x1, Pallas kernels: 2.52 us -> 1.49 us  [on_device(): call(finish_kernel, jax.ShapeDtypeStruct((toks, out_cols), BF), 10, 2 * t...]
  transfers between devices with their start and end apart: 20 -> 21, of which waited for: 4 -> 6; matrix products, arithmetic and copies ran while one was open for 0% -> 0% of each run, Pallas kernels for 16% -> 14%
where the time goes in v3:
time: 72.9 us; the launch traced here: 72.7 us
  starting transfers between devices  39 us (53%)
  Pallas kernels  21.3 us (29%)
  waiting for transfers between devices  11.6 us (16%)
  between operations  0.79 us (1%)
    ppermute x8, starting transfers between devices, swap(): return lax.ppermute(value, 'tp', [(i, i ^ 1) for i in range(n_tp)])  11.3 us
    pallas_call x1, Pallas kernels, on_device(): call(functools.partial(qkv_kernel, cuts), (flat, flat, flat, payload, jax...  9.79 us
    ppermute x4, starting transfers between devices, on_device(): got = lax.ppermute(total, 'seg', pairs)  9.51 us
    ppermute x6, starting transfers between devices, along(): lax.ppermute(value, 'tp', [(i, (i + 2 * by) % n_tp) for i in range(n_tp)])  8.04 us
    ppermute x4, waiting for transfers between devices, on_device(): got = lax.ppermute(total, 'seg', pairs)  7.64 us
    all_to_all x1, starting transfers between devices, on_device(): w_mine = stay(lax.all_to_all(stay(w_cut), 'tp', 0, 0, tiled=True))  7.33 us
    pallas_call x2, Pallas kernels, attend(): call(functools.partial(attend_kernel, h), (jax.ShapeDtypeStruct((toks, DH...  4.63 us
    ppermute x6, waiting for transfers between devices, along(): lax.ppermute(value, 'tp', [(i, (i + 2 * by) % n_tp) for i in range(n_tp)])  3.95 us
  transfers between devices with their start and end apart: 21, of which 6 were waited for; matrix products, arithmetic and copies ran while one was open for 0% of the time, Pallas kernels for 14%

profile of v3, /device:TPU:1, one launch (start us, length us, event | category | flops | bytes accessed | tf_op | source)
XLA Modules:
  0.0 72.7 jit_solution(11818224848763048456)
XLA Ops:
  0.7 9.8 %qkv.1 = (bf16[1024,256]{1,0:T(8,128)(2,1)S(1)}, bf16[1024,256]{1,0:T(8,128)(2,1)S(1)}, bf16[1024,256]{1,0:T(8,128)(2,1)S(1)}, bf16[2,136,128]{2,1,0:T(8,128)(2,...) custom-call(s32[1]{0:T(128)} %bitcast.at_ref, s32[1]{0:T(128)} %bitcast.1.dp_ref, ...), custom_call_target="tpu_custom_call" | custom-call | flops 6442450944 | bytes 16777216 | tf_op jit(solution)/shard_map/qkv/pallas_call | solution.py:273
  10.4 0.0 copy-start
  10.5 7.3 %all-to-all-start = ((bf16[8,256,256]{2,1,0:T(8,128)(2,1)}), bf16[8,256,256]{2,1,0:T(8,128)(2,1)}, u32[]{:S(2)}, u32[]{:S(2)}) async-start(bf16[8,256,256]{2,1,0:T(8,128)(2,1)} %get-tuple-element.30), calls=%async_computation | async-start | bytes 2097152 | tf_op jit(solution)/shard_map/all_to_all | solution.py:312
  17.8 1.4 %collective-permute-start.2 = (bf16[2,136,128]{2,1,0:T(8,128)(2,1)S(1)}, bf16[2,136,128]{2,1,0:T(8,128)(2,1)S(1)}, u32[]{:S(2)}, u32[]{:S(2)}) collective-permute-start(bf16[2,136,128]{2,1,0:T(8,128)(2,1)S(1)} %get-tuple-element.35.total_ref), channel_id=1, source_target_pairs={{0,16},{16,0},{32,48},{48,32},{64,80},{80,64},{96,112},{112,96},{1... | collective-permute-start | bytes 208904 | tf_op jit(solution)/shard_map/ppermute | solution.py:341
  19.2 3.7 %collective-permute-done.2.got_ref = bf16[2,136,128]{2,1,0:T(8,128)(2,1)S(1)} collective-permute-done((bf16[2,136,128]{2,1,0:T(8,128)(2,1)S(1)}, bf16[2,136,128]{2,1,0:T(8,128)(2,1)S(1)}, u32[]{:S(2)}, u32[]{:S(2)}) %collective-permute-start.2) | collective-permute-done | bytes 69664 | tf_op jit(solution)/shard_map/ppermute | solution.py:341
  22.9 0.1 merge.3
  23.0 0.6 collective-permute-start.3
  23.6 3.1 %collective-permute-done.3.got_ref = bf16[2,136,128]{2,1,0:T(8,128)(2,1)S(1)} collective-permute-done((bf16[2,136,128]{2,1,0:T(8,128)(2,1)S(1)}, bf16[2,136,128]{2,1,0:T(8,128)(2,1)S(1)}, u32[]{:S(2)}, u32[]{:S(2)}) %collective-permute-start.3) | collective-permute-done | bytes 69664 | tf_op jit(solution)/shard_map/ppermute | solution.py:341
  26.6 0.1 merge.4
  26.7 2.1 %collective-permute-start.4 = (bf16[2,136,128]{2,1,0:T(8,128)(2,1)S(1)}, bf16[2,136,128]{2,1,0:T(8,128)(2,1)S(1)}, u32[]{:S(2)}, u32[]{:S(2)}) collective-permute-start(bf16[2,136,128]{2,1,0:T(8,128)(2,1)S(1)} %get-tuple-element.38.total_ref), channel_id=1, source_target_pairs={{0,64},{16,80},{32,96},{48,112},{64,0},{80,16},{96,32},{112,48},{1... | collective-permute-start | bytes 208904 | tf_op jit(solution)/shard_map/ppermute | solution.py:341
  28.8 1.6 %collective-permute-start.1 = (bf16[256,256]{1,0:T(8,128)(2,1)S(1)}, bf16[256,256]{1,0:T(8,128)(2,1)S(1)}, u32[]{:S(2)}, u32[]{:S(2)}) collective-permute-start(bf16[256,256]{1,0:T(8,128)(2,1)S(1)} %get-tuple-element.34), channel_id=1, source_target_pairs={{0,2},{2,0},{4,6},{6,4},{8,10},{10,8},{12,14},{14,12},{1,3},{3,1},... | collective-permute-start | bytes 393224 | tf_op jit(solution)/shard_map/ppermute | solution.py:326
  30.4 0.8 %collective-permute-done.4.got_ref = bf16[2,136,128]{2,1,0:T(8,128)(2,1)S(1)} collective-permute-done((bf16[2,136,128]{2,1,0:T(8,128)(2,1)S(1)}, bf16[2,136,128]{2,1,0:T(8,128)(2,1)S(1)}, u32[]{:S(2)}, u32[]{:S(2)}) %collective-permute-start.4) | collective-permute-done | bytes 69664 | tf_op jit(solution)/shard_map/ppermute | solution.py:341
  31.3 0.1 merge.5
  31.3 5.4 %collective-permute-start.5 = (bf16[2,136,128]{2,1,0:T(8,128)(2,1)S(1)}, bf16[2,136,128]{2,1,0:T(8,128)(2,1)S(1)}, u32[]{:S(2)}, u32[]{:S(2)}) collective-permute-start(bf16[2,136,128]{2,1,0:T(8,128)(2,1)S(1)} %get-tuple-element.40), channel_id=1, source_target_pairs={{0,224},{16,240},{32,192},{48,208},{64,160},{80,176},{96,128},{112... | collective-permute-start | bytes 208904 | tf_op jit(solution)/shard_map/ppermute | solution.py:341
  36.8 0.0 copy-done
  36.8 2.3 %attend.3 = (bf16[1024,128]{1,0:T(8,128)(2,1)S(1)}, bf16[1024,128]{1,0:T(8,128)(2,1)S(1)}) custom-call(f32[2]{0:T(128)S(1)} %copy-done, bf16[1024,256]{1,0:T(8,128)(2,1)S(1)} %get-tuple-element.42.q_ref, bf16[1024,256]{1,0:T(8,128)(2,1)S(1)} %get-tuple-element.43.k_ref, bf16[1024,256]{1,0:T(8,128)(2,1)S(1)} %get-tuple-element.44.v_ref), custom_call_target="tpu_custom_call" | custom-call | flops 536870912 | bytes 1310720 | tf_op jit(solution)/shard_map/attend/pallas_call | solution.py:298
  39.1 2.3 %attend.2 = (bf16[1024,128]{1,0:T(8,128)(2,1)S(1)}, bf16[1024,128]{1,0:T(8,128)(2,1)S(1)}) custom-call(f32[2]{0:T(128)S(1)} %copy-done, bf16[1024,256]{1,0:T(8,128)(2,1)S(1)} %get-tuple-element.42.q_ref, bf16[1024,256]{1,0:T(8,128)(2,1)S(1)} %get-tuple-element.43.k_ref, bf16[1024,256]{1,0:T(8,128)(2,1)S(1)} %get-tuple-element.44.v_ref), custom_call_target="tpu_custom_call" | custom-call | flops 536870912 | bytes 1310720 | tf_op jit(solution)/shard_map/attend/pallas_call | solution.py:298
  41.4 0.0 collective-permute-done.5.got_ref
  41.4 1.1 %read.1 = (bf16[512,256]{1,0:T(8,128)(2,1)S(1)}, bf16[512,256]{1,0:T(8,128)(2,1)S(1)}) custom-call(s32[1]{0:T(128)} %bitcast.2.seg_ref, s32[1]{0:T(128)S(6)} %copy.8.resets_ref, f32[2]{0:T(128)S(1)} %copy-done, bf16[2,136,128]{2,1,0:T(8,128)(2,1)S(1)} %collective-permute-done.5.got_ref, f32[2,136,128]{2,1,0:T(8,128)S(1)} %get-tuple-element.41.before_ref, ...), custom_call_target="tpu_custom_call" | custom-call | flops 134217728 | bytes 2097152 | tf_op jit(solution)/shard_map/read/pallas_call | solution.py:359
  42.5 2.7 %collective-permute-start.6 = (bf16[512,256]{1,0:T(8,128)(2,1)S(1)}, bf16[512,256]{1,0:T(8,128)(2,1)S(1)}, u32[]{:S(2)}, u32[]{:S(2)}) collective-permute-start(bf16[512,256]{1,0:T(8,128)(2,1)S(1)} %get-tuple-element.49.rest_0_), channel_id=1, source_target_pairs={{0,2},{2,0},{4,6},{6,4},{8,10},{10,8},{12,14},{14,12},{1,3},{3,1},... | collective-permute-start | bytes 786440 | tf_op jit(solution)/shard_map/ppermute | solution.py:374
  45.2 0.1 collective-permute-start.7
  45.3 1.4 %collective-permute-start.8 = (bf16[512,256]{1,0:T(8,128)(2,1)S(1)}, bf16[512,256]{1,0:T(8,128)(2,1)S(1)}, u32[]{:S(2)}, u32[]{:S(2)}) collective-permute-start(bf16[512,256]{1,0:T(8,128)(2,1)S(1)} %get-tuple-element.49.rest_0_), channel_id=1, source_target_pairs={{0,4},{2,6},{4,8},{6,10},{8,12},{10,14},{12,0},{14,2},{1,5},{3,7},... | collective-permute-start | bytes 786440 | tf_op jit(solution)/shard_map/ppermute | solution.py:371
  46.7 1.3 %collective-permute-start.9 = (bf16[512,256]{1,0:T(8,128)(2,1)S(1)}, bf16[512,256]{1,0:T(8,128)(2,1)S(1)}, u32[]{:S(2)}, u32[]{:S(2)}) collective-permute-start(bf16[512,256]{1,0:T(8,128)(2,1)S(1)} %get-tuple-element.50.rest_2_), channel_id=1, source_target_pairs={{0,12},{2,14},{4,0},{6,2},{8,4},{10,6},{12,8},{14,10},{1,13},{3,15... | collective-permute-start | bytes 786440 | tf_op jit(solution)/shard_map/ppermute | solution.py:371
  48.0 0.0 all-to-all-done.mine_hbm
  48.0 1.6 %pack.1 = (bf16[6,256,256]{2,1,0:T(8,128)(2,1)S(1)}, bf16[8,256,256]{2,1,0:T(8,128)(2,1)S(1)}) custom-call(s32[1]{0:T(128)} %bitcast.at_ref, bf16[8,256,256]{2,1,0:T(8,128)(2,1)} %all-to-all-done.mine_hbm), custom_call_target="tpu_custom_call" | custom-call | bytes 3670016 | tf_op jit(solution)/shard_map/pack/pallas_call | solution.py:314
  49.7 0.0 collective-permute-done.1.part_ref
  49.7 1.3 %collective-permute-start = (bf16[6,256,256]{2,1,0:T(8,128)(2,1)S(1)}, bf16[6,256,256]{2,1,0:T(8,128)(2,1)S(1)}, u32[]{:S(2)}, u32[]{:S(2)}) collective-permute-start(bf16[6,256,256]{2,1,0:T(8,128)(2,1)S(1)} %get-tuple-element.32), channel_id=1, source_target_pairs={{0,1},{1,0},{2,3},{3,2},{4,5},{5,4},{6,7},{7,6},{8,9},{9,8},{10,11... | collective-permute-start | bytes 2359304 | tf_op jit(solution)/shard_map/ppermute | solution.py:325
  51.0 0.0 collective-permute-done.6.rest_1_
  51.0 0.3 collective-permute-start.12
  51.2 0.0 collective-permute-done.7.rest_3_
  51.2 2.4 %collective-permute-start.14 = (bf16[512,256]{1,0:T(8,128)(2,1)S(1)}, bf16[512,256]{1,0:T(8,128)(2,1)S(1)}, u32[]{:S(2)}, u32[]{:S(2)}) collective-permute-start(bf16[512,256]{1,0:T(8,128)(2,1)S(1)} %get-tuple-element.49.rest_0_), channel_id=1, source_target_pairs={{0,12},{2,14},{4,0},{6,2},{8,4},{10,6},{12,8},{14,10},{1,13},{3,15... | collective-permute-start | bytes 786440 | tf_op jit(solution)/shard_map/ppermute | solution.py:371
  53.7 0.4 collective-permute-done.8.rest_4_
  54.0 1.5 %collective-permute-start.10 = (bf16[512,256]{1,0:T(8,128)(2,1)S(1)}, bf16[512,256]{1,0:T(8,128)(2,1)S(1)}, u32[]{:S(2)}, u32[]{:S(2)}) collective-permute-start(bf16[512,256]{1,0:T(8,128)(2,1)S(1)} %collective-permute-done.8.rest_4_), channel_id=1, source_target_pairs={{0,2},{2,0},{4,6},{6,4},{8,10},{10,8},{12,14},{14,12},{1,3},{3,1},... | collective-permute-start | bytes 786440 | tf_op jit(solution)/shard_map/ppermute | solution.py:374
  55.5 0.0 collective-permute-done.9.rest_5_
  55.5 1.0 %collective-permute-start.11 = (bf16[512,256]{1,0:T(8,128)(2,1)S(1)}, bf16[512,256]{1,0:T(8,128)(2,1)S(1)}, u32[]{:S(2)}, u32[]{:S(2)}) collective-permute-start(bf16[512,256]{1,0:T(8,128)(2,1)S(1)} %collective-permute-done.9.rest_5_), channel_id=1, source_target_pairs={{0,2},{2,0},{4,6},{6,4},{8,10},{10,8},{12,14},{14,12},{1,3},{3,1},... | collective-permute-start | bytes 786440 | tf_op jit(solution)/shard_map/ppermute | solution.py:374
  56.5 2.3 %collective-permute-done.12.rest_8_ = bf16[512,256]{1,0:T(8,128)(2,1)S(1)} collective-permute-done((bf16[512,256]{1,0:T(8,128)(2,1)S(1)}, bf16[512,256]{1,0:T(8,128)(2,1)S(1)}, u32[]{:S(2)}, u32[]{:S(2)}) %collective-permute-start.12) | collective-permute-done | bytes 262176 | tf_op jit(solution)/shard_map/ppermute | solution.py:371
  58.8 1.0 %collective-permute-start.16 = (bf16[512,256]{1,0:T(8,128)(2,1)S(1)}, bf16[512,256]{1,0:T(8,128)(2,1)S(1)}, u32[]{:S(2)}, u32[]{:S(2)}) collective-permute-start(bf16[512,256]{1,0:T(8,128)(2,1)S(1)} %collective-permute-done.8.rest_4_), channel_id=1, source_target_pairs={{0,4},{2,6},{4,8},{6,10},{8,12},{10,14},{12,0},{14,2},{1,5},{3,7},... | collective-permute-start | bytes 786440 | tf_op jit(solution)/shard_map/ppermute | solution.py:371
  59.8 0.0 collective-permute-done.14.rest_10_
  59.8 1.7 %collective-permute-start.17 = (bf16[512,256]{1,0:T(8,128)(2,1)S(1)}, bf16[512,256]{1,0:T(8,128)(2,1)S(1)}, u32[]{:S(2)}, u32[]{:S(2)}) collective-permute-start(bf16[512,256]{1,0:T(8,128)(2,1)S(1)} %collective-permute-done.9.rest_5_), channel_id=1, source_target_pairs={{0,12},{2,14},{4,0},{6,2},{8,4},{10,6},{12,8},{14,10},{1,13},{3,15... | collective-permute-start | bytes 786440 | tf_op jit(solution)/shard_map/ppermute | solution.py:371
  61.5 0.0 collective-permute-done.10.rest_6_
  61.5 2.7 %collective-permute-start.13 = (bf16[512,256]{1,0:T(8,128)(2,1)S(1)}, bf16[512,256]{1,0:T(8,128)(2,1)S(1)}, u32[]{:S(2)}, u32[]{:S(2)}) collective-permute-start(bf16[512,256]{1,0:T(8,128)(2,1)S(1)} %collective-permute-done.12.rest_8_), channel_id=1, source_target_pairs={{0,2},{2,0},{4,6},{6,4},{8,10},{10,8},{12,14},{14,12},{1,3},{3,1},... | collective-permute-start | bytes 786440 | tf_op jit(solution)/shard_map/ppermute | solution.py:374
  64.1 0.0 collective-permute-done.11.rest_7_
  64.2 0.3 collective-permute-start.15
  64.5 1.3 %collective-permute-done.16.top_ref = bf16[512,256]{1,0:T(8,128)(2,1)S(1)} collective-permute-done((bf16[512,256]{1,0:T(8,128)(2,1)S(1)}, bf16[512,256]{1,0:T(8,128)(2,1)S(1)}, u32[]{:S(2)}, u32[]{:S(2)}) %collective-permute-start.16) | collective-permute-done | bytes 262176 | tf_op jit(solution)/shard_map/ppermute | solution.py:371
  65.8 3.0 %collective-permute-start.18 = (bf16[512,256]{1,0:T(8,128)(2,1)S(1)}, bf16[512,256]{1,0:T(8,128)(2,1)S(1)}, u32[]{:S(2)}, u32[]{:S(2)}) collective-permute-start(bf16[512,256]{1,0:T(8,128)(2,1)S(1)} %collective-permute-done.16.top_ref), channel_id=1, source_target_pairs={{0,2},{2,0},{4,6},{6,4},{8,10},{10,8},{12,14},{14,12},{1,3},{3,1},... | collective-permute-start | bytes 786440 | tf_op jit(solution)/shard_map/ppermute | solution.py:374
  68.7 0.0 collective-permute-done.17.low_ref
  68.7 0.0 collective-permute-start.19
  68.7 0.6 near.1.acc_ref
  69.3 0.0 collective-permute-done.13.rest_9_
  69.3 0.0 collective-permute-done.15.rest_11_
  69.3 0.0 collective-permute-done.twin_ref
  69.3 1.4 %middle.1 = (f32[1024,256]{1,0:T(8,128)S(1)}, f32[1024,256]{1,0:T(8,128)S(1)}) custom-call(s32[1]{0:T(128)} %bitcast.at_ref, bf16[8,256,256]{2,1,0:T(8,128)(2,1)S(1)} %get-tuple-element.31.w_ref.mine_ref, bf16[6,256,256]{2,1,0:T(8,128)(2,1)S(1)} %collective-permute-done.twin_ref, bf16[256,256]{1,0:T(8,128)(2,1)S(1)} %get-tuple-element.33.own_ref, ...), custom_call_target="tpu_custom_call" | custom-call | flops 1207959552 | bytes 6815744 | tf_op jit(solution)/shard_map/middle/pallas_call | solution.py:390
  70.8 0.4 later.1
  71.2 0.0 collective-permute-done.18.top_ref
  71.2 0.0 collective-permute-done.19.low_ref
  71.2 1.5 %finish.1 = bf16[1024,512]{1,0:T(8,128)(2,1)} custom-call(s32[1]{0:T(128)} %bitcast.at_ref, s32[1]{0:T(128)} %bitcast.1.dp_ref, bf16[8,256,256]{2,1,0:T(8,128)(2,1)S(1)} %get-tuple-element.31.w_ref.mine_ref, bf16[6,256,256]{2,1,0:T(8,128)(2,1)S(1)} %collective-permute-done.twin_ref, f32[1024,256]{1,0:T(8,128)S(1)} %get-tuple-element.53.acc_mine_ref, ...), custom_call_target="tpu_custom_call" | custom-call | flops 268435456 | bytes 3670016 | tf_op jit(solution)/shard_map/finish/pallas_call | solution.py:409
Async XLA Ops:
  10.4 26.3 %copy-start = (f32[2]{0:T(128)S(1)}, f32[2]{0:T(128)}, u32[]{:S(2)}) copy-start(f32[2]{0:T(128)} %gate_ref.5) | copy-start | bytes 28
  10.5 37.6 %all-to-all-start = ((bf16[8,256,256]{2,1,0:T(8,128)(2,1)}), bf16[8,256,256]{2,1,0:T(8,128)(2,1)}, u32[]{:S(2)}, u32[]{:S(2)}) async-start(bf16[8,256,256]{2,1,0:T(8,128)(2,1)} %get-tuple-element.30), calls=%async_computation | async-start | bytes 2097152 | tf_op jit(solution)/shard_map/all_to_all | solution.py:312
  17.8 5.1 %collective-permute-start.2 = (bf16[2,136,128]{2,1,0:T(8,128)(2,1)S(1)}, bf16[2,136,128]{2,1,0:T(8,128)(2,1)S(1)}, u32[]{:S(2)}, u32[]{:S(2)}) collective-permute-start(bf16[2,136,128]{2,1,0:T(8,128)(2,1)S(1)} %get-tuple-element.35.total_ref), channel_id=1, source_target_pairs={{0,16},{16,0},{32,48},{48,32},{64,80},{80,64},{96,112},{112,96},{1... | collective-permute-start | bytes 208904 | tf_op jit(solution)/shard_map/ppermute | solution.py:341
  23.0 3.6 %collective-permute-start.3 = (bf16[2,136,128]{2,1,0:T(8,128)(2,1)S(1)}, bf16[2,136,128]{2,1,0:T(8,128)(2,1)S(1)}, u32[]{:S(2)}, u32[]{:S(2)}) collective-permute-start(bf16[2,136,128]{2,1,0:T(8,128)(2,1)S(1)} %get-tuple-element.36.total_ref), channel_id=1, source_target_pairs={{0,32},{16,48},{32,0},{48,16},{64,96},{80,112},{96,64},{112,80},{1... | collective-permute-start | bytes 208904 | tf_op jit(solution)/shard_map/ppermute | solution.py:341
  26.7 4.5 %collective-permute-start.4 = (bf16[2,136,128]{2,1,0:T(8,128)(2,1)S(1)}, bf16[2,136,128]{2,1,0:T(8,128)(2,1)S(1)}, u32[]{:S(2)}, u32[]{:S(2)}) collective-permute-start(bf16[2,136,128]{2,1,0:T(8,128)(2,1)S(1)} %get-tuple-element.38.total_ref), channel_id=1, source_target_pairs={{0,64},{16,80},{32,96},{48,112},{64,0},{80,16},{96,32},{112,48},{1... | collective-permute-start | bytes 208904 | tf_op jit(solution)/shard_map/ppermute | solution.py:341
  28.8 20.8 %collective-permute-start.1 = (bf16[256,256]{1,0:T(8,128)(2,1)S(1)}, bf16[256,256]{1,0:T(8,128)(2,1)S(1)}, u32[]{:S(2)}, u32[]{:S(2)}) collective-permute-start(bf16[256,256]{1,0:T(8,128)(2,1)S(1)} %get-tuple-element.34), channel_id=1, source_target_pairs={{0,2},{2,0},{4,6},{6,4},{8,10},{10,8},{12,14},{14,12},{1,3},{3,1},... | collective-permute-start | bytes 393224 | tf_op jit(solution)/shard_map/ppermute | solution.py:326
  31.3 10.1 %collective-permute-start.5 = (bf16[2,136,128]{2,1,0:T(8,128)(2,1)S(1)}, bf16[2,136,128]{2,1,0:T(8,128)(2,1)S(1)}, u32[]{:S(2)}, u32[]{:S(2)}) collective-permute-start(bf16[2,136,128]{2,1,0:T(8,128)(2,1)S(1)} %get-tuple-element.40), channel_id=1, source_target_pairs={{0,224},{16,240},{32,192},{48,208},{64,160},{80,176},{96,128},{112... | collective-permute-start | bytes 208904 | tf_op jit(solution)/shard_map/ppermute | solution.py:341
  42.5 8.5 %collective-permute-start.6 = (bf16[512,256]{1,0:T(8,128)(2,1)S(1)}, bf16[512,256]{1,0:T(8,128)(2,1)S(1)}, u32[]{:S(2)}, u32[]{:S(2)}) collective-permute-start(bf16[512,256]{1,0:T(8,128)(2,1)S(1)} %get-tuple-element.49.rest_0_), channel_id=1, source_target_pairs={{0,2},{2,0},{4,6},{6,4},{8,10},{10,8},{12,14},{14,12},{1,3},{3,1},... | collective-permute-start | bytes 786440 | tf_op jit(solution)/shard_map/ppermute | solution.py:374
  45.2 6.0 %collective-permute-start.7 = (bf16[512,256]{1,0:T(8,128)(2,1)S(1)}, bf16[512,256]{1,0:T(8,128)(2,1)S(1)}, u32[]{:S(2)}, u32[]{:S(2)}) collective-permute-start(bf16[512,256]{1,0:T(8,128)(2,1)S(1)} %get-tuple-element.50.rest_2_), channel_id=1, source_target_pairs={{0,2},{2,0},{4,6},{6,4},{8,10},{10,8},{12,14},{14,12},{1,3},{3,1},... | collective-permute-start | bytes 786440 | tf_op jit(solution)/shard_map/ppermute | solution.py:374
  45.3 8.7 %collective-permute-start.8 = (bf16[512,256]{1,0:T(8,128)(2,1)S(1)}, bf16[512,256]{1,0:T(8,128)(2,1)S(1)}, u32[]{:S(2)}, u32[]{:S(2)}) collective-permute-start(bf16[512,256]{1,0:T(8,128)(2,1)S(1)} %get-tuple-element.49.rest_0_), channel_id=1, source_target_pairs={{0,4},{2,6},{4,8},{6,10},{8,12},{10,14},{12,0},{14,2},{1,5},{3,7},... | collective-permute-start | bytes 786440 | tf_op jit(solution)/shard_map/ppermute | solution.py:371
  46.7 8.8 %collective-permute-start.9 = (bf16[512,256]{1,0:T(8,128)(2,1)S(1)}, bf16[512,256]{1,0:T(8,128)(2,1)S(1)}, u32[]{:S(2)}, u32[]{:S(2)}) collective-permute-start(bf16[512,256]{1,0:T(8,128)(2,1)S(1)} %get-tuple-element.50.rest_2_), channel_id=1, source_target_pairs={{0,12},{2,14},{4,0},{6,2},{8,4},{10,6},{12,8},{14,10},{1,13},{3,15... | collective-permute-start | bytes 786440 | tf_op jit(solution)/shard_map/ppermute | solution.py:371
  49.7 19.7 %collective-permute-start = (bf16[6,256,256]{2,1,0:T(8,128)(2,1)S(1)}, bf16[6,256,256]{2,1,0:T(8,128)(2,1)S(1)}, u32[]{:S(2)}, u32[]{:S(2)}) collective-permute-start(bf16[6,256,256]{2,1,0:T(8,128)(2,1)S(1)} %get-tuple-element.32), channel_id=1, source_target_pairs={{0,1},{1,0},{2,3},{3,2},{4,5},{5,4},{6,7},{7,6},{8,9},{9,8},{10,11... | collective-permute-start | bytes 2359304 | tf_op jit(solution)/shard_map/ppermute | solution.py:325
  51.0 7.8 %collective-permute-start.12 = (bf16[512,256]{1,0:T(8,128)(2,1)S(1)}, bf16[512,256]{1,0:T(8,128)(2,1)S(1)}, u32[]{:S(2)}, u32[]{:S(2)}) collective-permute-start(bf16[512,256]{1,0:T(8,128)(2,1)S(1)} %get-tuple-element.50.rest_2_), channel_id=1, source_target_pairs={{0,4},{2,6},{4,8},{6,10},{8,12},{10,14},{12,0},{14,2},{1,5},{3,7},... | collective-permute-start | bytes 786440 | tf_op jit(solution)/shard_map/ppermute | solution.py:371
  51.2 8.5 %collective-permute-start.14 = (bf16[512,256]{1,0:T(8,128)(2,1)S(1)}, bf16[512,256]{1,0:T(8,128)(2,1)S(1)}, u32[]{:S(2)}, u32[]{:S(2)}) collective-permute-start(bf16[512,256]{1,0:T(8,128)(2,1)S(1)} %get-tuple-element.49.rest_0_), channel_id=1, source_target_pairs={{0,12},{2,14},{4,0},{6,2},{8,4},{10,6},{12,8},{14,10},{1,13},{3,15... | collective-permute-start | bytes 786440 | tf_op jit(solution)/shard_map/ppermute | solution.py:371
  54.0 7.5 %collective-permute-start.10 = (bf16[512,256]{1,0:T(8,128)(2,1)S(1)}, bf16[512,256]{1,0:T(8,128)(2,1)S(1)}, u32[]{:S(2)}, u32[]{:S(2)}) collective-permute-start(bf16[512,256]{1,0:T(8,128)(2,1)S(1)} %collective-permute-done.8.rest_4_), channel_id=1, source_target_pairs={{0,2},{2,0},{4,6},{6,4},{8,10},{10,8},{12,14},{14,12},{1,3},{3,1},... | collective-permute-start | bytes 786440 | tf_op jit(solution)/shard_map/ppermute | solution.py:374
  55.5 8.7 %collective-permute-start.11 = (bf16[512,256]{1,0:T(8,128)(2,1)S(1)}, bf16[512,256]{1,0:T(8,128)(2,1)S(1)}, u32[]{:S(2)}, u32[]{:S(2)}) collective-permute-start(bf16[512,256]{1,0:T(8,128)(2,1)S(1)} %collective-permute-done.9.rest_5_), channel_id=1, source_target_pairs={{0,2},{2,0},{4,6},{6,4},{8,10},{10,8},{12,14},{14,12},{1,3},{3,1},... | collective-permute-start | bytes 786440 | tf_op jit(solution)/shard_map/ppermute | solution.py:374
  58.8 7.0 %collective-permute-start.16 = (bf16[512,256]{1,0:T(8,128)(2,1)S(1)}, bf16[512,256]{1,0:T(8,128)(2,1)S(1)}, u32[]{:S(2)}, u32[]{:S(2)}) collective-permute-start(bf16[512,256]{1,0:T(8,128)(2,1)S(1)} %collective-permute-done.8.rest_4_), channel_id=1, source_target_pairs={{0,4},{2,6},{4,8},{6,10},{8,12},{10,14},{12,0},{14,2},{1,5},{3,7},... | collective-permute-start | bytes 786440 | tf_op jit(solution)/shard_map/ppermute | solution.py:371
  59.8 9.0 %collective-permute-start.17 = (bf16[512,256]{1,0:T(8,128)(2,1)S(1)}, bf16[512,256]{1,0:T(8,128)(2,1)S(1)}, u32[]{:S(2)}, u32[]{:S(2)}) collective-permute-start(bf16[512,256]{1,0:T(8,128)(2,1)S(1)} %collective-permute-done.9.rest_5_), channel_id=1, source_target_pairs={{0,12},{2,14},{4,0},{6,2},{8,4},{10,6},{12,8},{14,10},{1,13},{3,15... | collective-permute-start | bytes 786440 | tf_op jit(solution)/shard_map/ppermute | solution.py:371
  61.5 7.8 %collective-permute-start.13 = (bf16[512,256]{1,0:T(8,128)(2,1)S(1)}, bf16[512,256]{1,0:T(8,128)(2,1)S(1)}, u32[]{:S(2)}, u32[]{:S(2)}) collective-permute-start(bf16[512,256]{1,0:T(8,128)(2,1)S(1)} %collective-permute-done.12.rest_8_), channel_id=1, source_target_pairs={{0,2},{2,0},{4,6},{6,4},{8,10},{10,8},{12,14},{14,12},{1,3},{3,1},... | collective-permute-start | bytes 786440 | tf_op jit(solution)/shard_map/ppermute | solution.py:374
  64.2 5.2 %collective-permute-start.15 = (bf16[512,256]{1,0:T(8,128)(2,1)S(1)}, bf16[512,256]{1,0:T(8,128)(2,1)S(1)}, u32[]{:S(2)}, u32[]{:S(2)}) collective-permute-start(bf16[512,256]{1,0:T(8,128)(2,1)S(1)} %collective-permute-done.14.rest_10_), channel_id=1, source_target_pairs={{0,2},{2,0},{4,6},{6,4},{8,10},{10,8},{12,14},{14,12},{1,3},{3,1},... | collective-permute-start | bytes 786440 | tf_op jit(solution)/shard_map/ppermute | solution.py:374
  65.8 5.4 %collective-permute-start.18 = (bf16[512,256]{1,0:T(8,128)(2,1)S(1)}, bf16[512,256]{1,0:T(8,128)(2,1)S(1)}, u32[]{:S(2)}, u32[]{:S(2)}) collective-permute-start(bf16[512,256]{1,0:T(8,128)(2,1)S(1)} %collective-permute-done.16.top_ref), channel_id=1, source_target_pairs={{0,2},{2,0},{4,6},{6,4},{8,10},{10,8},{12,14},{14,12},{1,3},{3,1},... | collective-permute-start | bytes 786440 | tf_op jit(solution)/shard_map/ppermute | solution.py:374
  68.7 2.5 %collective-permute-start.19 = (bf16[512,256]{1,0:T(8,128)(2,1)S(1)}, bf16[512,256]{1,0:T(8,128)(2,1)S(1)}, u32[]{:S(2)}, u32[]{:S(2)}) collective-permute-start(bf16[512,256]{1,0:T(8,128)(2,1)S(1)} %collective-permute-done.17.low_ref), channel_id=1, source_target_pairs={{0,2},{2,0},{4,6},{6,4},{8,10},{10,8},{12,14},{14,12},{1,3},{3,1},... | collective-permute-start | bytes 786440 | tf_op jit(solution)/shard_map/ppermute | solution.py:374
